TPU v7x, 32 devices: a whole 2x2x4 slice. The times are simulated.
32 devices in a mesh: dp: 2 (over x), tm: 4 (over z), space: 4 (over y, core).
Axes of the slice: x: 2, y: 2, z: 4, core: 2. Of those that a mesh axis runs over, the one named last changes fastest.
Arguments:
- latent: bfloat16 [2, 12, 8, 104, 384], P('dp', 'tm', 'space'), may hold values from -16 to 16
- attn_gain: float32 [384], replicated, may hold values from 0.5 to 1.5
- w_query: bfloat16 [384, 384], replicated, may hold values from -1 to 1
- w_key: bfloat16 [384, 384], replicated, may hold values from -1 to 1
- w_value: bfloat16 [384, 384], replicated, may hold values from -0.3125 to 0.3125
- w_out: bfloat16 [384, 384], replicated, may hold values from -1.25 to 1.25
- conv_gain_first: float32 [384], replicated, may hold values from 0.5 to 1.5
- conv_first: bfloat16 [3, 3, 3, 384, 384], replicated, may hold values from -0.0625 to 0.0625
- conv_gain_second: float32 [384], replicated, may hold values from 0.5 to 1.5
- conv_second: bfloat16 [3, 3, 3, 384, 384], replicated, may hold values from -0.0625 to 0.0625
- student_in: bfloat16 [384, 384], replicated, may hold values from -0.3125 to 0.3125
- student_out: bfloat16 [384, 384], replicated, may hold values from -0.3125 to 0.3125
Outputs:
- teacher_out: bfloat16 [2, 12, 8, 104, 384], P('dp', 'tm', 'space')
- grad_in: float32 [384, 384], replicated
- grad_out: float32 [384, 384], replicated
All inputs are finite; a program needn't handle non-finite values.
Results may differ from a plain program's by a relative error of at most 0.007.
Values may be sent and summed in bfloat16 or wider, within the bound.
No kernel may reach another device: no remote copies, remote signals or barrier semaphores. Data moves between devices by JAX's collectives and lax.ppermute only.
A program may use at most 128 MiB of HBM per device.

v0:
```python
import functools

import jax
import jax.numpy as jnp
from jax import lax
from jax.experimental import pallas as pl
from jax.experimental.pallas import tpu as pltpu
from jax.sharding import PartitionSpec as P


F32 = jnp.float32
BF16 = jnp.bfloat16
VMEM = pl.BlockSpec(memory_space=pltpu.VMEM)
HBM = pl.BlockSpec(memory_space=pltpu.HBM)
LIMIT = 20 << 20


def xor_permute(value, axis, mask):
    count = lax.axis_size(axis)
    return lax.ppermute(value, axis, [(i, i ^ mask) for i in range(count)])


def gather_blocks(block):
    mask = lax.axis_size("space") // 2
    blocks = [block, xor_permute(block, "space", mask)]
    while mask > 1:
        mask //= 2
        blocks = blocks + [xor_permute(b, "space", mask) for b in blocks]
    return blocks


def across_pairs():
    pairs = []
    for low in range(1, lax.axis_size("space") - 1, 2):
        pairs += [(low, low + 1), (low + 1, low)]
    return pairs


def across_permute(value):
    return lax.ppermute(value, "space", across_pairs())


def across_next_frames(value):
    count = lax.axis_size("space")
    pairs = [
        (block * count + source, (block + 1) * count + target)
        for block in range(lax.axis_size("tm") - 1)
        for source, target in across_pairs()
    ]
    return lax.ppermute(value, ("tm", "space"), pairs)


def next_frames(value):
    count = lax.axis_size("tm")
    return lax.ppermute(value, "tm", [(i, i + 1) for i in range(count - 1)])


def take_rows(value, index, rows):
    return lax.dynamic_slice_in_dim(value, index * rows, rows, axis=0)


def plane_permute(value, mask, dp_count):
    chips = lax.axis_size("space") // 2
    pairs = []
    for member in range(dp_count * chips):
        other = member ^ mask
        for core in range(2):
            source = (member // chips * chips + member % chips) * 2 + core
            target = (other // chips * chips + other % chips) * 2 + core
            pairs.append((source, target))
    return lax.ppermute(value, ("dp", "space"), pairs)


def sum_everywhere(mine, yours):
    odd = is_odd()
    dp_count, tm_count, space_count = (lax.axis_size(a) for a in ("dp", "tm", "space"))
    mine = mine + xor_permute(yours, "space", 1).astype(F32)
    members = dp_count * space_count // 2
    member = lax.axis_index("dp") * (space_count // 2) + lax.axis_index("space") // 2
    rows = mine.shape[0] // members
    sent = mine.astype(BF16)
    arrived = [
        plane_permute(take_rows(sent, member ^ mask, rows), mask, dp_count)
        for mask in range(1, members)
    ]
    chunk = take_rows(mine, member, rows)
    for piece in arrived:
        chunk = chunk + piece.astype(F32)
    chunk = chunk.astype(BF16)
    pieces = [chunk] + [xor_permute(chunk, "tm", mask) for mask in range(1, tm_count)]
    pieces = [piece.astype(F32) for piece in pieces]
    while len(pieces) > 1:
        pieces = [pieces[i] + pieces[i + 1] for i in range(0, len(pieces), 2)]
    chunk = pieces[0].astype(BF16)
    whole = jnp.zeros(mine.shape, BF16)
    whole = lax.dynamic_update_slice_in_dim(whole, chunk, member * rows, axis=0)
    for mask in range(1, members):
        whole = lax.dynamic_update_slice_in_dim(
            whole, plane_permute(chunk, mask, dp_count), (member ^ mask) * rows, axis=0
        )
    other = xor_permute(whole, "space", 1)
    return (
        jnp.where(odd, other, whole).astype(F32),
        jnp.where(odd, whole, other).astype(F32),
    )


def root_norm(values, gain):
    return values * lax.rsqrt(jnp.mean(values * values, axis=-1, keepdims=True) + 1e-06) * gain


def silu(values):
    return values * jax.nn.sigmoid(values)


def dot(left, right):
    return jnp.dot(left, right, preferred_element_type=F32)


def call(body, outs, specs, out_specs, scratch, flops, moved, *args):
    return pl.pallas_call(
        body,
        out_shape=outs,
        in_specs=specs,
        out_specs=out_specs,
        scratch_shapes=scratch,
        compiler_params=pltpu.CompilerParams(vmem_limit_bytes=LIMIT),
        cost_estimate=pl.CostEstimate(
            flops=int(flops), bytes_accessed=int(moved), transcendentals=0
        ),
    )(*(
        pltpu.with_memory_space_constraint(arg, pltpu.HBM) if spec is HBM else arg
        for arg, spec in zip(args, specs, strict=True)
    ))


def shape(rows, columns, dtype):
    return jax.ShapeDtypeStruct((rows, columns), dtype)


def is_odd():
    return lax.rem(lax.axis_index("space"), 2) == 1


def edge_rows(values, columns, odd):
    first, last = values[:columns], values[values.shape[0] - columns :]
    return jnp.where(odd, first, last), jnp.where(odd, last, first)


def norm_body(late, latent_hbm, gain_hbm, latent, normed_late, normed_early, gain, sems):
    frame_count, per_frame = latent_hbm.shape[:2]
    pltpu.make_async_copy(gain_hbm, gain, sems.at[frame_count]).start()
    copies = {}
    for frame in range(frame_count - 1, -1, -1):
        here = pl.ds(frame * per_frame, per_frame)
        copies[frame] = pltpu.make_async_copy(latent_hbm.at[frame], latent.at[here], sems.at[frame])
        copies[frame].start()
    pltpu.make_async_copy(gain_hbm, gain, sems.at[frame_count]).wait()
    for frame in range(frame_count - 1, -1, -1):
        copies[frame].wait()
        wide = latent[pl.ds(frame * per_frame, per_frame)].astype(F32)
        normed = root_norm(wide, gain[...].reshape(1, -1)).astype(BF16)
        at = frame - (frame_count - late)
        target = normed_late if at >= 0 else normed_early
        target[pl.ds((at if at >= 0 else frame) * per_frame, per_frame)] = normed


def prepare_body(
    latent, query_hbm, key_hbm, value_hbm, out_hbm, in_hbm, back_hbm, first_hbm, second_hbm,
    w_query, w_both, w_out, s_out, first, second, pre, hidden_t, latent_t, predicted,
    s_in, sems,
):
    channels = latent.shape[1]
    student = [
        pltpu.make_async_copy(in_hbm, s_in, sems.at[0]),
        pltpu.make_async_copy(back_hbm, s_out, sems.at[1]),
    ]
    rest = [
        pltpu.make_async_copy(query_hbm, w_query, sems.at[2]),
        pltpu.make_async_copy(key_hbm, w_both.at[:, pl.ds(0, channels)], sems.at[3]),
        pltpu.make_async_copy(value_hbm, w_both.at[:, pl.ds(channels, channels)], sems.at[4]),
        pltpu.make_async_copy(out_hbm, w_out, sems.at[5]),
    ]
    for at, (taps, packed) in enumerate(((first_hbm, first), (second_hbm, second))):
        for t in range(3):
            for r in range(3):
                for c in range(3):
                    block = packed.at[t, pl.ds(r * channels, channels), pl.ds(c * channels, channels)]
                    rest.append(
                        pltpu.make_async_copy(taps.at[t, r, c], block, sems.at[6 + 3 * at + t])
                    )
    for copy in student + rest:
        copy.start()
    tokens = latent[...]
    latent_t[...] = tokens.T
    student[0].wait()
    before = dot(tokens, s_in[...])
    hidden = silu(before).astype(BF16)
    pre[...] = before
    hidden_t[...] = hidden.T
    student[1].wait()
    predicted[...] = tokens.astype(F32) + dot(hidden, s_out[...])
    for copy in rest:
        copy.wait()


def attend_body(blocks, start, count, later, columns, *refs):
    parts = refs[:blocks]
    latent, w_query, w_both, w_out, gain = refs[blocks : blocks + 5]
    act, mid, on, off = refs[-4:]
    channels = w_query.shape[0]
    odd = is_odd()
    per_frame = parts[0].shape[0] // count
    if later:
        for ends, others in zip((on, off), refs[blocks + 5 : -4], strict=True):
            ends[pl.ds(count * columns, others.shape[0])] = others[...]
    for frame in range(count - 1, -1, -1):
        here = pl.ds(frame * per_frame, per_frame)
        rows = jnp.concatenate([part[here] for part in parts], axis=0)
        queries = dot(parts[0][here], w_query[...]).astype(BF16)
        both = dot(rows, w_both[...]).astype(BF16)
        keys, values = both[:, :channels], both[:, channels:]
        scores = lax.dot_general(
            queries, keys, (((1,), (1,)), ((), ())), preferred_element_type=F32
        ) * channels ** (-0.5)
        expos = jnp.exp(scores - jnp.max(scores, axis=-1, keepdims=True))
        totals = jnp.sum(expos, axis=-1, keepdims=True)
        mixed = (dot(expos.astype(BF16), values) / totals).astype(BF16)
        own = latent[pl.ds((start + frame) * per_frame, per_frame)]
        middle = (own.astype(F32) + dot(mixed, w_out[...])).astype(BF16)
        mid[here] = middle
        active = silu(root_norm(middle.astype(F32), gain[...].reshape(1, -1))).astype(BF16)
        act[here] = active
        edge = pl.ds(frame * columns, columns)
        on[edge], off[edge] = edge_rows(active, columns, odd)


def stack_rows(columns, odd, own, on, off, stacked, at):
    per_frame, channels = own.shape
    base = at * per_frame
    split = per_frame - columns
    stacked[pl.ds(base, columns), 0:channels] = jnp.where(odd, on, off)
    stacked[pl.ds(base + columns, split), 0:channels] = own[:split]
    stacked[pl.ds(base, per_frame), channels : 2 * channels] = own
    stacked[pl.ds(base, split), 2 * channels :] = own[columns:]
    stacked[pl.ds(base + split, columns), 2 * channels :] = jnp.where(odd, off, on)


def taps_sum(sources, frame, stacked, packed, per_frame, total):
    for at, source in enumerate(sources):
        tap = source - frame
        if 0 <= tap < 3:
            term = dot(stacked[pl.ds(at * per_frame, per_frame)], packed[tap])
            total = term if total is None else total + term
    return total


def shift_columns(total, columns):
    rows, channels = total.shape[0], total.shape[1] // 3
    column = lax.broadcasted_iota(jnp.int32, (rows, channels), 0) % columns
    before = pltpu.roll(total[:, :channels], 1, 0)
    after = pltpu.roll(total[:, 2 * channels :], rows - 1, 0)
    return (
        total[:, channels : 2 * channels]
        + jnp.where(column == 0, 0.0, before)
        + jnp.where(column == columns - 1, 0.0, after)
    )


def own_body(groups, columns, *refs):
    odd = is_odd()
    off, on, packed, partial, stacked = refs[-5:]
    frame_count = sum(groups)
    per_frame = partial.shape[0] // frame_count
    at = 0
    for own, frames in zip(refs[:-5], groups, strict=True):
        for frame in range(frames):
            edge = pl.ds(at * columns, columns)
            stack_rows(
                columns, odd, own[pl.ds(frame * per_frame, per_frame)], on[edge], off[edge],
                stacked, at,
            )
            at += 1
    sources = range(2, frame_count + 2)
    for frame in range(frame_count):
        total = taps_sum(sources, frame, stacked, packed, per_frame, None)
        partial[pl.ds(frame * per_frame, per_frame)] = total


def stack_earlier(columns, odd, tail, partner, off, stacked):
    per_frame = stacked.shape[0] // 2
    for frame in range(2):
        here = pl.ds(frame * per_frame, per_frame)
        on, _ = edge_rows(partner[here], columns, jnp.logical_not(odd))
        edge = pl.ds(frame * columns, columns)
        stack_rows(columns, odd, tail[here], on, off[edge], stacked, frame)


def first_body(
    columns, tail, partner, tail_off, packed, partial, gain, act, late, on, off,
    off_late, stacked,
):
    odd = is_odd()
    stack_earlier(columns, odd, tail, partner, tail_off, stacked)
    per_frame = stacked.shape[0] // 2
    frame_count = partial.shape[0] // per_frame
    for frame in range(frame_count - 1, -1, -1):
        here = pl.ds(frame * per_frame, per_frame)
        total = taps_sum((0, 1), frame, stacked, packed, per_frame, partial[here])
        total = shift_columns(total, columns)
        active = silu(root_norm(total, gain[...].reshape(1, -1))).astype(BF16)
        act[here] = active
        edge = pl.ds(frame * columns, columns)
        near, far = edge_rows(active, columns, odd)
        on[edge], off[edge] = near, far
        at = frame - (frame_count - 2)
        if at >= 0:
            late[pl.ds(at * per_frame, per_frame)] = active
            off_late[pl.ds(at * columns, columns)] = far


def last_body(
    columns, token_total, tail, partner, tail_off, packed, partial, mid_early, mid_late,
    pre, hidden_t, latent_t, predicted, s_out, teacher, mine, yours, stacked, signals,
):
    odd = is_odd()
    stack_earlier(columns, odd, tail, partner, tail_off, stacked)
    per_frame = stacked.shape[0] // 2
    frame_count = partial.shape[0] // per_frame
    for frame in range(frame_count - 1, -1, -1):
        here = pl.ds(frame * per_frame, per_frame)
        total = taps_sum((0, 1), frame, stacked, packed, per_frame, partial[here])
        total = shift_columns(total, columns)
        at = frame - (frame_count - 2)
        mid = mid_late[pl.ds(at * per_frame, per_frame)] if at >= 0 else mid_early[here]
        taught = (mid.astype(F32) + total).astype(BF16)
        teacher[here] = taught
        error = predicted[here] - taught.astype(F32)
        signals[here] = (
            error * lax.rsqrt(error * error + 0.0625) * token_total ** (-0.5)
        ).astype(BF16)
    signal = signals[...]
    grad_out = dot(hidden_t[...], signal)
    back = lax.dot_general(
        signal, s_out[...], (((1,), (1,)), ((), ())), preferred_element_type=F32
    )
    before = pre[...]
    logistic = jax.nn.sigmoid(before)
    back_pre = (back * logistic * (1.0 + before * (1.0 - logistic))).astype(BF16)
    grad_in = dot(latent_t[...], back_pre)
    mine[...] = jnp.where(odd, grad_out, grad_in)
    yours[...] = jnp.where(odd, grad_in, grad_out).astype(BF16)


def shards(
    latent,
    attn_gain,
    w_query,
    w_key,
    w_value,
    w_out,
    conv_gain_first,
    conv_first,
    conv_gain_second,
    conv_second,
    student_in,
    student_out,
):
    frame_count, row_count, columns, channels = latent.shape[1:]
    per_frame = row_count * columns
    tokens = frame_count * per_frame
    early = frame_count - 2
    frames = latent.reshape(frame_count, per_frame, channels)
    unit = 2 * channels * channels
    square = shape(channels, channels, BF16)

    def rows_of(count):
        return shape(count * per_frame, channels, BF16)

    def edges_of(count):
        return shape(count * columns, channels, BF16)

    latent_rows, normed_late, normed_early = call(
        functools.partial(norm_body, 2),
        [rows_of(frame_count), rows_of(2), rows_of(early)], [HBM] * 2, [VMEM] * 3,
        [pltpu.VMEM((channels,), F32), pltpu.SemaphoreType.DMA((frame_count + 1,))],
        0, 4 * tokens * channels, frames, attn_gain,
    )
    blocks_late = gather_blocks(normed_late)
    blocks_early = gather_blocks(normed_early)

    packed_shape = jax.ShapeDtypeStruct((3, 3 * channels, 3 * channels), BF16)
    wide = shape(tokens, channels, F32)
    turned = shape(channels, tokens, BF16)
    weights = (w_query, w_key, w_value, w_out, student_in, student_out, conv_first, conv_second)
    (
        w_query, w_both, w_out, student_out, packed_first, packed_second,
        pre, hidden_t, latent_t, predicted,
    ) = call(
        prepare_body,
        [square, shape(channels, 2 * channels, BF16), square, square, packed_shape, packed_shape,
         wide, turned, turned, wide],
        [VMEM] + [HBM] * len(weights), [VMEM] * 10,
        [pltpu.VMEM((channels, channels), BF16), pltpu.SemaphoreType.DMA((12,))],
        2 * tokens * unit, 60 * channels * channels * 2, latent_rows, *weights,
    )

    def attend(blocks, start, count, *others):
        args = [*blocks, latent_rows, w_query, w_both, w_out, conv_gain_first, *others]
        ends = edges_of(count + 2 if others else count)
        return call(
            functools.partial(attend_body, len(blocks), start, count, bool(others), columns),
            [rows_of(count), rows_of(count), ends, ends],
            [VMEM] * len(args), [VMEM] * 4, [],
            (2 + 4 * len(blocks)) * count * per_frame * unit, 4 * count * per_frame * channels,
            *args,
        )

    def stacked(count):
        return pltpu.VMEM((count * per_frame, 3 * channels), BF16)

    def from_earlier(late, off):
        tail = next_frames(late)
        corner = across_next_frames(off)
        partner = xor_permute(tail, "space", 1)
        return tail, corner, partner

    def own_part(groups, on, off, packed):
        halo = [across_permute(off), xor_permute(on, "space", 1)]
        args = [*(own for _, own in groups), *halo, packed]
        return call(
            functools.partial(own_body, [group[0] for group in groups], columns),
            shape(tokens, 3 * channels, F32), [VMEM] * len(args), VMEM,
            [stacked(frame_count)], 18 * tokens * unit, 8 * tokens * channels, *args,
        )

    act_late, mid_late, on_late, off_late = attend(blocks_late, early, 2)
    tail, tail_off, partner = from_earlier(act_late, off_late)
    act_early, mid_early, on, off = attend(blocks_early, 0, early, on_late, off_late)
    partial = own_part([(early, act_early), (2, act_late)], on, off, packed_first)
    args = [tail, partner, tail_off, packed_first, partial, conv_gain_second]
    act, late, on, off, off_late = call(
        functools.partial(first_body, columns),
        [rows_of(frame_count), rows_of(2), edges_of(frame_count), edges_of(frame_count), edges_of(2)],
        [VMEM] * len(args), [VMEM] * 5, [stacked(2)],
        9 * tokens * unit, 8 * tokens * channels, *args,
    )
    tail, tail_off, partner = from_earlier(late, off_late)
    partial = own_part([(frame_count, act)], on, off, packed_second)
    token_total = tokens * lax.axis_size("dp") * lax.axis_size("tm") * lax.axis_size("space")
    args = [
        tail, partner, tail_off, packed_second, partial, mid_early, mid_late,
        pre, hidden_t, latent_t, predicted, student_out,
    ]
    teacher, mine, yours = call(
        functools.partial(last_body, columns, token_total),
        [rows_of(frame_count), shape(channels, channels, F32), square],
        [VMEM] * len(args), [VMEM] * 3,
        [stacked(2), pltpu.VMEM((tokens, channels), BF16)],
        12 * tokens * unit, 8 * tokens * channels, *args,
    )
    grad_in, grad_out = sum_everywhere(mine, yours)
    return (teacher.reshape(latent.shape), grad_in, grad_out)


def solution(mesh):
    return jax.shard_map(
        shards,
        mesh=mesh,
        in_specs=(
            P("dp", "tm", "space", None, None),
            P(),
            P(),
            P(),
            P(),
            P(),
            P(),
            P(),
            P(),
            P(),
            P(),
            P(),
        ),
        out_specs=(P("dp", "tm", "space", None, None), P(), P()),
        check_vma=False,
    )
```

profile of v0, /device:TPU:0, one launch (start us, length us, event | category | flops | bytes accessed | tf_op | source)
XLA Modules:
  0.0 98.3 jit_solution(323007240743773609)
XLA Ops:
  0.6 1.4 %shard_map.139 = (bf16[624,384]{1,0:T(8,128)(2,1)S(1)}, bf16[416,384]{1,0:T(8,128)(2,1)S(1)}, bf16[208,384]{1,0:T(8,128)(2,1)S(1)}) custom-call(bf16[3,208,384]{2,1,0:T(8,128)(2,1)} %bitcast.2, f32[384]{0:T(512)} %gain_hbm.1), custom_call_target="tpu_custom_call" | custom-call | bytes 958464 | tf_op jit(solution)/shard_map/pallas_call | solution.py:121
  2.0 3.1 %collective-permute-start = (bf16[416,384]{1,0:T(8,128)(2,1)S(1)}, bf16[416,384]{1,0:T(8,128)(2,1)S(1)}, u32[]{:S(2)}, u32[]{:S(2)}) collective-permute-start(bf16[416,384]{1,0:T(8,128)(2,1)S(1)} %get-tuple-element.32.refs_0_), channel_id=1, source_target_pairs={{0,2},{1,3},{2,0},{3,1},{4,6},{5,7},{6,4},{7,5},{8,10},{9,11},{10,... | collective-permute-start | bytes 958472 | tf_op jit(solution)/shard_map/ppermute | solution.py:20
  5.1 7.5 %collective-permute-done.refs_1_ = bf16[416,384]{1,0:T(8,128)(2,1)S(1)} collective-permute-done((bf16[416,384]{1,0:T(8,128)(2,1)S(1)}, bf16[416,384]{1,0:T(8,128)(2,1)S(1)}, u32[]{:S(2)}, u32[]{:S(2)}) %collective-permute-start) | collective-permute-done | bytes 319520 | tf_op jit(solution)/shard_map/ppermute | solution.py:20
  12.6 1.7 %collective-permute-start.6 = (bf16[208,384]{1,0:T(8,128)(2,1)S(1)}, bf16[208,384]{1,0:T(8,128)(2,1)S(1)}, u32[]{:S(2)}, u32[]{:S(2)}) collective-permute-start(bf16[208,384]{1,0:T(8,128)(2,1)S(1)} %get-tuple-element.40.refs_0_), channel_id=1, source_target_pairs={{0,2},{1,3},{2,0},{3,1},{4,6},{5,7},{6,4},{7,5},{8,10},{9,11},{10,... | collective-permute-start | bytes 479240 | tf_op jit(solution)/shard_map/ppermute | solution.py:20
  14.6 6.1 %shard_map.140 = (bf16[384,384]{1,0:T(8,128)(2,1)S(1)}, bf16[384,768]{1,0:T(8,128)(2,1)S(1)}, bf16[384,384]{1,0:T(8,128)(2,1)S(1)}, bf16[384,384]{1,0:T(8,128)(2...) custom-call(bf16[624,384]{1,0:T(8,128)(2,1)S(1)} %get-tuple-element., ...), custom_call_target="tpu_custom_call" | custom-call | flops 368050176 | bytes 17694720 | tf_op jit(solution)/shard_map/pallas_call | solution.py:121
  21.1 3.7 %shard_map.141 = (bf16[416,384]{1,0:T(8,128)(2,1)S(1)}, bf16[416,384]{1,0:T(8,128)(2,1)S(1)}, bf16[208,384]{1,0:T(8,128)(2,1)S(1)}, bf16[208,384]{1,0:T(8,128)(2,1)S(1)}) custom-call(bf16[416,384]{1,0:T(8,128)(2,1)S(1)} %get-tuple-element.32.refs_0_, bf16[416,384]{1,0:T(8,128)(2,1)S(1)} %collective-permute-done.refs_1_, ...), custom_call_target="tpu_custom_call" | custom-call | flops 2208301056 | bytes 638976 | tf_op jit(solution)/shard_map/pallas_call | solution.py:121
  24.8 3.5 %collective-permute-start.3 = (bf16[416,384]{1,0:T(8,128)(2,1)S(1)}, bf16[416,384]{1,0:T(8,128)(2,1)S(1)}, u32[]{:S(2)}, u32[]{:S(2)}) collective-permute-start(bf16[416,384]{1,0:T(8,128)(2,1)S(1)} %get-tuple-element.37.refs_1_), channel_id=1, source_target_pairs={{0,4},{4,8},{8,12},{1,5},{5,9},{9,13},{2,6},{6,10},{10,14},{3,7},{... | collective-permute-start | bytes 958472 | tf_op jit(solution)/shard_map/ppermute | solution.py:55
  28.3 2.0 %shard_map.142 = (bf16[208,384]{1,0:T(8,128)(2,1)S(1)}, bf16[208,384]{1,0:T(8,128)(2,1)S(1)}, bf16[312,384]{1,0:T(8,128)(2,1)S(1)}, bf16[312,384]{1,0:T(8,128)(2,1)S(1)}) custom-call(bf16[208,384]{1,0:T(8,128)(2,1)S(1)} %get-tuple-element.40.refs_0_, bf16[208,384]{1,0:T(8,128)(2,1)S(1)} %collective-permute-done.6.refs_1_, ...), custom_call_target="tpu_custom_call" | custom-call | flops 1104150528 | bytes 319488 | tf_op jit(solution)/shard_map/pallas_call | solution.py:121
  31.1 4.4 %collective-permute-done.3.tail = bf16[416,384]{1,0:T(8,128)(2,1)S(1)} collective-permute-done((bf16[416,384]{1,0:T(8,128)(2,1)S(1)}, bf16[416,384]{1,0:T(8,128)(2,1)S(1)}, u32[]{:S(2)}, u32[]{:S(2)}) %collective-permute-start.3) | collective-permute-done | bytes 319520 | tf_op jit(solution)/shard_map/ppermute | solution.py:55
  36.3 4.4 %shard_map.143.partial = f32[624,1152]{1,0:T(8,128)S(1)} custom-call(bf16[208,384]{1,0:T(8,128)(2,1)S(1)} %get-tuple-element.42.refs_0_, bf16[416,384]{1,0:T(8,128)(2,1)S(1)} %get-tuple-element.37.refs_1_, bf16[312,384]{1,0:T(8,128)(2,1)S(1)} %collective-permute-done.9.refs_2_, bf16[312,384]{1,0:T(8,128)(2,1)S(1)} %collective-permute-done.10.refs_3_, ...), custom_call_target="tpu_custom_call" | custom-call | flops 3312451584 | bytes 1916928 | tf_op jit(solution)/shard_map/pallas_call | solution.py:121
  40.8 2.8 %shard_map.144 = (bf16[624,384]{1,0:T(8,128)(2,1)S(1)}, bf16[416,384]{1,0:T(8,128)(2,1)S(1)}, bf16[312,384]{1,0:T(8,128)(2,1)S(1)}, bf16[312,384]{1,0:T(8,128)(2,1)S(1)}, bf16[208,384]{1,0:T(8,128)(2,1)S(1)}) custom-call(bf16[416,384]{1,0:T(8,128)(2,1)S(1)} %collective-permute-done.3.tail, bf16[416,384]{1,0:T(8,128)(2,1)S(1)} %collective-permute-done.4.partner, ...), custom_call_target="tpu_custom_call" | custom-call | flops 1656225792 | bytes 1916928 | tf_op jit(solution)/shard_map/pallas_call | solution.py:121
  43.6 4.4 %collective-permute-start.11 = (bf16[416,384]{1,0:T(8,128)(2,1)S(1)}, bf16[416,384]{1,0:T(8,128)(2,1)S(1)}, u32[]{:S(2)}, u32[]{:S(2)}) collective-permute-start(bf16[416,384]{1,0:T(8,128)(2,1)S(1)} %get-tuple-element.45), channel_id=1, source_target_pairs={{0,4},{4,8},{8,12},{1,5},{5,9},{9,13},{2,6},{6,10},{10,14},{3,7},{... | collective-permute-start | bytes 958472 | tf_op jit(solution)/shard_map/ppermute | solution.py:55
  48.7 5.8 %collective-permute-start.15 = (bf16[312,384]{1,0:T(8,128)(2,1)S(1)}, bf16[312,384]{1,0:T(8,128)(2,1)S(1)}, u32[]{:S(2)}, u32[]{:S(2)}) collective-permute-start(bf16[312,384]{1,0:T(8,128)(2,1)S(1)} %get-tuple-element.50), channel_id=1, source_target_pairs={{0,1},{1,0},{2,3},{3,2},{4,5},{5,4},{6,7},{7,6},{8,9},{9,8},{10,11... | collective-permute-start | bytes 718856 | tf_op jit(solution)/shard_map/ppermute | solution.py:20
  54.5 1.5 %collective-permute-start.12 = (bf16[416,384]{1,0:T(8,128)(2,1)S(1)}, bf16[416,384]{1,0:T(8,128)(2,1)S(1)}, u32[]{:S(2)}, u32[]{:S(2)}) collective-permute-start(bf16[416,384]{1,0:T(8,128)(2,1)S(1)} %collective-permute-done.11.tail), channel_id=1, source_target_pairs={{0,1},{1,0},{2,3},{3,2},{4,5},{5,4},{6,7},{7,6},{8,9},{9,8},{10,11... | collective-permute-start | bytes 958472 | tf_op jit(solution)/shard_map/ppermute | solution.py:20
  56.9 4.4 %shard_map.145.partial = f32[624,1152]{1,0:T(8,128)S(1)} custom-call(bf16[624,384]{1,0:T(8,128)(2,1)S(1)} %get-tuple-element.48.refs_0_, bf16[312,384]{1,0:T(8,128)(2,1)S(1)} %collective-permute-done.14.refs_1_, bf16[312,384]{1,0:T(8,128)(2,1)S(1)} %collective-permute-done.15.refs_2_, bf16[3,1152,1152]{2,1,0:T(8,128)(2,1)S(1)} %get-tuple-element.47.refs_3_.packed), custom_call_target="tpu_custom_call" | custom-call | flops 3312451584 | bytes 1916928 | tf_op jit(solution)/shard_map/pallas_call | solution.py:121
  61.3 3.9 %shard_map.146 = (bf16[624,384]{1,0:T(8,128)(2,1)}, f32[384,384]{1,0:T(8,128)S(1)}, bf16[384,384]{1,0:T(8,128)(2,1)S(1)}) custom-call(bf16[416,384]{1,0:T(8,128)(2,1)S(1)} %collective-permute-done.11.tail, bf16[416,384]{1,0:T(8,128)(2,1)S(1)} %collective-permute-done.12.partner, bf16[208,384]{1,0:T(8,128)(2,1)S(1)} %collective-permute-done.13.tail_off, ...), custom_call_target="tpu_custom_call" | custom-call | flops 2208301056 | bytes 1916928 | tf_op jit(solution)/shard_map/pallas_call | solution.py:121
  65.2 4.2 %collective-permute-start.16 = (bf16[384,384]{1,0:T(8,128)(2,1)S(1)}, bf16[384,384]{1,0:T(8,128)(2,1)S(1)}, u32[]{:S(2)}, u32[]{:S(2)}) collective-permute-start(bf16[384,384]{1,0:T(8,128)(2,1)S(1)} %get-tuple-element.60), channel_id=1, source_target_pairs={{0,1},{1,0},{2,3},{3,2},{4,5},{5,4},{6,7},{7,6},{8,9},{9,8},{10,11... | collective-permute-start | bytes 884744 | tf_op jit(solution)/shard_map/ppermute | solution.py:20
  69.4 1.2 %collective-permute-done.16 = bf16[384,384]{1,0:T(8,128)(2,1)S(1)} collective-permute-done((bf16[384,384]{1,0:T(8,128)(2,1)S(1)}, bf16[384,384]{1,0:T(8,128)(2,1)S(1)}, u32[]{:S(2)}, u32[]{:S(2)}) %collective-permute-start.16) | collective-permute-done | bytes 294944 | tf_op jit(solution)/shard_map/ppermute | solution.py:20
  71.5 1.5 %collective-permute-start.18 = (bf16[96,384]{1,0:T(8,128)(2,1)S(1)}, bf16[96,384]{1,0:T(8,128)(2,1)S(1)}, u32[]{:S(2)}, u32[]{:S(2)}) collective-permute-start(bf16[96,384]{1,0:T(8,128)(2,1)S(1)} %get-tuple-element.69), channel_id=1, source_target_pairs={{0,16},{1,17},{2,18},{3,19},{16,0},{17,1},{18,2},{19,3},{4,20},{5,... | collective-permute-start | bytes 221192 | tf_op jit(solution)/shard_map/ppermute | solution.py:71
  73.0 1.2 %collective-permute-start.19 = (bf16[96,384]{1,0:T(8,128)(2,1)S(1)}, bf16[96,384]{1,0:T(8,128)(2,1)S(1)}, u32[]{:S(2)}, u32[]{:S(2)}) collective-permute-start(bf16[96,384]{1,0:T(8,128)(2,1)S(1)} %get-tuple-element.68), channel_id=1, source_target_pairs={{0,18},{1,19},{2,16},{3,17},{16,2},{17,3},{18,0},{19,1},{4,22},{5,... | collective-permute-start | bytes 221192 | tf_op jit(solution)/shard_map/ppermute | solution.py:71
  74.3 1.1 %collective-permute-done.17 = bf16[96,384]{1,0:T(8,128)(2,1)S(1)} collective-permute-done((bf16[96,384]{1,0:T(8,128)(2,1)S(1)}, bf16[96,384]{1,0:T(8,128)(2,1)S(1)}, u32[]{:S(2)}, u32[]{:S(2)}) %collective-permute-start.17) | collective-permute-done | bytes 73760 | tf_op jit(solution)/shard_map/ppermute | solution.py:71
  75.9 2.4 %collective-permute-done.19 = bf16[96,384]{1,0:T(8,128)(2,1)S(1)} collective-permute-done((bf16[96,384]{1,0:T(8,128)(2,1)S(1)}, bf16[96,384]{1,0:T(8,128)(2,1)S(1)}, u32[]{:S(2)}, u32[]{:S(2)}) %collective-permute-start.19) | collective-permute-done | bytes 73760 | tf_op jit(solution)/shard_map/ppermute | solution.py:71
  78.3 1.6 %collective-permute-start.20 = (bf16[96,384]{1,0:T(8,128)(2,1)S(1)}, bf16[96,384]{1,0:T(8,128)(2,1)S(1)}, u32[]{:S(2)}, u32[]{:S(2)}) collective-permute-start(bf16[96,384]{1,0:T(8,128)(2,1)S(1)} %add_convert_fusion.1), channel_id=1, source_target_pairs={{0,4},{4,0},{8,12},{12,8},{1,5},{5,1},{9,13},{13,9},{2,6},{6,2},{1... | collective-permute-start | bytes 221192 | tf_op jit(solution)/shard_map/ppermute | solution.py:20
  80.0 1.1 %collective-permute-start.21 = (bf16[96,384]{1,0:T(8,128)(2,1)S(1)}, bf16[96,384]{1,0:T(8,128)(2,1)S(1)}, u32[]{:S(2)}, u32[]{:S(2)}) collective-permute-start(bf16[96,384]{1,0:T(8,128)(2,1)S(1)} %add_convert_fusion.1), channel_id=1, source_target_pairs={{0,8},{4,12},{8,0},{12,4},{1,9},{5,13},{9,1},{13,5},{2,10},{6,14},... | collective-permute-start | bytes 221192 | tf_op jit(solution)/shard_map/ppermute | solution.py:20
  81.1 1.7 %collective-permute-start.22 = (bf16[96,384]{1,0:T(8,128)(2,1)S(1)}, bf16[96,384]{1,0:T(8,128)(2,1)S(1)}, u32[]{:S(2)}, u32[]{:S(2)}) collective-permute-start(bf16[96,384]{1,0:T(8,128)(2,1)S(1)} %add_convert_fusion.1), channel_id=1, source_target_pairs={{0,12},{4,8},{8,4},{12,0},{1,13},{5,9},{9,5},{13,1},{2,14},{6,10},... | collective-permute-start | bytes 221192 | tf_op jit(solution)/shard_map/ppermute | solution.py:20
  82.9 4.7 %collective-permute-done.21 = bf16[96,384]{1,0:T(8,128)(2,1)S(1)} collective-permute-done((bf16[96,384]{1,0:T(8,128)(2,1)S(1)}, bf16[96,384]{1,0:T(8,128)(2,1)S(1)}, u32[]{:S(2)}, u32[]{:S(2)}) %collective-permute-start.21) | collective-permute-done | bytes 73760 | tf_op jit(solution)/shard_map/ppermute | solution.py:20
  87.7 1.1 %collective-permute-start.23 = (bf16[96,384]{1,0:T(8,128)(2,1)S(1)}, bf16[96,384]{1,0:T(8,128)(2,1)S(1)}, u32[]{:S(2)}, u32[]{:S(2)}) collective-permute-start(bf16[96,384]{1,0:T(8,128)(2,1)S(1)} %get-tuple-element.62), channel_id=1, source_target_pairs={{0,2},{1,3},{2,0},{3,1},{16,18},{17,19},{18,16},{19,17},{4,6},{5,7... | collective-permute-start | bytes 221192 | tf_op jit(solution)/shard_map/ppermute | solution.py:71
  88.8 1.5 %collective-permute-start.24 = (bf16[96,384]{1,0:T(8,128)(2,1)S(1)}, bf16[96,384]{1,0:T(8,128)(2,1)S(1)}, u32[]{:S(2)}, u32[]{:S(2)}) collective-permute-start(bf16[96,384]{1,0:T(8,128)(2,1)S(1)} %get-tuple-element.62), channel_id=1, source_target_pairs={{0,16},{1,17},{2,18},{3,19},{16,0},{17,1},{18,2},{19,3},{4,20},{5,... | collective-permute-start | bytes 221192 | tf_op jit(solution)/shard_map/ppermute | solution.py:71
  91.3 1.4 %collective-permute-done.23 = bf16[96,384]{1,0:T(8,128)(2,1)S(1)} collective-permute-done((bf16[96,384]{1,0:T(8,128)(2,1)S(1)}, bf16[96,384]{1,0:T(8,128)(2,1)S(1)}, u32[]{:S(2)}, u32[]{:S(2)}) %collective-permute-start.23) | collective-permute-done | bytes 73760 | tf_op jit(solution)/shard_map/ppermute | solution.py:71
  93.2 2.3 %collective-permute-done.25 = bf16[96,384]{1,0:T(8,128)(2,1)S(1)} collective-permute-done((bf16[96,384]{1,0:T(8,128)(2,1)S(1)}, bf16[96,384]{1,0:T(8,128)(2,1)S(1)}, u32[]{:S(2)}, u32[]{:S(2)}) %collective-permute-start.25) | collective-permute-done | bytes 73760 | tf_op jit(solution)/shard_map/ppermute | solution.py:71
  95.6 1.6 %collective-permute-done.26 = bf16[384,384]{1,0:T(8,128)(2,1)S(1)} collective-permute-done((bf16[384,384]{1,0:T(8,128)(2,1)S(1)}, bf16[384,384]{1,0:T(8,128)(2,1)S(1)}, u32[]{:S(2)}, u32[]{:S(2)}) %collective-permute-start.26) | collective-permute-done | bytes 294944 | tf_op jit(solution)/shard_map/ppermute | solution.py:20
  97.2 1.1 %select_convert_fusion = (f32[384,384]{1,0:T(8,128)}, f32[384,384]{1,0:T(8,128)}) fusion(bf16[384,384]{1,0:T(8,128)(2,1)S(1)} %constant_dynamic-update-slice_fusion, bf16[384,384]{1,0:T(8,128)(2,1)S(1)} %collective-permute-done.26, pred[]{:T(512)S(6)} %eq.3), kind=kLoop, calls=%fused_computation.1 | loop fusion | flops 589824 | bytes 1769473 | tf_op jit(solution)/shard_map/convert_element_type | solution.py:104
  (43 shorter events, 7.2 us)
Async XLA Ops:
  2.0 10.6 %collective-permute-start = (bf16[416,384]{1,0:T(8,128)(2,1)S(1)}, bf16[416,384]{1,0:T(8,128)(2,1)S(1)}, u32[]{:S(2)}, u32[]{:S(2)}) collective-permute-start(bf16[416,384]{1,0:T(8,128)(2,1)S(1)} %get-tuple-element.32.refs_0_), channel_id=1, source_target_pairs={{0,2},{1,3},{2,0},{3,1},{4,6},{5,7},{6,4},{7,5},{8,10},{9,11},{10,... | collective-permute-start | bytes 958472 | tf_op jit(solution)/shard_map/ppermute | solution.py:20
  5.1 16.0 %collective-permute-start.1 = (bf16[416,384]{1,0:T(8,128)(2,1)S(1)}, bf16[416,384]{1,0:T(8,128)(2,1)S(1)}, u32[]{:S(2)}, u32[]{:S(2)}) collective-permute-start(bf16[416,384]{1,0:T(8,128)(2,1)S(1)} %get-tuple-element.32.refs_0_), channel_id=1, source_target_pairs={{0,1},{1,0},{2,3},{3,2},{4,5},{5,4},{6,7},{7,6},{8,9},{9,8},{10,11... | collective-permute-start | bytes 958472 | tf_op jit(solution)/shard_map/ppermute | solution.py:20
  12.6 8.5 %collective-permute-start.2 = (bf16[416,384]{1,0:T(8,128)(2,1)S(1)}, bf16[416,384]{1,0:T(8,128)(2,1)S(1)}, u32[]{:S(2)}, u32[]{:S(2)}) collective-permute-start(bf16[416,384]{1,0:T(8,128)(2,1)S(1)} %collective-permute-done.refs_1_), channel_id=1, source_target_pairs={{0,1},{1,0},{2,3},{3,2},{4,5},{5,4},{6,7},{7,6},{8,9},{9,8},{10,11... | collective-permute-start | bytes 958472 | tf_op jit(solution)/shard_map/ppermute | solution.py:20
  12.6 8.1 %collective-permute-start.6 = (bf16[208,384]{1,0:T(8,128)(2,1)S(1)}, bf16[208,384]{1,0:T(8,128)(2,1)S(1)}, u32[]{:S(2)}, u32[]{:S(2)}) collective-permute-start(bf16[208,384]{1,0:T(8,128)(2,1)S(1)} %get-tuple-element.40.refs_0_), channel_id=1, source_target_pairs={{0,2},{1,3},{2,0},{3,1},{4,6},{5,7},{6,4},{7,5},{8,10},{9,11},{10,... | collective-permute-start | bytes 479240 | tf_op jit(solution)/shard_map/ppermute | solution.py:20
  14.3 14.0 %collective-permute-start.7 = (bf16[208,384]{1,0:T(8,128)(2,1)S(1)}, bf16[208,384]{1,0:T(8,128)(2,1)S(1)}, u32[]{:S(2)}, u32[]{:S(2)}) collective-permute-start(bf16[208,384]{1,0:T(8,128)(2,1)S(1)} %get-tuple-element.40.refs_0_), channel_id=1, source_target_pairs={{0,1},{1,0},{2,3},{3,2},{4,5},{5,4},{6,7},{7,6},{8,9},{9,8},{10,11... | collective-permute-start | bytes 479240 | tf_op jit(solution)/shard_map/ppermute | solution.py:20
  14.6 6.5 %copy-start.1 = (f32[384]{0:T(512)S(1)}, f32[384]{0:T(512)}, u32[]{:S(2)}) copy-start(f32[384]{0:T(512)} %refs_8_.3) | copy-start | bytes 4612
  20.7 7.6 %collective-permute-start.8 = (bf16[208,384]{1,0:T(8,128)(2,1)S(1)}, bf16[208,384]{1,0:T(8,128)(2,1)S(1)}, u32[]{:S(2)}, u32[]{:S(2)}) collective-permute-start(bf16[208,384]{1,0:T(8,128)(2,1)S(1)} %collective-permute-done.6.refs_1_), channel_id=1, source_target_pairs={{0,1},{1,0},{2,3},{3,2},{4,5},{5,4},{6,7},{7,6},{8,9},{9,8},{10,11... | collective-permute-start | bytes 479240 | tf_op jit(solution)/shard_map/ppermute | solution.py:20
  24.8 10.7 %collective-permute-start.3 = (bf16[416,384]{1,0:T(8,128)(2,1)S(1)}, bf16[416,384]{1,0:T(8,128)(2,1)S(1)}, u32[]{:S(2)}, u32[]{:S(2)}) collective-permute-start(bf16[416,384]{1,0:T(8,128)(2,1)S(1)} %get-tuple-element.37.refs_1_), channel_id=1, source_target_pairs={{0,4},{4,8},{8,12},{1,5},{5,9},{9,13},{2,6},{6,10},{10,14},{3,7},{... | collective-permute-start | bytes 958472 | tf_op jit(solution)/shard_map/ppermute | solution.py:55
  28.3 12.4 %copy-start = (f32[384]{0:T(512)S(1)}, f32[384]{0:T(512)}, u32[]{:S(2)}) copy-start(f32[384]{0:T(512)} %gain.1) | copy-start | bytes 4612
  30.3 6.0 %collective-permute-start.10 = (bf16[312,384]{1,0:T(8,128)(2,1)S(1)}, bf16[312,384]{1,0:T(8,128)(2,1)S(1)}, u32[]{:S(2)}, u32[]{:S(2)}) collective-permute-start(bf16[312,384]{1,0:T(8,128)(2,1)S(1)} %get-tuple-element.44), channel_id=1, source_target_pairs={{0,1},{1,0},{2,3},{3,2},{4,5},{5,4},{6,7},{7,6},{8,9},{9,8},{10,11... | collective-permute-start | bytes 718856 | tf_op jit(solution)/shard_map/ppermute | solution.py:20
  30.4 5.9 %collective-permute-start.9 = (bf16[312,384]{1,0:T(8,128)(2,1)S(1)}, bf16[312,384]{1,0:T(8,128)(2,1)S(1)}, u32[]{:S(2)}, u32[]{:S(2)}) collective-permute-start(bf16[312,384]{1,0:T(8,128)(2,1)S(1)} %get-tuple-element.43), channel_id=1, source_target_pairs={{1,2},{2,1},{5,6},{6,5},{9,10},{10,9},{13,14},{14,13},{17,18},{18,... | collective-permute-start | bytes 718856 | tf_op jit(solution)/shard_map/ppermute | solution.py:40
  35.5 5.3 %collective-permute-start.4 = (bf16[416,384]{1,0:T(8,128)(2,1)S(1)}, bf16[416,384]{1,0:T(8,128)(2,1)S(1)}, u32[]{:S(2)}, u32[]{:S(2)}) collective-permute-start(bf16[416,384]{1,0:T(8,128)(2,1)S(1)} %collective-permute-done.3.tail), channel_id=1, source_target_pairs={{0,1},{1,0},{2,3},{3,2},{4,5},{5,4},{6,7},{7,6},{8,9},{9,8},{10,11... | collective-permute-start | bytes 958472 | tf_op jit(solution)/shard_map/ppermute | solution.py:20
  35.5 5.3 %collective-permute-start.5 = (bf16[208,384]{1,0:T(8,128)(2,1)S(1)}, bf16[208,384]{1,0:T(8,128)(2,1)S(1)}, u32[]{:S(2)}, u32[]{:S(2)}) collective-permute-start(bf16[208,384]{1,0:T(8,128)(2,1)S(1)} %get-tuple-element.38.refs_10_), channel_id=1, source_target_pairs={{1,6},{2,5},{5,10},{6,9},{9,14},{10,13},{17,22},{18,21},{21,26},{2... | collective-permute-start | bytes 479240 | tf_op jit(solution)/shard_map/ppermute | solution.py:50
  43.6 10.9 %collective-permute-start.11 = (bf16[416,384]{1,0:T(8,128)(2,1)S(1)}, bf16[416,384]{1,0:T(8,128)(2,1)S(1)}, u32[]{:S(2)}, u32[]{:S(2)}) collective-permute-start(bf16[416,384]{1,0:T(8,128)(2,1)S(1)} %get-tuple-element.45), channel_id=1, source_target_pairs={{0,4},{4,8},{8,12},{1,5},{5,9},{9,13},{2,6},{6,10},{10,14},{3,7},{... | collective-permute-start | bytes 958472 | tf_op jit(solution)/shard_map/ppermute | solution.py:55
  48.0 8.9 %collective-permute-start.14 = (bf16[312,384]{1,0:T(8,128)(2,1)S(1)}, bf16[312,384]{1,0:T(8,128)(2,1)S(1)}, u32[]{:S(2)}, u32[]{:S(2)}) collective-permute-start(bf16[312,384]{1,0:T(8,128)(2,1)S(1)} %get-tuple-element.49), channel_id=1, source_target_pairs={{1,2},{2,1},{5,6},{6,5},{9,10},{10,9},{13,14},{14,13},{17,18},{18,... | collective-permute-start | bytes 718856 | tf_op jit(solution)/shard_map/ppermute | solution.py:40
  48.7 8.2 %collective-permute-start.15 = (bf16[312,384]{1,0:T(8,128)(2,1)S(1)}, bf16[312,384]{1,0:T(8,128)(2,1)S(1)}, u32[]{:S(2)}, u32[]{:S(2)}) collective-permute-start(bf16[312,384]{1,0:T(8,128)(2,1)S(1)} %get-tuple-element.50), channel_id=1, source_target_pairs={{0,1},{1,0},{2,3},{3,2},{4,5},{5,4},{6,7},{7,6},{8,9},{9,8},{10,11... | collective-permute-start | bytes 718856 | tf_op jit(solution)/shard_map/ppermute | solution.py:20
  54.5 6.9 %collective-permute-start.12 = (bf16[416,384]{1,0:T(8,128)(2,1)S(1)}, bf16[416,384]{1,0:T(8,128)(2,1)S(1)}, u32[]{:S(2)}, u32[]{:S(2)}) collective-permute-start(bf16[416,384]{1,0:T(8,128)(2,1)S(1)} %collective-permute-done.11.tail), channel_id=1, source_target_pairs={{0,1},{1,0},{2,3},{3,2},{4,5},{5,4},{6,7},{7,6},{8,9},{9,8},{10,11... | collective-permute-start | bytes 958472 | tf_op jit(solution)/shard_map/ppermute | solution.py:20
  56.0 5.3 %collective-permute-start.13 = (bf16[208,384]{1,0:T(8,128)(2,1)S(1)}, bf16[208,384]{1,0:T(8,128)(2,1)S(1)}, u32[]{:S(2)}, u32[]{:S(2)}) collective-permute-start(bf16[208,384]{1,0:T(8,128)(2,1)S(1)} %get-tuple-element.46), channel_id=1, source_target_pairs={{1,6},{2,5},{5,10},{6,9},{9,14},{10,13},{17,22},{18,21},{21,26},{2... | collective-permute-start | bytes 479240 | tf_op jit(solution)/shard_map/ppermute | solution.py:50
  65.2 5.4 %collective-permute-start.16 = (bf16[384,384]{1,0:T(8,128)(2,1)S(1)}, bf16[384,384]{1,0:T(8,128)(2,1)S(1)}, u32[]{:S(2)}, u32[]{:S(2)}) collective-permute-start(bf16[384,384]{1,0:T(8,128)(2,1)S(1)} %get-tuple-element.60), channel_id=1, source_target_pairs={{0,1},{1,0},{2,3},{3,2},{4,5},{5,4},{6,7},{7,6},{8,9},{9,8},{10,11... | collective-permute-start | bytes 884744 | tf_op jit(solution)/shard_map/ppermute | solution.py:20
  70.7 4.6 %collective-permute-start.17 = (bf16[96,384]{1,0:T(8,128)(2,1)S(1)}, bf16[96,384]{1,0:T(8,128)(2,1)S(1)}, u32[]{:S(2)}, u32[]{:S(2)}) collective-permute-start(bf16[96,384]{1,0:T(8,128)(2,1)S(1)} %get-tuple-element.67), channel_id=1, source_target_pairs={{0,2},{1,3},{2,0},{3,1},{16,18},{17,19},{18,16},{19,17},{4,6},{5,7... | collective-permute-start | bytes 221192 | tf_op jit(solution)/shard_map/ppermute | solution.py:71
  71.5 4.4 %collective-permute-start.18 = (bf16[96,384]{1,0:T(8,128)(2,1)S(1)}, bf16[96,384]{1,0:T(8,128)(2,1)S(1)}, u32[]{:S(2)}, u32[]{:S(2)}) collective-permute-start(bf16[96,384]{1,0:T(8,128)(2,1)S(1)} %get-tuple-element.69), channel_id=1, source_target_pairs={{0,16},{1,17},{2,18},{3,19},{16,0},{17,1},{18,2},{19,3},{4,20},{5,... | collective-permute-start | bytes 221192 | tf_op jit(solution)/shard_map/ppermute | solution.py:71
  73.0 5.3 %collective-permute-start.19 = (bf16[96,384]{1,0:T(8,128)(2,1)S(1)}, bf16[96,384]{1,0:T(8,128)(2,1)S(1)}, u32[]{:S(2)}, u32[]{:S(2)}) collective-permute-start(bf16[96,384]{1,0:T(8,128)(2,1)S(1)} %get-tuple-element.68), channel_id=1, source_target_pairs={{0,18},{1,19},{2,16},{3,17},{16,2},{17,3},{18,0},{19,1},{4,22},{5,... | collective-permute-start | bytes 221192 | tf_op jit(solution)/shard_map/ppermute | solution.py:71
  78.3 4.6 %collective-permute-start.20 = (bf16[96,384]{1,0:T(8,128)(2,1)S(1)}, bf16[96,384]{1,0:T(8,128)(2,1)S(1)}, u32[]{:S(2)}, u32[]{:S(2)}) collective-permute-start(bf16[96,384]{1,0:T(8,128)(2,1)S(1)} %add_convert_fusion.1), channel_id=1, source_target_pairs={{0,4},{4,0},{8,12},{12,8},{1,5},{5,1},{9,13},{13,9},{2,6},{6,2},{1... | collective-permute-start | bytes 221192 | tf_op jit(solution)/shard_map/ppermute | solution.py:20
  80.0 7.7 %collective-permute-start.21 = (bf16[96,384]{1,0:T(8,128)(2,1)S(1)}, bf16[96,384]{1,0:T(8,128)(2,1)S(1)}, u32[]{:S(2)}, u32[]{:S(2)}) collective-permute-start(bf16[96,384]{1,0:T(8,128)(2,1)S(1)} %add_convert_fusion.1), channel_id=1, source_target_pairs={{0,8},{4,12},{8,0},{12,4},{1,9},{5,13},{9,1},{13,5},{2,10},{6,14},... | collective-permute-start | bytes 221192 | tf_op jit(solution)/shard_map/ppermute | solution.py:20
  81.1 6.6 %collective-permute-start.22 = (bf16[96,384]{1,0:T(8,128)(2,1)S(1)}, bf16[96,384]{1,0:T(8,128)(2,1)S(1)}, u32[]{:S(2)}, u32[]{:S(2)}) collective-permute-start(bf16[96,384]{1,0:T(8,128)(2,1)S(1)} %add_convert_fusion.1), channel_id=1, source_target_pairs={{0,12},{4,8},{8,4},{12,0},{1,13},{5,9},{9,5},{13,1},{2,14},{6,10},... | collective-permute-start | bytes 221192 | tf_op jit(solution)/shard_map/ppermute | solution.py:20
  87.7 4.9 %collective-permute-start.23 = (bf16[96,384]{1,0:T(8,128)(2,1)S(1)}, bf16[96,384]{1,0:T(8,128)(2,1)S(1)}, u32[]{:S(2)}, u32[]{:S(2)}) collective-permute-start(bf16[96,384]{1,0:T(8,128)(2,1)S(1)} %get-tuple-element.62), channel_id=1, source_target_pairs={{0,2},{1,3},{2,0},{3,1},{16,18},{17,19},{18,16},{19,17},{4,6},{5,7... | collective-permute-start | bytes 221192 | tf_op jit(solution)/shard_map/ppermute | solution.py:71
  88.8 4.4 %collective-permute-start.24 = (bf16[96,384]{1,0:T(8,128)(2,1)S(1)}, bf16[96,384]{1,0:T(8,128)(2,1)S(1)}, u32[]{:S(2)}, u32[]{:S(2)}) collective-permute-start(bf16[96,384]{1,0:T(8,128)(2,1)S(1)} %get-tuple-element.62), channel_id=1, source_target_pairs={{0,16},{1,17},{2,18},{3,19},{16,0},{17,1},{18,2},{19,3},{4,20},{5,... | collective-permute-start | bytes 221192 | tf_op jit(solution)/shard_map/ppermute | solution.py:71
  90.3 5.3 %collective-permute-start.25 = (bf16[96,384]{1,0:T(8,128)(2,1)S(1)}, bf16[96,384]{1,0:T(8,128)(2,1)S(1)}, u32[]{:S(2)}, u32[]{:S(2)}) collective-permute-start(bf16[96,384]{1,0:T(8,128)(2,1)S(1)} %get-tuple-element.62), channel_id=1, source_target_pairs={{0,18},{1,19},{2,16},{3,17},{16,2},{17,3},{18,0},{19,1},{4,22},{5,... | collective-permute-start | bytes 221192 | tf_op jit(solution)/shard_map/ppermute | solution.py:71
  95.6 1.6 %collective-permute-start.26 = (bf16[384,384]{1,0:T(8,128)(2,1)S(1)}, bf16[384,384]{1,0:T(8,128)(2,1)S(1)}, u32[]{:S(2)}, u32[]{:S(2)}) collective-permute-start(bf16[384,384]{1,0:T(8,128)(2,1)S(1)} %constant_dynamic-update-slice_fusion), channel_id=1, source_target_pairs={{0,1},{1,0},{2,3},{3,2},{4,5},{5,4},{6,7},{7,6},{8,9},{9,8},{10,11... | collective-permute-start | bytes 884744 | tf_op jit(solution)/shard_map/ppermute | solution.py:20
where the time goes:
time: 98.6 us; the launch traced here: 98.3 us
  starting transfers between devices  39.6 us (40%)
  Pallas kernels  28.6 us (29%)
  waiting for transfers between devices  27.8 us (28%)
  other arithmetic  1.26 us (1%)
    pallas_call x8, Pallas kernels, call(): pl.pallas_call(body, out_shape=outs, in_specs=specs, out_specs=out_specs,...  28.6 us
    ppermute x15, starting transfers between devices, xor_permute(): return lax.ppermute(value, axis, [(i, i ^ mask) for i in range(count)])  21.5 us
    ppermute x15, waiting for transfers between devices, xor_permute(): return lax.ppermute(value, axis, [(i, i ^ mask) for i in range(count)])  15.2 us
    ppermute x6, waiting for transfers between devices, plane_permute(): return lax.ppermute(value, ('dp', 'space'), pairs)  8.24 us
    ppermute x2, starting transfers between devices, next_frames(): return lax.ppermute(value, 'tm', [(i, i + 1) for i in range(count - 1)])  7.9 us
    ppermute x6, starting transfers between devices, plane_permute(): return lax.ppermute(value, ('dp', 'space'), pairs)  7.11 us
    ppermute x2, waiting for transfers between devices, next_frames(): return lax.ppermute(value, 'tm', [(i, i + 1) for i in range(count - 1)])  4.37 us
  transfers between devices with their start and end apart: 27, of which 12 were waited for; matrix products, arithmetic and copies ran while one was open for 0% of the time, Pallas kernels for 21%

commit v1 on v0

--- a/solution.py
+++ b/solution.py
@@ -37,7 +37,15 @@
 
 
 def across_permute(value):
-    return lax.ppermute(value, "space", across_pairs())
+    clips, count = lax.axis_size("dp"), lax.axis_size("space")
+    rows = dict(across_pairs())
+    pairs = []
+    for clip in range(clips):
+        for place in range(count):
+            other = (clip, rows[place]) if place in rows else (clip ^ 1, place)
+            if other[0] < clips:
+                pairs.append((clip * count + place, other[0] * count + other[1]))
+    return lax.ppermute(value, ("dp", "space"), pairs)
 
 
 def across_next_frames(value):
@@ -50,9 +58,19 @@
     return lax.ppermute(value, ("tm", "space"), pairs)
 
 
-def next_frames(value):
-    count = lax.axis_size("tm")
-    return lax.ppermute(value, "tm", [(i, i + 1) for i in range(count - 1)])
+def frame_pairings(value):
+    blocks, count = lax.axis_size("tm"), lax.axis_size("space")
+    results = []
+    for first in range(2):
+        pairs = []
+        for block in range(blocks):
+            other = ((block - first) ^ 1) + first
+            for place in range(count):
+                inside = 0 <= other < blocks
+                target = other * count + place if inside else block * count + (place ^ 1)
+                pairs.append((block * count + place, target))
+        results.append(lax.ppermute(value, ("tm", "space"), pairs))
+    return results
 
 
 def take_rows(value, index, rows):
@@ -142,6 +160,18 @@
     return lax.rem(lax.axis_index("space"), 2) == 1
 
 
+def has_across():
+    place = lax.axis_index("space")
+    return jnp.logical_and(place > 0, place < lax.axis_size("space") - 1)
+
+
+def choose_frames(pair, here):
+    block = lax.axis_index("tm")
+    low, high = pair[0][here], pair[1][here]
+    chosen = jnp.where(lax.rem(block, 2) == 1, low, high)
+    return jnp.where(block > 0, chosen, jnp.zeros_like(chosen))
+
+
 def edge_rows(values, columns, odd):
     first, last = values[:columns], values[values.shape[0] - columns :]
     return jnp.where(odd, first, last), jnp.where(odd, last, first)
@@ -167,7 +197,7 @@
 
 def prepare_body(
     latent, query_hbm, key_hbm, value_hbm, out_hbm, in_hbm, back_hbm, first_hbm, second_hbm,
-    w_query, w_both, w_out, s_out, first, second, pre, hidden_t, latent_t, predicted,
+    w_query, w_both, w_out, s_out, first, second, slope, hidden_t, latent_t, predicted,
     s_in, sems,
 ):
     channels = latent.shape[1]
@@ -196,7 +226,8 @@
     student[0].wait()
     before = dot(tokens, s_in[...])
     hidden = silu(before).astype(BF16)
-    pre[...] = before
+    logistic = jax.nn.sigmoid(before)
+    slope[...] = logistic * (1.0 + before * (1.0 - logistic))
     hidden_t[...] = hidden.T
     student[1].wait()
     predicted[...] = tokens.astype(F32) + dot(hidden, s_out[...])
@@ -269,6 +300,7 @@
 
 def own_body(groups, columns, *refs):
     odd = is_odd()
+    far = has_across()
     off, on, packed, partial, stacked = refs[-5:]
     frame_count = sum(groups)
     per_frame = partial.shape[0] // frame_count
@@ -277,8 +309,8 @@
         for frame in range(frames):
             edge = pl.ds(at * columns, columns)
             stack_rows(
-                columns, odd, own[pl.ds(frame * per_frame, per_frame)], on[edge], off[edge],
-                stacked, at,
+                columns, odd, own[pl.ds(frame * per_frame, per_frame)], on[edge],
+                jnp.where(far, off[edge], jnp.zeros_like(off[edge])), stacked, at,
             )
             at += 1
     sources = range(2, frame_count + 2)
@@ -287,26 +319,52 @@
         partial[pl.ds(frame * per_frame, per_frame)] = total
 
 
-def stack_earlier(columns, odd, tail, partner, off, stacked):
+def earlier_body(columns, low, high, off, packed, partial, total, stacked):
+    odd = is_odd()
     per_frame = stacked.shape[0] // 2
     for frame in range(2):
+        tail = choose_frames((low, high), pl.ds(frame * per_frame, per_frame))
+        edge = off[pl.ds(frame * columns, columns)]
+        stack_rows(columns, odd, tail, jnp.zeros_like(edge), edge, stacked, frame)
+    for frame in range(partial.shape[0] // per_frame):
         here = pl.ds(frame * per_frame, per_frame)
-        on, _ = edge_rows(partner[here], columns, jnp.logical_not(odd))
-        edge = pl.ds(frame * columns, columns)
-        stack_rows(columns, odd, tail[here], on, off[edge], stacked, frame)
+        total[here] = taps_sum((0, 1), frame, stacked, packed, per_frame, partial[here])
+
+
+def partner_terms(columns, odd, pair, packed):
+    per_frame = pair[0].shape[0] // 2
+    channels = pair[0].shape[1]
+    tap_row = pl.ds(pl.multiple_of(jnp.where(odd, 0, 2 * channels), channels), channels)
+    edges = []
+    for source in range(2):
+        rows = choose_frames(pair, pl.ds(source * per_frame, per_frame))
+        edges.append(edge_rows(rows, columns, jnp.logical_not(odd))[0])
+    terms = []
+    for frame in range(2):
+        term = None
+        for source in range(frame, 2):
+            part = dot(edges[source], packed[source - frame, tap_row])
+            term = part if term is None else term + part
+        zeros = jnp.zeros_like(term)
+        pieces = [jnp.where(odd, term, zeros), jnp.where(odd, zeros, term)]
+        if per_frame > 2 * columns:
+            pieces.insert(1, jnp.zeros((per_frame - 2 * columns, term.shape[1]), F32))
+        terms.append(jnp.concatenate(pieces, axis=0))
+    return terms
 
 
 def first_body(
-    columns, tail, partner, tail_off, packed, partial, gain, act, late, on, off,
-    off_late, stacked,
+    columns, low, high, packed, partial, gain, act, late, on, off, off_late
 ):
     odd = is_odd()
-    stack_earlier(columns, odd, tail, partner, tail_off, stacked)
-    per_frame = stacked.shape[0] // 2
+    terms = partner_terms(columns, odd, (low, high), packed)
+    per_frame = low.shape[0] // 2
     frame_count = partial.shape[0] // per_frame
     for frame in range(frame_count - 1, -1, -1):
         here = pl.ds(frame * per_frame, per_frame)
-        total = taps_sum((0, 1), frame, stacked, packed, per_frame, partial[here])
+        total = partial[here]
+        if frame < 2:
+            total = total + terms[frame]
         total = shift_columns(total, columns)
         active = silu(root_norm(total, gain[...].reshape(1, -1))).astype(BF16)
         act[here] = active
@@ -320,16 +378,18 @@
 
 
 def last_body(
-    columns, token_total, tail, partner, tail_off, packed, partial, mid_early, mid_late,
-    pre, hidden_t, latent_t, predicted, s_out, teacher, mine, yours, stacked, signals,
+    columns, token_total, low, high, packed, partial, mid_early, mid_late,
+    slope, hidden_t, latent_t, predicted, s_out, teacher, mine, yours, signals,
 ):
     odd = is_odd()
-    stack_earlier(columns, odd, tail, partner, tail_off, stacked)
-    per_frame = stacked.shape[0] // 2
+    terms = partner_terms(columns, odd, (low, high), packed)
+    per_frame = low.shape[0] // 2
     frame_count = partial.shape[0] // per_frame
     for frame in range(frame_count - 1, -1, -1):
         here = pl.ds(frame * per_frame, per_frame)
-        total = taps_sum((0, 1), frame, stacked, packed, per_frame, partial[here])
+        total = partial[here]
+        if frame < 2:
+            total = total + terms[frame]
         total = shift_columns(total, columns)
         at = frame - (frame_count - 2)
         mid = mid_late[pl.ds(at * per_frame, per_frame)] if at >= 0 else mid_early[here]
@@ -344,9 +404,7 @@
     back = lax.dot_general(
         signal, s_out[...], (((1,), (1,)), ((), ())), preferred_element_type=F32
     )
-    before = pre[...]
-    logistic = jax.nn.sigmoid(before)
-    back_pre = (back * logistic * (1.0 + before * (1.0 - logistic))).astype(BF16)
+    back_pre = (back * slope[...]).astype(BF16)
     grad_in = dot(latent_t[...], back_pre)
     mine[...] = jnp.where(odd, grad_out, grad_in)
     yours[...] = jnp.where(odd, grad_in, grad_out).astype(BF16)
@@ -395,7 +453,7 @@
     weights = (w_query, w_key, w_value, w_out, student_in, student_out, conv_first, conv_second)
     (
         w_query, w_both, w_out, student_out, packed_first, packed_second,
-        pre, hidden_t, latent_t, predicted,
+        slope, hidden_t, latent_t, predicted,
     ) = call(
         prepare_body,
         [square, shape(channels, 2 * channels, BF16), square, square, packed_shape, packed_shape,
@@ -420,13 +478,22 @@
         return pltpu.VMEM((count * per_frame, 3 * channels), BF16)
 
     def from_earlier(late, off):
-        tail = next_frames(late)
+        pair = frame_pairings(late)
         corner = across_next_frames(off)
-        partner = xor_permute(tail, "space", 1)
-        return tail, corner, partner
+        partner = [xor_permute(frames, "space", 1) for frames in pair]
+        return pair, corner, partner
+
+    def earlier_part(pair, corner, packed, partial):
+        args = [*pair, corner, packed, partial]
+        return call(
+            functools.partial(earlier_body, columns),
+            shape(tokens, 3 * channels, F32), [VMEM] * len(args), VMEM,
+            [stacked(2)], 9 * tokens * unit, 8 * tokens * channels, *args,
+        )
 
     def own_part(groups, on, off, packed):
-        halo = [across_permute(off), xor_permute(on, "space", 1)]
+        halo = [across_permute(off)]
+        halo.append(xor_permute(on, "space", 1))
         args = [*(own for _, own in groups), *halo, packed]
         return call(
             functools.partial(own_body, [group[0] for group in groups], columns),
@@ -435,28 +502,30 @@
         )
 
     act_late, mid_late, on_late, off_late = attend(blocks_late, early, 2)
-    tail, tail_off, partner = from_earlier(act_late, off_late)
+    pair, corner, partner = from_earlier(act_late, off_late)
     act_early, mid_early, on, off = attend(blocks_early, 0, early, on_late, off_late)
     partial = own_part([(early, act_early), (2, act_late)], on, off, packed_first)
-    args = [tail, partner, tail_off, packed_first, partial, conv_gain_second]
+    partial = earlier_part(pair, corner, packed_first, partial)
+    args = [*partner, packed_first, partial, conv_gain_second]
     act, late, on, off, off_late = call(
         functools.partial(first_body, columns),
         [rows_of(frame_count), rows_of(2), edges_of(frame_count), edges_of(frame_count), edges_of(2)],
-        [VMEM] * len(args), [VMEM] * 5, [stacked(2)],
+        [VMEM] * len(args), [VMEM] * 5, [],
         9 * tokens * unit, 8 * tokens * channels, *args,
     )
-    tail, tail_off, partner = from_earlier(late, off_late)
+    pair, corner, partner = from_earlier(late, off_late)
     partial = own_part([(frame_count, act)], on, off, packed_second)
     token_total = tokens * lax.axis_size("dp") * lax.axis_size("tm") * lax.axis_size("space")
+    partial = earlier_part(pair, corner, packed_second, partial)
     args = [
-        tail, partner, tail_off, packed_second, partial, mid_early, mid_late,
-        pre, hidden_t, latent_t, predicted, student_out,
+        *partner, packed_second, partial, mid_early, mid_late,
+        slope, hidden_t, latent_t, predicted, student_out,
     ]
     teacher, mine, yours = call(
         functools.partial(last_body, columns, token_total),
         [rows_of(frame_count), shape(channels, channels, F32), square],
         [VMEM] * len(args), [VMEM] * 3,
-        [stacked(2), pltpu.VMEM((tokens, channels), BF16)],
+        [pltpu.VMEM((tokens, channels), BF16)],
         12 * tokens * unit, 8 * tokens * channels, *args,
     )
     grad_in, grad_out = sum_everywhere(mine, yours)

time: 98.6 us -> 94.2 us (0.955)
  starting transfers between devices: 39.6 us -> 28.6 us
  waiting for transfers between devices: 27.8 us -> 32.5 us
  Pallas kernels: 28.6 us -> 30.7 us
    ppermute x15 -> x17, starting transfers between devices: 21.5 us -> 12.3 us  [xor_permute(): return lax.ppermute(value, axis, [(i, i ^ mask) for i in range(count)])]
    ppermute x4 -> x6, waiting for transfers between devices: 4.38 us -> 9.24 us  [the longest x4 9.23 us: frame_pairings(): results.append(lax.ppermute(value, ('tm', 'space'), pairs))]
    pallas_call x8 -> x10, Pallas kernels: 28.6 us -> 30.7 us  [call(): pl.pallas_call(body, out_shape=outs, in_specs=specs, out_specs=out_specs,...]
    ppermute x4 -> x6, starting transfers between devices: 9.26 us -> 7.48 us  [the longest x4 4.43 us: frame_pairings(): results.append(lax.ppermute(value, ('tm', 'space'), pairs))]
    ppermute x6, waiting for transfers between devices: 8.24 us -> 6.96 us  [plane_permute(): return lax.ppermute(value, ('dp', 'space'), pairs)]
    ppermute x15 -> x17, waiting for transfers between devices: 15.2 us -> 16.3 us  [xor_permute(): return lax.ppermute(value, axis, [(i, i ^ mask) for i in range(count)])]
  transfers between devices with their start and end apart: 27 -> 31, of which waited for: 12 -> 12; matrix products, arithmetic and copies ran while one was open for 0% -> 0% of each run, Pallas kernels for 21% -> 27%
where the time goes in v1:
time: 94.2 us; the launch traced here: 94 us
  waiting for transfers between devices  32.5 us (35%)
  Pallas kernels  30.7 us (33%)
  starting transfers between devices  28.6 us (30%)
  other arithmetic  1.26 us (1%)
    pallas_call x10, Pallas kernels, call(): pl.pallas_call(body, out_shape=outs, in_specs=specs, out_specs=out_specs,...  30.7 us
    ppermute x17, waiting for transfers between devices, xor_permute(): return lax.ppermute(value, axis, [(i, i ^ mask) for i in range(count)])  16.3 us
    ppermute x17, starting transfers between devices, xor_permute(): return lax.ppermute(value, axis, [(i, i ^ mask) for i in range(count)])  12.3 us
    ppermute x4, waiting for transfers between devices, frame_pairings(): results.append(lax.ppermute(value, ('tm', 'space'), pairs))  9.23 us
    ppermute x6, starting transfers between devices, plane_permute(): return lax.ppermute(value, ('dp', 'space'), pairs)  7.11 us
    ppermute x6, waiting for transfers between devices, plane_permute(): return lax.ppermute(value, ('dp', 'space'), pairs)  6.96 us
    ppermute x4, starting transfers between devices, frame_pairings(): results.append(lax.ppermute(value, ('tm', 'space'), pairs))  4.43 us
    ppermute x2, starting transfers between devices, across_permute(): return lax.ppermute(value, ('dp', 'space'), pairs)  3.06 us
  transfers between devices with their start and end apart: 31, of which 12 were waited for; matrix products, arithmetic and copies ran while one was open for 0% of the time, Pallas kernels for 27%

profile of v1, /device:TPU:0, one launch (start us, length us, event | category | flops | bytes accessed | tf_op | source)
XLA Modules:
  0.0 94.0 jit_solution(7487423454910067663)
XLA Ops:
  0.6 1.4 %shard_map.139 = (bf16[624,384]{1,0:T(8,128)(2,1)S(1)}, bf16[416,384]{1,0:T(8,128)(2,1)S(1)}, bf16[208,384]{1,0:T(8,128)(2,1)S(1)}) custom-call(bf16[3,208,384]{2,1,0:T(8,128)(2,1)} %bitcast.2, f32[384]{0:T(512)} %gain_hbm.1), custom_call_target="tpu_custom_call" | custom-call | bytes 958464 | tf_op jit(solution)/shard_map/pallas_call | solution.py:139
  2.0 3.1 %collective-permute-start = (bf16[416,384]{1,0:T(8,128)(2,1)S(1)}, bf16[416,384]{1,0:T(8,128)(2,1)S(1)}, u32[]{:S(2)}, u32[]{:S(2)}) collective-permute-start(bf16[416,384]{1,0:T(8,128)(2,1)S(1)} %get-tuple-element.32.refs_0_), channel_id=1, source_target_pairs={{0,2},{1,3},{2,0},{3,1},{4,6},{5,7},{6,4},{7,5},{8,10},{9,11},{10,... | collective-permute-start | bytes 958472 | tf_op jit(solution)/shard_map/ppermute | solution.py:20
  5.1 7.5 %collective-permute-done.refs_1_ = bf16[416,384]{1,0:T(8,128)(2,1)S(1)} collective-permute-done((bf16[416,384]{1,0:T(8,128)(2,1)S(1)}, bf16[416,384]{1,0:T(8,128)(2,1)S(1)}, u32[]{:S(2)}, u32[]{:S(2)}) %collective-permute-start) | collective-permute-done | bytes 319520 | tf_op jit(solution)/shard_map/ppermute | solution.py:20
  12.6 1.7 %collective-permute-start.8 = (bf16[208,384]{1,0:T(8,128)(2,1)S(1)}, bf16[208,384]{1,0:T(8,128)(2,1)S(1)}, u32[]{:S(2)}, u32[]{:S(2)}) collective-permute-start(bf16[208,384]{1,0:T(8,128)(2,1)S(1)} %get-tuple-element.40.refs_0_), channel_id=1, source_target_pairs={{0,2},{1,3},{2,0},{3,1},{4,6},{5,7},{6,4},{7,5},{8,10},{9,11},{10,... | collective-permute-start | bytes 479240 | tf_op jit(solution)/shard_map/ppermute | solution.py:20
  14.6 6.1 %shard_map.140 = (bf16[384,384]{1,0:T(8,128)(2,1)S(1)}, bf16[384,768]{1,0:T(8,128)(2,1)S(1)}, bf16[384,384]{1,0:T(8,128)(2,1)S(1)}, bf16[384,384]{1,0:T(8,128)(2...) custom-call(bf16[624,384]{1,0:T(8,128)(2,1)S(1)} %get-tuple-element., ...), custom_call_target="tpu_custom_call" | custom-call | flops 368050176 | bytes 17694720 | tf_op jit(solution)/shard_map/pallas_call | solution.py:139
  21.1 3.7 %shard_map.141 = (bf16[416,384]{1,0:T(8,128)(2,1)S(1)}, bf16[416,384]{1,0:T(8,128)(2,1)S(1)}, bf16[208,384]{1,0:T(8,128)(2,1)S(1)}, bf16[208,384]{1,0:T(8,128)(2,1)S(1)}) custom-call(bf16[416,384]{1,0:T(8,128)(2,1)S(1)} %get-tuple-element.32.refs_0_, bf16[416,384]{1,0:T(8,128)(2,1)S(1)} %collective-permute-done.refs_1_, ...), custom_call_target="tpu_custom_call" | custom-call | flops 2208301056 | bytes 638976 | tf_op jit(solution)/shard_map/pallas_call | solution.py:139
  24.8 1.6 %collective-permute-start.3 = (bf16[416,384]{1,0:T(8,128)(2,1)S(1)}, bf16[416,384]{1,0:T(8,128)(2,1)S(1)}, u32[]{:S(2)}, u32[]{:S(2)}) collective-permute-start(bf16[416,384]{1,0:T(8,128)(2,1)S(1)} %get-tuple-element.37.refs_1_), channel_id=1, source_target_pairs={{0,4},{1,5},{2,6},{3,7},{4,0},{5,1},{6,2},{7,3},{8,12},{9,13},{10,... | collective-permute-start | bytes 958472 | tf_op jit(solution)/shard_map/ppermute | solution.py:72
  26.5 2.0 %shard_map.142 = (bf16[208,384]{1,0:T(8,128)(2,1)S(1)}, bf16[208,384]{1,0:T(8,128)(2,1)S(1)}, bf16[312,384]{1,0:T(8,128)(2,1)S(1)}, bf16[312,384]{1,0:T(8,128)(2,1)S(1)}) custom-call(bf16[208,384]{1,0:T(8,128)(2,1)S(1)} %get-tuple-element.40.refs_0_, bf16[208,384]{1,0:T(8,128)(2,1)S(1)} %collective-permute-done.8.refs_1_, ...), custom_call_target="tpu_custom_call" | custom-call | flops 1104150528 | bytes 319488 | tf_op jit(solution)/shard_map/pallas_call | solution.py:139
  28.4 1.6 %collective-permute-start.11 = (bf16[312,384]{1,0:T(8,128)(2,1)S(1)}, bf16[312,384]{1,0:T(8,128)(2,1)S(1)}, u32[]{:S(2)}, u32[]{:S(2)}) collective-permute-start(bf16[312,384]{1,0:T(8,128)(2,1)S(1)} %get-tuple-element.43), channel_id=1, source_target_pairs={{0,16},{1,2},{2,1},{3,19},{16,0},{17,18},{18,17},{19,3},{4,20},{5,... | collective-permute-start | bytes 718856 | tf_op jit(solution)/shard_map/ppermute | solution.py:48
  30.8 3.7 %collective-permute-done.3.low = bf16[416,384]{1,0:T(8,128)(2,1)S(1)} collective-permute-done((bf16[416,384]{1,0:T(8,128)(2,1)S(1)}, bf16[416,384]{1,0:T(8,128)(2,1)S(1)}, u32[]{:S(2)}, u32[]{:S(2)}) %collective-permute-start.3) | collective-permute-done | bytes 319520 | tf_op jit(solution)/shard_map/ppermute | solution.py:72
  35.1 4.4 %shard_map.143.partial = f32[624,1152]{1,0:T(8,128)S(1)} custom-call(bf16[208,384]{1,0:T(8,128)(2,1)S(1)} %get-tuple-element.42.refs_0_, bf16[416,384]{1,0:T(8,128)(2,1)S(1)} %get-tuple-element.37.refs_1_, bf16[312,384]{1,0:T(8,128)(2,1)S(1)} %collective-permute-done.11.refs_2_, bf16[312,384]{1,0:T(8,128)(2,1)S(1)} %collective-permute-done.12.refs_3_, ...), custom_call_target="tpu_custom_call" | custom-call | flops 3312451584 | bytes 1916928 | tf_op jit(solution)/shard_map/pallas_call | solution.py:139
  39.5 2.3 %shard_map.144.partial = f32[624,1152]{1,0:T(8,128)S(1)} custom-call(bf16[416,384]{1,0:T(8,128)(2,1)S(1)} %collective-permute-done.3.low, bf16[416,384]{1,0:T(8,128)(2,1)S(1)} %collective-permute-done.5.high, bf16[208,384]{1,0:T(8,128)(2,1)S(1)} %collective-permute-done.7.off, bf16[3,1152,1152]{2,1,0:T(8,128)(2,1)S(1)} %get-tuple-element.38.refs_4_.packed, ...), custom_call_target="tpu_custom_call" | custom-call | flops 1656225792 | bytes 1916928 | tf_op jit(solution)/shard_map/pallas_call | solution.py:139
  41.8 1.3 %shard_map.145 = (bf16[624,384]{1,0:T(8,128)(2,1)S(1)}, bf16[416,384]{1,0:T(8,128)(2,1)S(1)}, bf16[312,384]{1,0:T(8,128)(2,1)S(1)}, bf16[312,384]{1,0:T(8,128)(2,1)S(1)}, bf16[208,384]{1,0:T(8,128)(2,1)S(1)}) custom-call(bf16[416,384]{1,0:T(8,128)(2,1)S(1)} %collective-permute-done.4.low, bf16[416,384]{1,0:T(8,128)(2,1)S(1)} %collective-permute-done.6.high, ...), custom_call_target="tpu_custom_call" | custom-call | flops 1656225792 | bytes 1916928 | tf_op jit(solution)/shard_map/pallas_call | solution.py:139
  43.1 2.8 %collective-permute-start.13 = (bf16[416,384]{1,0:T(8,128)(2,1)S(1)}, bf16[416,384]{1,0:T(8,128)(2,1)S(1)}, u32[]{:S(2)}, u32[]{:S(2)}) collective-permute-start(bf16[416,384]{1,0:T(8,128)(2,1)S(1)} %get-tuple-element.45), channel_id=1, source_target_pairs={{0,4},{1,5},{2,6},{3,7},{4,0},{5,1},{6,2},{7,3},{8,12},{9,13},{10,... | collective-permute-start | bytes 958472 | tf_op jit(solution)/shard_map/ppermute | solution.py:72
  45.9 1.5 %collective-permute-start.18 = (bf16[312,384]{1,0:T(8,128)(2,1)S(1)}, bf16[312,384]{1,0:T(8,128)(2,1)S(1)}, u32[]{:S(2)}, u32[]{:S(2)}) collective-permute-start(bf16[312,384]{1,0:T(8,128)(2,1)S(1)} %get-tuple-element.49), channel_id=1, source_target_pairs={{0,16},{1,2},{2,1},{3,19},{16,0},{17,18},{18,17},{19,3},{4,20},{5,... | collective-permute-start | bytes 718856 | tf_op jit(solution)/shard_map/ppermute | solution.py:48
  48.3 5.5 %collective-permute-done.13.low = bf16[416,384]{1,0:T(8,128)(2,1)S(1)} collective-permute-done((bf16[416,384]{1,0:T(8,128)(2,1)S(1)}, bf16[416,384]{1,0:T(8,128)(2,1)S(1)}, u32[]{:S(2)}, u32[]{:S(2)}) %collective-permute-start.13) | collective-permute-done | bytes 319520 | tf_op jit(solution)/shard_map/ppermute | solution.py:72
  54.4 4.4 %shard_map.146.partial = f32[624,1152]{1,0:T(8,128)S(1)} custom-call(bf16[624,384]{1,0:T(8,128)(2,1)S(1)} %get-tuple-element.48.refs_0_, bf16[312,384]{1,0:T(8,128)(2,1)S(1)} %collective-permute-done.18.refs_1_, bf16[312,384]{1,0:T(8,128)(2,1)S(1)} %collective-permute-done.19.refs_2_, bf16[3,1152,1152]{2,1,0:T(8,128)(2,1)S(1)} %get-tuple-element.46.refs_3_.packed), custom_call_target="tpu_custom_call" | custom-call | flops 3312451584 | bytes 1916928 | tf_op jit(solution)/shard_map/pallas_call | solution.py:139
  58.8 2.3 %shard_map.147.partial = f32[624,1152]{1,0:T(8,128)S(1)} custom-call(bf16[416,384]{1,0:T(8,128)(2,1)S(1)} %collective-permute-done.13.low, bf16[416,384]{1,0:T(8,128)(2,1)S(1)} %collective-permute-done.15.high, bf16[208,384]{1,0:T(8,128)(2,1)S(1)} %collective-permute-done.17.off, bf16[3,1152,1152]{2,1,0:T(8,128)(2,1)S(1)} %get-tuple-element.46.refs_3_.packed, ...), custom_call_target="tpu_custom_call" | custom-call | flops 1656225792 | bytes 1916928 | tf_op jit(solution)/shard_map/pallas_call | solution.py:139
  61.1 2.8 %shard_map.148 = (bf16[624,384]{1,0:T(8,128)(2,1)}, f32[384,384]{1,0:T(8,128)S(1)}, bf16[384,384]{1,0:T(8,128)(2,1)S(1)}) custom-call(bf16[416,384]{1,0:T(8,128)(2,1)S(1)} %collective-permute-done.14.low, bf16[416,384]{1,0:T(8,128)(2,1)S(1)} %collective-permute-done.16.high, bf16[3,1152,1152]{2,1,0:T(8,128)(2,1)S(1)} %get-tuple-element.46.refs_3_.packed, ...), custom_call_target="tpu_custom_call" | custom-call | flops 2208301056 | bytes 1916928 | tf_op jit(solution)/shard_map/pallas_call | solution.py:139
  64.0 1.6 %collective-permute-done.20 = bf16[384,384]{1,0:T(8,128)(2,1)S(1)} collective-permute-done((bf16[384,384]{1,0:T(8,128)(2,1)S(1)}, bf16[384,384]{1,0:T(8,128)(2,1)S(1)}, u32[]{:S(2)}, u32[]{:S(2)}) %collective-permute-start.20) | collective-permute-done | bytes 294944 | tf_op jit(solution)/shard_map/ppermute | solution.py:20
  65.6 1.3 %collective-permute-start.21 = (bf16[96,384]{1,0:T(8,128)(2,1)S(1)}, bf16[96,384]{1,0:T(8,128)(2,1)S(1)}, u32[]{:S(2)}, u32[]{:S(2)}) collective-permute-start(bf16[96,384]{1,0:T(8,128)(2,1)S(1)} %get-tuple-element.67), channel_id=1, source_target_pairs={{0,2},{1,3},{2,0},{3,1},{16,18},{17,19},{18,16},{19,17},{4,6},{5,7... | collective-permute-start | bytes 221192 | tf_op jit(solution)/shard_map/ppermute | solution.py:89
  67.5 1.7 %collective-permute-start.23 = (bf16[96,384]{1,0:T(8,128)(2,1)S(1)}, bf16[96,384]{1,0:T(8,128)(2,1)S(1)}, u32[]{:S(2)}, u32[]{:S(2)}) collective-permute-start(bf16[96,384]{1,0:T(8,128)(2,1)S(1)} %get-tuple-element.68), channel_id=1, source_target_pairs={{0,18},{1,19},{2,16},{3,17},{16,2},{17,3},{18,0},{19,1},{4,22},{5,... | collective-permute-start | bytes 221192 | tf_op jit(solution)/shard_map/ppermute | solution.py:89
  70.1 1.6 %collective-permute-done.22 = bf16[96,384]{1,0:T(8,128)(2,1)S(1)} collective-permute-done((bf16[96,384]{1,0:T(8,128)(2,1)S(1)}, bf16[96,384]{1,0:T(8,128)(2,1)S(1)}, u32[]{:S(2)}, u32[]{:S(2)}) %collective-permute-start.22) | collective-permute-done | bytes 73760 | tf_op jit(solution)/shard_map/ppermute | solution.py:89
  71.7 1.4 %collective-permute-done.23 = bf16[96,384]{1,0:T(8,128)(2,1)S(1)} collective-permute-done((bf16[96,384]{1,0:T(8,128)(2,1)S(1)}, bf16[96,384]{1,0:T(8,128)(2,1)S(1)}, u32[]{:S(2)}, u32[]{:S(2)}) %collective-permute-start.23) | collective-permute-done | bytes 73760 | tf_op jit(solution)/shard_map/ppermute | solution.py:89
  73.1 2.6 %collective-permute-start.24 = (bf16[96,384]{1,0:T(8,128)(2,1)S(1)}, bf16[96,384]{1,0:T(8,128)(2,1)S(1)}, u32[]{:S(2)}, u32[]{:S(2)}) collective-permute-start(bf16[96,384]{1,0:T(8,128)(2,1)S(1)} %add_convert_fusion.1), channel_id=1, source_target_pairs={{0,4},{4,0},{8,12},{12,8},{1,5},{5,1},{9,13},{13,9},{2,6},{6,2},{1... | collective-permute-start | bytes 221192 | tf_op jit(solution)/shard_map/ppermute | solution.py:20
  75.7 2.1 %collective-permute-start.25 = (bf16[96,384]{1,0:T(8,128)(2,1)S(1)}, bf16[96,384]{1,0:T(8,128)(2,1)S(1)}, u32[]{:S(2)}, u32[]{:S(2)}) collective-permute-start(bf16[96,384]{1,0:T(8,128)(2,1)S(1)} %add_convert_fusion.1), channel_id=1, source_target_pairs={{0,8},{4,12},{8,0},{12,4},{1,9},{5,13},{9,1},{13,5},{2,10},{6,14},... | collective-permute-start | bytes 221192 | tf_op jit(solution)/shard_map/ppermute | solution.py:20
  77.7 1.1 %collective-permute-start.26 = (bf16[96,384]{1,0:T(8,128)(2,1)S(1)}, bf16[96,384]{1,0:T(8,128)(2,1)S(1)}, u32[]{:S(2)}, u32[]{:S(2)}) collective-permute-start(bf16[96,384]{1,0:T(8,128)(2,1)S(1)} %add_convert_fusion.1), channel_id=1, source_target_pairs={{0,12},{4,8},{8,4},{12,0},{1,13},{5,9},{9,5},{13,1},{2,14},{6,10},... | collective-permute-start | bytes 221192 | tf_op jit(solution)/shard_map/ppermute | solution.py:20
  78.9 5.6 %collective-permute-done.25 = bf16[96,384]{1,0:T(8,128)(2,1)S(1)} collective-permute-done((bf16[96,384]{1,0:T(8,128)(2,1)S(1)}, bf16[96,384]{1,0:T(8,128)(2,1)S(1)}, u32[]{:S(2)}, u32[]{:S(2)}) %collective-permute-start.25) | collective-permute-done | bytes 73760 | tf_op jit(solution)/shard_map/ppermute | solution.py:20
  86.0 2.1 %collective-permute-start.29 = (bf16[96,384]{1,0:T(8,128)(2,1)S(1)}, bf16[96,384]{1,0:T(8,128)(2,1)S(1)}, u32[]{:S(2)}, u32[]{:S(2)}) collective-permute-start(bf16[96,384]{1,0:T(8,128)(2,1)S(1)} %get-tuple-element.62), channel_id=1, source_target_pairs={{0,18},{1,19},{2,16},{3,17},{16,2},{17,3},{18,0},{19,1},{4,22},{5,... | collective-permute-start | bytes 221192 | tf_op jit(solution)/shard_map/ppermute | solution.py:89
  90.0 1.2 %collective-permute-done.29 = bf16[96,384]{1,0:T(8,128)(2,1)S(1)} collective-permute-done((bf16[96,384]{1,0:T(8,128)(2,1)S(1)}, bf16[96,384]{1,0:T(8,128)(2,1)S(1)}, u32[]{:S(2)}, u32[]{:S(2)}) %collective-permute-start.29) | collective-permute-done | bytes 73760 | tf_op jit(solution)/shard_map/ppermute | solution.py:89
  91.3 1.6 %collective-permute-done.30 = bf16[384,384]{1,0:T(8,128)(2,1)S(1)} collective-permute-done((bf16[384,384]{1,0:T(8,128)(2,1)S(1)}, bf16[384,384]{1,0:T(8,128)(2,1)S(1)}, u32[]{:S(2)}, u32[]{:S(2)}) %collective-permute-start.30) | collective-permute-done | bytes 294944 | tf_op jit(solution)/shard_map/ppermute | solution.py:20
  92.9 1.1 %select_convert_fusion = (f32[384,384]{1,0:T(8,128)}, f32[384,384]{1,0:T(8,128)}) fusion(bf16[384,384]{1,0:T(8,128)(2,1)S(1)} %constant_dynamic-update-slice_fusion, bf16[384,384]{1,0:T(8,128)(2,1)S(1)} %collective-permute-done.30, pred[]{:T(512)S(6)} %eq.3), kind=kLoop, calls=%fused_computation.1 | loop fusion | flops 589824 | bytes 1769473 | tf_op jit(solution)/shard_map/convert_element_type | solution.py:122
  (53 shorter events, 8.4 us)
Async XLA Ops:
  2.0 10.6 %collective-permute-start = (bf16[416,384]{1,0:T(8,128)(2,1)S(1)}, bf16[416,384]{1,0:T(8,128)(2,1)S(1)}, u32[]{:S(2)}, u32[]{:S(2)}) collective-permute-start(bf16[416,384]{1,0:T(8,128)(2,1)S(1)} %get-tuple-element.32.refs_0_), channel_id=1, source_target_pairs={{0,2},{1,3},{2,0},{3,1},{4,6},{5,7},{6,4},{7,5},{8,10},{9,11},{10,... | collective-permute-start | bytes 958472 | tf_op jit(solution)/shard_map/ppermute | solution.py:20
  5.1 16.0 %collective-permute-start.1 = (bf16[416,384]{1,0:T(8,128)(2,1)S(1)}, bf16[416,384]{1,0:T(8,128)(2,1)S(1)}, u32[]{:S(2)}, u32[]{:S(2)}) collective-permute-start(bf16[416,384]{1,0:T(8,128)(2,1)S(1)} %get-tuple-element.32.refs_0_), channel_id=1, source_target_pairs={{0,1},{1,0},{2,3},{3,2},{4,5},{5,4},{6,7},{7,6},{8,9},{9,8},{10,11... | collective-permute-start | bytes 958472 | tf_op jit(solution)/shard_map/ppermute | solution.py:20
  12.6 8.5 %collective-permute-start.2 = (bf16[416,384]{1,0:T(8,128)(2,1)S(1)}, bf16[416,384]{1,0:T(8,128)(2,1)S(1)}, u32[]{:S(2)}, u32[]{:S(2)}) collective-permute-start(bf16[416,384]{1,0:T(8,128)(2,1)S(1)} %collective-permute-done.refs_1_), channel_id=1, source_target_pairs={{0,1},{1,0},{2,3},{3,2},{4,5},{5,4},{6,7},{7,6},{8,9},{9,8},{10,11... | collective-permute-start | bytes 958472 | tf_op jit(solution)/shard_map/ppermute | solution.py:20
  12.6 8.1 %collective-permute-start.8 = (bf16[208,384]{1,0:T(8,128)(2,1)S(1)}, bf16[208,384]{1,0:T(8,128)(2,1)S(1)}, u32[]{:S(2)}, u32[]{:S(2)}) collective-permute-start(bf16[208,384]{1,0:T(8,128)(2,1)S(1)} %get-tuple-element.40.refs_0_), channel_id=1, source_target_pairs={{0,2},{1,3},{2,0},{3,1},{4,6},{5,7},{6,4},{7,5},{8,10},{9,11},{10,... | collective-permute-start | bytes 479240 | tf_op jit(solution)/shard_map/ppermute | solution.py:20
  14.3 12.1 %collective-permute-start.9 = (bf16[208,384]{1,0:T(8,128)(2,1)S(1)}, bf16[208,384]{1,0:T(8,128)(2,1)S(1)}, u32[]{:S(2)}, u32[]{:S(2)}) collective-permute-start(bf16[208,384]{1,0:T(8,128)(2,1)S(1)} %get-tuple-element.40.refs_0_), channel_id=1, source_target_pairs={{0,1},{1,0},{2,3},{3,2},{4,5},{5,4},{6,7},{7,6},{8,9},{9,8},{10,11... | collective-permute-start | bytes 479240 | tf_op jit(solution)/shard_map/ppermute | solution.py:20
  14.6 6.5 %copy-start.1 = (f32[384]{0:T(512)S(1)}, f32[384]{0:T(512)}, u32[]{:S(2)}) copy-start(f32[384]{0:T(512)} %refs_8_.3) | copy-start | bytes 4612
  20.7 5.7 %collective-permute-start.10 = (bf16[208,384]{1,0:T(8,128)(2,1)S(1)}, bf16[208,384]{1,0:T(8,128)(2,1)S(1)}, u32[]{:S(2)}, u32[]{:S(2)}) collective-permute-start(bf16[208,384]{1,0:T(8,128)(2,1)S(1)} %collective-permute-done.8.refs_1_), channel_id=1, source_target_pairs={{0,1},{1,0},{2,3},{3,2},{4,5},{5,4},{6,7},{7,6},{8,9},{9,8},{10,11... | collective-permute-start | bytes 479240 | tf_op jit(solution)/shard_map/ppermute | solution.py:20
  24.8 9.7 %collective-permute-start.3 = (bf16[416,384]{1,0:T(8,128)(2,1)S(1)}, bf16[416,384]{1,0:T(8,128)(2,1)S(1)}, u32[]{:S(2)}, u32[]{:S(2)}) collective-permute-start(bf16[416,384]{1,0:T(8,128)(2,1)S(1)} %get-tuple-element.37.refs_1_), channel_id=1, source_target_pairs={{0,4},{1,5},{2,6},{3,7},{4,0},{5,1},{6,2},{7,3},{8,12},{9,13},{10,... | collective-permute-start | bytes 958472 | tf_op jit(solution)/shard_map/ppermute | solution.py:72
  26.4 8.3 %collective-permute-start.5 = (bf16[416,384]{1,0:T(8,128)(2,1)S(1)}, bf16[416,384]{1,0:T(8,128)(2,1)S(1)}, u32[]{:S(2)}, u32[]{:S(2)}) collective-permute-start(bf16[416,384]{1,0:T(8,128)(2,1)S(1)} %get-tuple-element.37.refs_1_), channel_id=1, source_target_pairs={{0,1},{1,0},{2,3},{3,2},{4,8},{5,9},{6,10},{7,11},{8,4},{9,5},{10,... | collective-permute-start | bytes 958472 | tf_op jit(solution)/shard_map/ppermute | solution.py:72
  28.4 6.6 %collective-permute-start.11 = (bf16[312,384]{1,0:T(8,128)(2,1)S(1)}, bf16[312,384]{1,0:T(8,128)(2,1)S(1)}, u32[]{:S(2)}, u32[]{:S(2)}) collective-permute-start(bf16[312,384]{1,0:T(8,128)(2,1)S(1)} %get-tuple-element.43), channel_id=1, source_target_pairs={{0,16},{1,2},{2,1},{3,19},{16,0},{17,18},{18,17},{19,3},{4,20},{5,... | collective-permute-start | bytes 718856 | tf_op jit(solution)/shard_map/ppermute | solution.py:48
  30.0 5.1 %collective-permute-start.12 = (bf16[312,384]{1,0:T(8,128)(2,1)S(1)}, bf16[312,384]{1,0:T(8,128)(2,1)S(1)}, u32[]{:S(2)}, u32[]{:S(2)}) collective-permute-start(bf16[312,384]{1,0:T(8,128)(2,1)S(1)} %get-tuple-element.44), channel_id=1, source_target_pairs={{0,1},{1,0},{2,3},{3,2},{4,5},{5,4},{6,7},{7,6},{8,9},{9,8},{10,11... | collective-permute-start | bytes 718856 | tf_op jit(solution)/shard_map/ppermute | solution.py:20
  30.0 9.5 %collective-permute-start.7 = (bf16[208,384]{1,0:T(8,128)(2,1)S(1)}, bf16[208,384]{1,0:T(8,128)(2,1)S(1)}, u32[]{:S(2)}, u32[]{:S(2)}) collective-permute-start(bf16[208,384]{1,0:T(8,128)(2,1)S(1)} %get-tuple-element.39.refs_10_), channel_id=1, source_target_pairs={{1,6},{2,5},{5,10},{6,9},{9,14},{10,13},{17,22},{18,21},{21,26},{2... | collective-permute-start | bytes 479240 | tf_op jit(solution)/shard_map/ppermute | solution.py:58
  34.5 7.2 %collective-permute-start.4 = (bf16[416,384]{1,0:T(8,128)(2,1)S(1)}, bf16[416,384]{1,0:T(8,128)(2,1)S(1)}, u32[]{:S(2)}, u32[]{:S(2)}) collective-permute-start(bf16[416,384]{1,0:T(8,128)(2,1)S(1)} %collective-permute-done.3.low), channel_id=1, source_target_pairs={{0,1},{1,0},{2,3},{3,2},{4,5},{5,4},{6,7},{7,6},{8,9},{9,8},{10,11... | collective-permute-start | bytes 958472 | tf_op jit(solution)/shard_map/ppermute | solution.py:20
  34.7 7.0 %collective-permute-start.6 = (bf16[416,384]{1,0:T(8,128)(2,1)S(1)}, bf16[416,384]{1,0:T(8,128)(2,1)S(1)}, u32[]{:S(2)}, u32[]{:S(2)}) collective-permute-start(bf16[416,384]{1,0:T(8,128)(2,1)S(1)} %collective-permute-done.5.high), channel_id=1, source_target_pairs={{0,1},{1,0},{2,3},{3,2},{4,5},{5,4},{6,7},{7,6},{8,9},{9,8},{10,11... | collective-permute-start | bytes 958472 | tf_op jit(solution)/shard_map/ppermute | solution.py:20
  43.1 10.7 %collective-permute-start.13 = (bf16[416,384]{1,0:T(8,128)(2,1)S(1)}, bf16[416,384]{1,0:T(8,128)(2,1)S(1)}, u32[]{:S(2)}, u32[]{:S(2)}) collective-permute-start(bf16[416,384]{1,0:T(8,128)(2,1)S(1)} %get-tuple-element.45), channel_id=1, source_target_pairs={{0,4},{1,5},{2,6},{3,7},{4,0},{5,1},{6,2},{7,3},{8,12},{9,13},{10,... | collective-permute-start | bytes 958472 | tf_op jit(solution)/shard_map/ppermute | solution.py:72
  45.9 7.9 %collective-permute-start.15 = (bf16[416,384]{1,0:T(8,128)(2,1)S(1)}, bf16[416,384]{1,0:T(8,128)(2,1)S(1)}, u32[]{:S(2)}, u32[]{:S(2)}) collective-permute-start(bf16[416,384]{1,0:T(8,128)(2,1)S(1)} %get-tuple-element.45), channel_id=1, source_target_pairs={{0,1},{1,0},{2,3},{3,2},{4,8},{5,9},{6,10},{7,11},{8,4},{9,5},{10,... | collective-permute-start | bytes 958472 | tf_op jit(solution)/shard_map/ppermute | solution.py:72
  45.9 8.4 %collective-permute-start.18 = (bf16[312,384]{1,0:T(8,128)(2,1)S(1)}, bf16[312,384]{1,0:T(8,128)(2,1)S(1)}, u32[]{:S(2)}, u32[]{:S(2)}) collective-permute-start(bf16[312,384]{1,0:T(8,128)(2,1)S(1)} %get-tuple-element.49), channel_id=1, source_target_pairs={{0,16},{1,2},{2,1},{3,19},{16,0},{17,18},{18,17},{19,3},{4,20},{5,... | collective-permute-start | bytes 718856 | tf_op jit(solution)/shard_map/ppermute | solution.py:48
  47.4 6.9 %collective-permute-start.19 = (bf16[312,384]{1,0:T(8,128)(2,1)S(1)}, bf16[312,384]{1,0:T(8,128)(2,1)S(1)}, u32[]{:S(2)}, u32[]{:S(2)}) collective-permute-start(bf16[312,384]{1,0:T(8,128)(2,1)S(1)} %get-tuple-element.50), channel_id=1, source_target_pairs={{0,1},{1,0},{2,3},{3,2},{4,5},{5,4},{6,7},{7,6},{8,9},{9,8},{10,11... | collective-permute-start | bytes 718856 | tf_op jit(solution)/shard_map/ppermute | solution.py:20
  47.4 11.4 %collective-permute-start.17 = (bf16[208,384]{1,0:T(8,128)(2,1)S(1)}, bf16[208,384]{1,0:T(8,128)(2,1)S(1)}, u32[]{:S(2)}, u32[]{:S(2)}) collective-permute-start(bf16[208,384]{1,0:T(8,128)(2,1)S(1)} %get-tuple-element.47), channel_id=1, source_target_pairs={{1,6},{2,5},{5,10},{6,9},{9,14},{10,13},{17,22},{18,21},{21,26},{2... | collective-permute-start | bytes 479240 | tf_op jit(solution)/shard_map/ppermute | solution.py:58
  53.9 7.3 %collective-permute-start.14 = (bf16[416,384]{1,0:T(8,128)(2,1)S(1)}, bf16[416,384]{1,0:T(8,128)(2,1)S(1)}, u32[]{:S(2)}, u32[]{:S(2)}) collective-permute-start(bf16[416,384]{1,0:T(8,128)(2,1)S(1)} %collective-permute-done.13.low), channel_id=1, source_target_pairs={{0,1},{1,0},{2,3},{3,2},{4,5},{5,4},{6,7},{7,6},{8,9},{9,8},{10,11... | collective-permute-start | bytes 958472 | tf_op jit(solution)/shard_map/ppermute | solution.py:20
  53.9 7.3 %collective-permute-start.16 = (bf16[416,384]{1,0:T(8,128)(2,1)S(1)}, bf16[416,384]{1,0:T(8,128)(2,1)S(1)}, u32[]{:S(2)}, u32[]{:S(2)}) collective-permute-start(bf16[416,384]{1,0:T(8,128)(2,1)S(1)} %collective-permute-done.15.high), channel_id=1, source_target_pairs={{0,1},{1,0},{2,3},{3,2},{4,5},{5,4},{6,7},{7,6},{8,9},{9,8},{10,11... | collective-permute-start | bytes 958472 | tf_op jit(solution)/shard_map/ppermute | solution.py:20
  63.9 1.6 %collective-permute-start.20 = (bf16[384,384]{1,0:T(8,128)(2,1)S(1)}, bf16[384,384]{1,0:T(8,128)(2,1)S(1)}, u32[]{:S(2)}, u32[]{:S(2)}) collective-permute-start(bf16[384,384]{1,0:T(8,128)(2,1)S(1)} %get-tuple-element.60), channel_id=1, source_target_pairs={{0,1},{1,0},{2,3},{3,2},{4,5},{5,4},{6,7},{7,6},{8,9},{9,8},{10,11... | collective-permute-start | bytes 884744 | tf_op jit(solution)/shard_map/ppermute | solution.py:20
  65.6 4.4 %collective-permute-start.21 = (bf16[96,384]{1,0:T(8,128)(2,1)S(1)}, bf16[96,384]{1,0:T(8,128)(2,1)S(1)}, u32[]{:S(2)}, u32[]{:S(2)}) collective-permute-start(bf16[96,384]{1,0:T(8,128)(2,1)S(1)} %get-tuple-element.67), channel_id=1, source_target_pairs={{0,2},{1,3},{2,0},{3,1},{16,18},{17,19},{18,16},{19,17},{4,6},{5,7... | collective-permute-start | bytes 221192 | tf_op jit(solution)/shard_map/ppermute | solution.py:89
  66.9 4.8 %collective-permute-start.22 = (bf16[96,384]{1,0:T(8,128)(2,1)S(1)}, bf16[96,384]{1,0:T(8,128)(2,1)S(1)}, u32[]{:S(2)}, u32[]{:S(2)}) collective-permute-start(bf16[96,384]{1,0:T(8,128)(2,1)S(1)} %get-tuple-element.69), channel_id=1, source_target_pairs={{0,16},{1,17},{2,18},{3,19},{16,0},{17,1},{18,2},{19,3},{4,20},{5,... | collective-permute-start | bytes 221192 | tf_op jit(solution)/shard_map/ppermute | solution.py:89
  67.5 5.6 %collective-permute-start.23 = (bf16[96,384]{1,0:T(8,128)(2,1)S(1)}, bf16[96,384]{1,0:T(8,128)(2,1)S(1)}, u32[]{:S(2)}, u32[]{:S(2)}) collective-permute-start(bf16[96,384]{1,0:T(8,128)(2,1)S(1)} %get-tuple-element.68), channel_id=1, source_target_pairs={{0,18},{1,19},{2,16},{3,17},{16,2},{17,3},{18,0},{19,1},{4,22},{5,... | collective-permute-start | bytes 221192 | tf_op jit(solution)/shard_map/ppermute | solution.py:89
  73.1 5.8 %collective-permute-start.24 = (bf16[96,384]{1,0:T(8,128)(2,1)S(1)}, bf16[96,384]{1,0:T(8,128)(2,1)S(1)}, u32[]{:S(2)}, u32[]{:S(2)}) collective-permute-start(bf16[96,384]{1,0:T(8,128)(2,1)S(1)} %add_convert_fusion.1), channel_id=1, source_target_pairs={{0,4},{4,0},{8,12},{12,8},{1,5},{5,1},{9,13},{13,9},{2,6},{6,2},{1... | collective-permute-start | bytes 221192 | tf_op jit(solution)/shard_map/ppermute | solution.py:20
  75.7 8.8 %collective-permute-start.25 = (bf16[96,384]{1,0:T(8,128)(2,1)S(1)}, bf16[96,384]{1,0:T(8,128)(2,1)S(1)}, u32[]{:S(2)}, u32[]{:S(2)}) collective-permute-start(bf16[96,384]{1,0:T(8,128)(2,1)S(1)} %add_convert_fusion.1), channel_id=1, source_target_pairs={{0,8},{4,12},{8,0},{12,4},{1,9},{5,13},{9,1},{13,5},{2,10},{6,14},... | collective-permute-start | bytes 221192 | tf_op jit(solution)/shard_map/ppermute | solution.py:20
  77.7 6.7 %collective-permute-start.26 = (bf16[96,384]{1,0:T(8,128)(2,1)S(1)}, bf16[96,384]{1,0:T(8,128)(2,1)S(1)}, u32[]{:S(2)}, u32[]{:S(2)}) collective-permute-start(bf16[96,384]{1,0:T(8,128)(2,1)S(1)} %add_convert_fusion.1), channel_id=1, source_target_pairs={{0,12},{4,8},{8,4},{12,0},{1,13},{5,9},{9,5},{13,1},{2,14},{6,10},... | collective-permute-start | bytes 221192 | tf_op jit(solution)/shard_map/ppermute | solution.py:20
  84.6 4.4 %collective-permute-start.27 = (bf16[96,384]{1,0:T(8,128)(2,1)S(1)}, bf16[96,384]{1,0:T(8,128)(2,1)S(1)}, u32[]{:S(2)}, u32[]{:S(2)}) collective-permute-start(bf16[96,384]{1,0:T(8,128)(2,1)S(1)} %get-tuple-element.62), channel_id=1, source_target_pairs={{0,2},{1,3},{2,0},{3,1},{16,18},{17,19},{18,16},{19,17},{4,6},{5,7... | collective-permute-start | bytes 221192 | tf_op jit(solution)/shard_map/ppermute | solution.py:89
  85.6 4.4 %collective-permute-start.28 = (bf16[96,384]{1,0:T(8,128)(2,1)S(1)}, bf16[96,384]{1,0:T(8,128)(2,1)S(1)}, u32[]{:S(2)}, u32[]{:S(2)}) collective-permute-start(bf16[96,384]{1,0:T(8,128)(2,1)S(1)} %get-tuple-element.62), channel_id=1, source_target_pairs={{0,16},{1,17},{2,18},{3,19},{16,0},{17,1},{18,2},{19,3},{4,20},{5,... | collective-permute-start | bytes 221192 | tf_op jit(solution)/shard_map/ppermute | solution.py:89
  86.0 5.3 %collective-permute-start.29 = (bf16[96,384]{1,0:T(8,128)(2,1)S(1)}, bf16[96,384]{1,0:T(8,128)(2,1)S(1)}, u32[]{:S(2)}, u32[]{:S(2)}) collective-permute-start(bf16[96,384]{1,0:T(8,128)(2,1)S(1)} %get-tuple-element.62), channel_id=1, source_target_pairs={{0,18},{1,19},{2,16},{3,17},{16,2},{17,3},{18,0},{19,1},{4,22},{5,... | collective-permute-start | bytes 221192 | tf_op jit(solution)/shard_map/ppermute | solution.py:89
  91.3 1.6 %collective-permute-start.30 = (bf16[384,384]{1,0:T(8,128)(2,1)S(1)}, bf16[384,384]{1,0:T(8,128)(2,1)S(1)}, u32[]{:S(2)}, u32[]{:S(2)}) collective-permute-start(bf16[384,384]{1,0:T(8,128)(2,1)S(1)} %constant_dynamic-update-slice_fusion), channel_id=1, source_target_pairs={{0,1},{1,0},{2,3},{3,2},{4,5},{5,4},{6,7},{7,6},{8,9},{9,8},{10,11... | collective-permute-start | bytes 884744 | tf_op jit(solution)/shard_map/ppermute | solution.py:20
  (1 other events, 2.4 us)

commit v2 on v1

--- a/solution.py
+++ b/solution.py
@@ -20,13 +20,13 @@
     return lax.ppermute(value, axis, [(i, i ^ mask) for i in range(count)])
 
 
-def gather_blocks(block):
+def gather_chips(block):
     mask = lax.axis_size("space") // 2
-    blocks = [block, xor_permute(block, "space", mask)]
+    blocks = [block]
     while mask > 1:
+        blocks = blocks + [xor_permute(b, "space", mask) for b in blocks]
         mask //= 2
-        blocks = blocks + [xor_permute(b, "space", mask) for b in blocks]
-    return blocks
+    return blocks[1:]
 
 
 def across_pairs():
@@ -46,16 +46,6 @@
             if other[0] < clips:
                 pairs.append((clip * count + place, other[0] * count + other[1]))
     return lax.ppermute(value, ("dp", "space"), pairs)
-
-
-def across_next_frames(value):
-    count = lax.axis_size("space")
-    pairs = [
-        (block * count + source, (block + 1) * count + target)
-        for block in range(lax.axis_size("tm") - 1)
-        for source, target in across_pairs()
-    ]
-    return lax.ppermute(value, ("tm", "space"), pairs)
 
 
 def frame_pairings(value):
@@ -70,6 +60,26 @@
                 target = other * count + place if inside else block * count + (place ^ 1)
                 pairs.append((block * count + place, target))
         results.append(lax.ppermute(value, ("tm", "space"), pairs))
+    return results
+
+
+def corner_pairings(value):
+    clips, blocks, count = (lax.axis_size(axis) for axis in ("dp", "tm", "space"))
+    rows = dict(across_pairs())
+    results = []
+    for first in range(2):
+        pairs = []
+        for clip in range(clips):
+            for block in range(blocks):
+                other = ((block - first) ^ 1) + first
+                for place in range(count):
+                    if place in rows and 0 <= other < blocks:
+                        target = (clip * blocks + other) * count + rows[place]
+                    else:
+                        target = ((clip ^ 1) * blocks + block) * count + place
+                    if target < clips * blocks * count:
+                        pairs.append(((clip * blocks + block) * count + place, target))
+        results.append(lax.ppermute(value, ("dp", "tm", "space"), pairs))
     return results
 
 
@@ -177,93 +187,98 @@
     return jnp.where(odd, first, last), jnp.where(odd, last, first)
 
 
-def norm_body(late, latent_hbm, gain_hbm, latent, normed_late, normed_early, gain, sems):
+def norm_body(latent_hbm, gain_hbm, latent, normed, *refs):
     frame_count, per_frame = latent_hbm.shape[:2]
-    pltpu.make_async_copy(gain_hbm, gain, sems.at[frame_count]).start()
+    frames, gain, sems = refs[:frame_count], refs[-2], refs[-1]
+    gain_copy = pltpu.make_async_copy(gain_hbm, gain, sems.at[frame_count])
+    gain_copy.start()
     copies = {}
     for frame in range(frame_count - 1, -1, -1):
         here = pl.ds(frame * per_frame, per_frame)
         copies[frame] = pltpu.make_async_copy(latent_hbm.at[frame], latent.at[here], sems.at[frame])
         copies[frame].start()
-    pltpu.make_async_copy(gain_hbm, gain, sems.at[frame_count]).wait()
+    gain_copy.wait()
     for frame in range(frame_count - 1, -1, -1):
+        here = pl.ds(frame * per_frame, per_frame)
         copies[frame].wait()
-        wide = latent[pl.ds(frame * per_frame, per_frame)].astype(F32)
-        normed = root_norm(wide, gain[...].reshape(1, -1)).astype(BF16)
-        at = frame - (frame_count - late)
-        target = normed_late if at >= 0 else normed_early
-        target[pl.ds((at if at >= 0 else frame) * per_frame, per_frame)] = normed
+        wide = latent[here].astype(F32)
+        result = root_norm(wide, gain[...].reshape(1, -1)).astype(BF16)
+        normed[here] = result
+        frames[frame][...] = result
 
 
 def prepare_body(
-    latent, query_hbm, key_hbm, value_hbm, out_hbm, in_hbm, back_hbm, first_hbm, second_hbm,
-    w_query, w_both, w_out, s_out, first, second, slope, hidden_t, latent_t, predicted,
-    s_in, sems,
+    latent, normed, partner, query_hbm, key_hbm, value_hbm, out_hbm, in_hbm, back_hbm, first_hbm, second_hbm,
+    w_both, w_out, s_out, first, second, slope, hidden_t, latent_t, predicted,
+    queries, own_both, partner_both, w_query, s_in, sems,
 ):
     channels = latent.shape[1]
-    student = [
+    early = [
+        pltpu.make_async_copy(query_hbm, w_query, sems.at[2]),
+        pltpu.make_async_copy(key_hbm, w_both.at[:, pl.ds(0, channels)], sems.at[3]),
+        pltpu.make_async_copy(value_hbm, w_both.at[:, pl.ds(channels, channels)], sems.at[4]),
         pltpu.make_async_copy(in_hbm, s_in, sems.at[0]),
         pltpu.make_async_copy(back_hbm, s_out, sems.at[1]),
     ]
-    rest = [
-        pltpu.make_async_copy(query_hbm, w_query, sems.at[2]),
-        pltpu.make_async_copy(key_hbm, w_both.at[:, pl.ds(0, channels)], sems.at[3]),
-        pltpu.make_async_copy(value_hbm, w_both.at[:, pl.ds(channels, channels)], sems.at[4]),
-        pltpu.make_async_copy(out_hbm, w_out, sems.at[5]),
-    ]
+    rest = [pltpu.make_async_copy(out_hbm, w_out, sems.at[5])]
     for at, (taps, packed) in enumerate(((first_hbm, first), (second_hbm, second))):
         for t in range(3):
             for r in range(3):
                 for c in range(3):
-                    block = packed.at[t, pl.ds(r * channels, channels), pl.ds(c * channels, channels)]
+                    row = (3 * t + r) * channels
+                    block = packed.at[pl.ds(row, channels), pl.ds(c * channels, channels)]
                     rest.append(
                         pltpu.make_async_copy(taps.at[t, r, c], block, sems.at[6 + 3 * at + t])
                     )
-    for copy in student + rest:
+    for copy in early + rest:
         copy.start()
     tokens = latent[...]
     latent_t[...] = tokens.T
-    student[0].wait()
+    early[0].wait()
+    queries[...] = dot(normed[...], w_query[...]).astype(BF16)
+    early[1].wait()
+    early[2].wait()
+    own_both[...] = dot(normed[...], w_both[...]).astype(BF16)
+    partner_both[...] = dot(partner[...], w_both[...]).astype(BF16)
+    early[3].wait()
     before = dot(tokens, s_in[...])
     hidden = silu(before).astype(BF16)
     logistic = jax.nn.sigmoid(before)
     slope[...] = logistic * (1.0 + before * (1.0 - logistic))
     hidden_t[...] = hidden.T
-    student[1].wait()
+    early[4].wait()
     predicted[...] = tokens.astype(F32) + dot(hidden, s_out[...])
     for copy in rest:
         copy.wait()
 
 
-def attend_body(blocks, start, count, later, columns, *refs):
-    parts = refs[:blocks]
-    latent, w_query, w_both, w_out, gain = refs[blocks : blocks + 5]
-    act, mid, on, off = refs[-4:]
-    channels = w_query.shape[0]
+def attend_body(frame, remote, columns, kept, *refs):
+    blocks, refs = refs[:remote], refs[remote:]
+    latent, queries, own_both, partner_both, w_both, w_out, gain = refs[:7]
+    others, (act, mid, on, off) = refs[7 : 7 + kept], refs[7 + kept :]
+    channels = w_out.shape[0]
+    per_frame = mid.shape[0]
     odd = is_odd()
-    per_frame = parts[0].shape[0] // count
-    if later:
-        for ends, others in zip((on, off), refs[blocks + 5 : -4], strict=True):
-            ends[pl.ds(count * columns, others.shape[0])] = others[...]
-    for frame in range(count - 1, -1, -1):
-        here = pl.ds(frame * per_frame, per_frame)
-        rows = jnp.concatenate([part[here] for part in parts], axis=0)
-        queries = dot(parts[0][here], w_query[...]).astype(BF16)
-        both = dot(rows, w_both[...]).astype(BF16)
-        keys, values = both[:, :channels], both[:, channels:]
-        scores = lax.dot_general(
-            queries, keys, (((1,), (1,)), ((), ())), preferred_element_type=F32
-        ) * channels ** (-0.5)
-        expos = jnp.exp(scores - jnp.max(scores, axis=-1, keepdims=True))
-        totals = jnp.sum(expos, axis=-1, keepdims=True)
-        mixed = (dot(expos.astype(BF16), values) / totals).astype(BF16)
-        own = latent[pl.ds((start + frame) * per_frame, per_frame)]
-        middle = (own.astype(F32) + dot(mixed, w_out[...])).astype(BF16)
-        mid[here] = middle
-        active = silu(root_norm(middle.astype(F32), gain[...].reshape(1, -1))).astype(BF16)
-        act[here] = active
-        edge = pl.ds(frame * columns, columns)
-        on[edge], off[edge] = edge_rows(active, columns, odd)
+    for target, other in zip((on, off, act), others):
+        rows = other.shape[0]
+        target[pl.ds(target.shape[0] - rows, rows)] = other[...]
+    here = pl.ds(frame * per_frame, per_frame)
+    far = dot(jnp.concatenate([block[...] for block in blocks], axis=0), w_both[...]).astype(BF16)
+    parts = [own_both[here], partner_both[here], far]
+    keys = jnp.concatenate([part[:, :channels] for part in parts], axis=0)
+    values = jnp.concatenate([part[:, channels:] for part in parts], axis=0)
+    scores = lax.dot_general(
+        queries[here], keys, (((1,), (1,)), ((), ())), preferred_element_type=F32
+    ) * channels ** (-0.5)
+    expos = jnp.exp(scores - jnp.max(scores, axis=-1, keepdims=True))
+    totals = jnp.sum(expos, axis=-1, keepdims=True)
+    mixed = (dot(expos.astype(BF16), values) / totals).astype(BF16)
+    middle = (latent[here].astype(F32) + dot(mixed, w_out[...])).astype(BF16)
+    mid[...] = middle
+    active = silu(root_norm(middle.astype(F32), gain[...].reshape(1, -1))).astype(BF16)
+    act[pl.ds(0, per_frame)] = active
+    edge = pl.ds(0, columns)
+    on[edge], off[edge] = edge_rows(active, columns, odd)
 
 
 def stack_rows(columns, odd, own, on, off, stacked, at):
@@ -278,12 +293,14 @@
 
 
 def taps_sum(sources, frame, stacked, packed, per_frame, total):
-    for at, source in enumerate(sources):
-        tap = source - frame
-        if 0 <= tap < 3:
-            term = dot(stacked[pl.ds(at * per_frame, per_frame)], packed[tap])
-            total = term if total is None else total + term
-    return total
+    at = [i for i, source in enumerate(sources) if 0 <= source - frame < 3]
+    if not at:
+        return total
+    rows = [stacked[pl.ds(i * per_frame, per_frame)] for i in at]
+    depth = stacked.shape[1]
+    taps = packed[pl.ds((sources[at[0]] - frame) * depth, len(at) * depth)]
+    term = dot(jnp.concatenate(rows, axis=1), taps)
+    return term if total is None else total + term
 
 
 def shift_columns(total, columns):
@@ -319,12 +336,13 @@
         partial[pl.ds(frame * per_frame, per_frame)] = total
 
 
-def earlier_body(columns, low, high, off, packed, partial, total, stacked):
+def earlier_body(columns, low, high, off_low, off_high, packed, partial, total, stacked):
     odd = is_odd()
     per_frame = stacked.shape[0] // 2
     for frame in range(2):
         tail = choose_frames((low, high), pl.ds(frame * per_frame, per_frame))
-        edge = off[pl.ds(frame * columns, columns)]
+        edge = choose_frames((off_low, off_high), pl.ds(frame * columns, columns))
+        edge = jnp.where(has_across(), edge, jnp.zeros_like(edge))
         stack_rows(columns, odd, tail, jnp.zeros_like(edge), edge, stacked, frame)
     for frame in range(partial.shape[0] // per_frame):
         here = pl.ds(frame * per_frame, per_frame)
@@ -334,7 +352,7 @@
 def partner_terms(columns, odd, pair, packed):
     per_frame = pair[0].shape[0] // 2
     channels = pair[0].shape[1]
-    tap_row = pl.ds(pl.multiple_of(jnp.where(odd, 0, 2 * channels), channels), channels)
+    row = jnp.where(odd, 0, 2 * channels)
     edges = []
     for source in range(2):
         rows = choose_frames(pair, pl.ds(source * per_frame, per_frame))
@@ -343,7 +361,8 @@
     for frame in range(2):
         term = None
         for source in range(frame, 2):
-            part = dot(edges[source], packed[source - frame, tap_row])
+            start = pl.multiple_of(3 * (source - frame) * channels + row, channels)
+            part = dot(edges[source], packed[pl.ds(start, channels)])
             term = part if term is None else term + part
         zeros = jnp.zeros_like(term)
         pieces = [jnp.where(odd, term, zeros), jnp.where(odd, zeros, term)]
@@ -377,10 +396,9 @@
             off_late[pl.ds(at * columns, columns)] = far
 
 
-def last_body(
-    columns, token_total, low, high, packed, partial, mid_early, mid_late,
-    slope, hidden_t, latent_t, predicted, s_out, teacher, mine, yours, signals,
-):
+def last_body(columns, token_total, low, high, packed, partial, *refs):
+    slope, hidden_t, latent_t, predicted, s_out, teacher, mine, yours, signals = refs[-9:]
+    mids = refs[:-9]
     odd = is_odd()
     terms = partner_terms(columns, odd, (low, high), packed)
     per_frame = low.shape[0] // 2
@@ -391,9 +409,7 @@
         if frame < 2:
             total = total + terms[frame]
         total = shift_columns(total, columns)
-        at = frame - (frame_count - 2)
-        mid = mid_late[pl.ds(at * per_frame, per_frame)] if at >= 0 else mid_early[here]
-        taught = (mid.astype(F32) + total).astype(BF16)
+        taught = (mids[frame][...].astype(F32) + total).astype(BF16)
         teacher[here] = taught
         error = predicted[here] - taught.astype(F32)
         signals[here] = (
@@ -438,53 +454,64 @@
     def edges_of(count):
         return shape(count * columns, channels, BF16)
 
-    latent_rows, normed_late, normed_early = call(
-        functools.partial(norm_body, 2),
-        [rows_of(frame_count), rows_of(2), rows_of(early)], [HBM] * 2, [VMEM] * 3,
+    latent_rows, normed, *singles = call(
+        norm_body,
+        [rows_of(frame_count), rows_of(frame_count)] + [rows_of(1)] * frame_count,
+        [HBM] * 2, [VMEM] * (2 + frame_count),
         [pltpu.VMEM((channels,), F32), pltpu.SemaphoreType.DMA((frame_count + 1,))],
         0, 4 * tokens * channels, frames, attn_gain,
     )
-    blocks_late = gather_blocks(normed_late)
-    blocks_early = gather_blocks(normed_early)
-
-    packed_shape = jax.ShapeDtypeStruct((3, 3 * channels, 3 * channels), BF16)
+    order = list(range(frame_count - 1, -1, -1))
+    gathered = {frame: gather_chips(singles[frame]) for frame in order}
+
+    packed_shape = shape(9 * channels, 3 * channels, BF16)
     wide = shape(tokens, channels, F32)
     turned = shape(channels, tokens, BF16)
+    both = shape(tokens, 2 * channels, BF16)
     weights = (w_query, w_key, w_value, w_out, student_in, student_out, conv_first, conv_second)
     (
-        w_query, w_both, w_out, student_out, packed_first, packed_second,
-        slope, hidden_t, latent_t, predicted,
+        w_both, w_out, student_out, packed_first, packed_second,
+        slope, hidden_t, latent_t, predicted, queries, own_both, partner_both,
     ) = call(
         prepare_body,
-        [square, shape(channels, 2 * channels, BF16), square, square, packed_shape, packed_shape,
-         wide, turned, turned, wide],
-        [VMEM] + [HBM] * len(weights), [VMEM] * 10,
-        [pltpu.VMEM((channels, channels), BF16), pltpu.SemaphoreType.DMA((12,))],
-        2 * tokens * unit, 60 * channels * channels * 2, latent_rows, *weights,
-    )
-
-    def attend(blocks, start, count, *others):
-        args = [*blocks, latent_rows, w_query, w_both, w_out, conv_gain_first, *others]
-        ends = edges_of(count + 2 if others else count)
-        return call(
-            functools.partial(attend_body, len(blocks), start, count, bool(others), columns),
-            [rows_of(count), rows_of(count), ends, ends],
+        [shape(channels, 2 * channels, BF16), square, square, packed_shape, packed_shape,
+         wide, turned, turned, wide, rows_of(frame_count), both, both],
+        [VMEM] * 3 + [HBM] * len(weights), [VMEM] * 12,
+        [pltpu.VMEM((channels, channels), BF16)] * 2 + [pltpu.SemaphoreType.DMA((12,))],
+        7 * tokens * unit, 60 * channels * channels * 2,
+        latent_rows, normed, xor_permute(normed, "space", 1), *weights,
+    )
+
+    acts, mids, others = {}, {}, ()
+    for turn, frame in enumerate(order):
+        chips = gathered[frame]
+        blocks = [*chips, *(xor_permute(block, "space", 1) for block in chips)]
+        args = [
+            *blocks, latent_rows, queries, own_both, partner_both, w_both, w_out,
+            conv_gain_first, *others,
+        ]
+        ends = edges_of(turn + 1)
+        acts[frame], mids[frame], on, off = call(
+            functools.partial(attend_body, frame, len(blocks), columns, len(others)),
+            [rows_of(2 if turn == 1 else 1), rows_of(1), ends, ends],
             [VMEM] * len(args), [VMEM] * 4, [],
-            (2 + 4 * len(blocks)) * count * per_frame * unit, 4 * count * per_frame * channels,
-            *args,
+            (4 + 2 * len(blocks)) * per_frame * unit, 4 * per_frame * channels, *args,
         )
+        others = (on, off, acts[frame]) if turn == 0 else (on, off)
+        if turn == 1:
+            late, off_late = acts[frame], off
 
     def stacked(count):
         return pltpu.VMEM((count * per_frame, 3 * channels), BF16)
 
     def from_earlier(late, off):
         pair = frame_pairings(late)
-        corner = across_next_frames(off)
+        corner = corner_pairings(off)
         partner = [xor_permute(frames, "space", 1) for frames in pair]
         return pair, corner, partner
 
     def earlier_part(pair, corner, packed, partial):
-        args = [*pair, corner, packed, partial]
+        args = [*pair, *corner, packed, partial]
         return call(
             functools.partial(earlier_body, columns),
             shape(tokens, 3 * channels, F32), [VMEM] * len(args), VMEM,
@@ -501,10 +528,9 @@
             [stacked(frame_count)], 18 * tokens * unit, 8 * tokens * channels, *args,
         )
 
-    act_late, mid_late, on_late, off_late = attend(blocks_late, early, 2)
-    pair, corner, partner = from_earlier(act_late, off_late)
-    act_early, mid_early, on, off = attend(blocks_early, 0, early, on_late, off_late)
-    partial = own_part([(early, act_early), (2, act_late)], on, off, packed_first)
+    pair, corner, partner = from_earlier(late, off_late)
+    groups = [(1, acts[frame]) for frame in range(early)] + [(2, late)]
+    partial = own_part(groups, on, off, packed_first)
     partial = earlier_part(pair, corner, packed_first, partial)
     args = [*partner, packed_first, partial, conv_gain_second]
     act, late, on, off, off_late = call(
@@ -518,7 +544,7 @@
     token_total = tokens * lax.axis_size("dp") * lax.axis_size("tm") * lax.axis_size("space")
     partial = earlier_part(pair, corner, packed_second, partial)
     args = [
-        *partner, packed_second, partial, mid_early, mid_late,
+        *partner, packed_second, partial, *(mids[frame] for frame in range(frame_count)),
         slope, hidden_t, latent_t, predicted, student_out,
     ]
     teacher, mine, yours = call(

time: 94.2 us -> 96.2 us (1.021)
  waiting for transfers between devices: 32.5 us -> 36.1 us
  Pallas kernels: 30.7 us -> 28.9 us
    ppermute x2, waiting for transfers between devices: 0.01 us -> 8.62 us  [across_permute(): return lax.ppermute(value, ('dp', 'space'), pairs)]
    ppermute x4, waiting for transfers between devices: 9.23 us -> 2.39 us  [frame_pairings(): results.append(lax.ppermute(value, ('tm', 'space'), pairs))]
    ppermute x2 -> x4, starting transfers between devices: 1.72 us -> 5.21 us  [corner_pairings(): results.append(lax.ppermute(value, ('dp', 'tm', 'space'), pairs))]
    pallas_call x10 -> x11, Pallas kernels: 30.7 us -> 28.9 us  [call(): pl.pallas_call(body, out_shape=outs, in_specs=specs, out_specs=out_specs,...]
    ppermute x17 -> x18, starting transfers between devices: 12.3 us -> 10.9 us  [xor_permute(): return lax.ppermute(value, axis, [(i, i ^ mask) for i in range(count)])]
    ppermute x17 -> x18, waiting for transfers between devices: 16.3 us -> 17.6 us  [xor_permute(): return lax.ppermute(value, axis, [(i, i ^ mask) for i in range(count)])]
    ppermute x4, starting transfers between devices: 4.43 us -> 3.38 us  [frame_pairings(): results.append(lax.ppermute(value, ('tm', 'space'), pairs))]
  transfers between devices with their start and end apart: 31 -> 34, of which waited for: 12 -> 17; matrix products, arithmetic and copies ran while one was open for 0% -> 0% of each run, Pallas kernels for 27% -> 24%
where the time goes in v2:
time: 96.2 us; the launch traced here: 96.1 us
  waiting for transfers between devices  36.1 us (38%)
  Pallas kernels  28.9 us (30%)
  starting transfers between devices  28.8 us (30%)
  other arithmetic  1.26 us (1%)
    pallas_call x11, Pallas kernels, call(): pl.pallas_call(body, out_shape=outs, in_specs=specs, out_specs=out_specs,...  28.9 us
    ppermute x18, waiting for transfers between devices, xor_permute(): return lax.ppermute(value, axis, [(i, i ^ mask) for i in range(count)])  17.6 us
    ppermute x18, starting transfers between devices, xor_permute(): return lax.ppermute(value, axis, [(i, i ^ mask) for i in range(count)])  10.9 us
    ppermute x2, waiting for transfers between devices, across_permute(): return lax.ppermute(value, ('dp', 'space'), pairs)  8.62 us
    ppermute x6, waiting for transfers between devices, plane_permute(): return lax.ppermute(value, ('dp', 'space'), pairs)  7.55 us
    ppermute x6, starting transfers between devices, plane_permute(): return lax.ppermute(value, ('dp', 'space'), pairs)  7.1 us
    ppermute x4, starting transfers between devices, corner_pairings(): results.append(lax.ppermute(value, ('dp', 'tm', 'space'), pairs))  5.21 us
    ppermute x4, starting transfers between devices, frame_pairings(): results.append(lax.ppermute(value, ('tm', 'space'), pairs))  3.38 us
  transfers between devices with their start and end apart: 34, of which 17 were waited for; matrix products, arithmetic and copies ran while one was open for 0% of the time, Pallas kernels for 24%

profile of v2, /device:TPU:0, one launch (start us, length us, event | category | flops | bytes accessed | tf_op | source)
XLA Modules:
  0.0 96.1 jit_solution(13755763684984496941)
XLA Ops:
  0.6 1.4 %shard_map.139 = (bf16[624,384]{1,0:T(8,128)(2,1)S(1)}, bf16[624,384]{1,0:T(8,128)(2,1)S(1)}, bf16[208,384]{1,0:T(8,128)(2,1)S(1)}, bf16[208,384]{1,0:T(8,128)(2,1)S(1)}, bf16[208,384]{1,0:T(8,128)(2,1)S(1)}) custom-call(bf16[3,208,384]{2,1,0:T(8,128)(2,1)} %bitcast.2, f32[384]{0:T(512)} %gain_hbm.1), custom_call_target="tpu_custom_call" | custom-call | bytes 958464 | tf_op jit(solution)/shard_map/pallas_call | solution.py:149
  2.6 2.6 %collective-permute-start.3 = (bf16[208,384]{1,0:T(8,128)(2,1)S(1)}, bf16[208,384]{1,0:T(8,128)(2,1)S(1)}, u32[]{:S(2)}, u32[]{:S(2)}) collective-permute-start(bf16[208,384]{1,0:T(8,128)(2,1)S(1)} %get-tuple-element.48), channel_id=1, source_target_pairs={{0,2},{1,3},{2,0},{3,1},{4,6},{5,7},{6,4},{7,5},{8,10},{9,11},{10,... | collective-permute-start | bytes 479240 | tf_op jit(solution)/shard_map/ppermute | solution.py:20
  5.2 1.9 %collective-permute-start.11 = (bf16[208,384]{1,0:T(8,128)(2,1)S(1)}, bf16[208,384]{1,0:T(8,128)(2,1)S(1)}, u32[]{:S(2)}, u32[]{:S(2)}) collective-permute-start(bf16[208,384]{1,0:T(8,128)(2,1)S(1)} %get-tuple-element.55), channel_id=1, source_target_pairs={{0,2},{1,3},{2,0},{3,1},{4,6},{5,7},{6,4},{7,5},{8,10},{9,11},{10,... | collective-permute-start | bytes 479240 | tf_op jit(solution)/shard_map/ppermute | solution.py:20
  7.2 2.9 %collective-permute-done.3.refs_0_ = bf16[208,384]{1,0:T(8,128)(2,1)S(1)} collective-permute-done((bf16[208,384]{1,0:T(8,128)(2,1)S(1)}, bf16[208,384]{1,0:T(8,128)(2,1)S(1)}, u32[]{:S(2)}, u32[]{:S(2)}) %collective-permute-start.3) | collective-permute-done | bytes 159776 | tf_op jit(solution)/shard_map/ppermute | solution.py:20
  10.1 3.4 %collective-permute-done.refs_0_ = bf16[208,384]{1,0:T(8,128)(2,1)S(1)} collective-permute-done((bf16[208,384]{1,0:T(8,128)(2,1)S(1)}, bf16[208,384]{1,0:T(8,128)(2,1)S(1)}, u32[]{:S(2)}, u32[]{:S(2)}) %collective-permute-start) | collective-permute-done | bytes 159776 | tf_op jit(solution)/shard_map/ppermute | solution.py:20
  13.5 3.2 %collective-permute-done.11.refs_0_ = bf16[208,384]{1,0:T(8,128)(2,1)S(1)} collective-permute-done((bf16[208,384]{1,0:T(8,128)(2,1)S(1)}, bf16[208,384]{1,0:T(8,128)(2,1)S(1)}, u32[]{:S(2)}, u32[]{:S(2)}) %collective-permute-start.11) | collective-permute-done | bytes 159776 | tf_op jit(solution)/shard_map/ppermute | solution.py:20
  16.7 6.1 %shard_map.140 = (bf16[384,768]{1,0:T(8,128)(2,1)S(1)}, bf16[384,384]{1,0:T(8,128)(2,1)S(1)}, bf16[384,384]{1,0:T(8,128)(2,1)S(1)}, bf16[3456,1152]{1,0:T(8,128)...) custom-call(bf16[624,384]{1,0:T(8,128)(2,1)S(1)} %get-tuple-element., ...), custom_call_target="tpu_custom_call" | custom-call | flops 1288175616 | bytes 17694720 | tf_op jit(solution)/shard_map/pallas_call | solution.py:149
  22.9 1.6 %shard_map.141 = (bf16[208,384]{1,0:T(8,128)(2,1)S(1)}, bf16[208,384]{1,0:T(8,128)(2,1)S(1)}, bf16[104,384]{1,0:T(8,128)(2,1)S(1)}, bf16[104,384]{1,0:T(8,128)(2,1)S(1)}) custom-call(bf16[208,384]{1,0:T(8,128)(2,1)S(1)} %collective-permute-done.3.refs_0_, bf16[208,384]{1,0:T(8,128)(2,1)S(1)} %collective-permute-done.4.refs_1_, ...), custom_call_target="tpu_custom_call" | custom-call | flops 490733568 | bytes 319488 | tf_op jit(solution)/shard_map/pallas_call | solution.py:149
  24.4 1.6 %shard_map.142 = (bf16[416,384]{1,0:T(8,128)(2,1)S(1)}, bf16[208,384]{1,0:T(8,128)(2,1)S(1)}, bf16[208,384]{1,0:T(8,128)(2,1)S(1)}, bf16[208,384]{1,0:T(8,128)(2,1)S(1)}) custom-call(bf16[208,384]{1,0:T(8,128)(2,1)S(1)} %collective-permute-done.refs_0_, bf16[208,384]{1,0:T(8,128)(2,1)S(1)} %collective-permute-done.1.refs_1_, ...), custom_call_target="tpu_custom_call" | custom-call | flops 490733568 | bytes 319488 | tf_op jit(solution)/shard_map/pallas_call | solution.py:149
  26.0 1.9 %collective-permute-start.5 = (bf16[416,384]{1,0:T(8,128)(2,1)S(1)}, bf16[416,384]{1,0:T(8,128)(2,1)S(1)}, u32[]{:S(2)}, u32[]{:S(2)}) collective-permute-start(bf16[416,384]{1,0:T(8,128)(2,1)S(1)} %get-tuple-element.52.refs_1_), channel_id=1, source_target_pairs={{0,4},{1,5},{2,6},{3,7},{4,0},{5,1},{6,2},{7,3},{8,12},{9,13},{10,... | collective-permute-start | bytes 958472 | tf_op jit(solution)/shard_map/ppermute | solution.py:62
  28.1 1.6 %shard_map.143 = (bf16[208,384]{1,0:T(8,128)(2,1)S(1)}, bf16[208,384]{1,0:T(8,128)(2,1)S(1)}, bf16[312,384]{1,0:T(8,128)(2,1)S(1)}, bf16[312,384]{1,0:T(8,128)(2,1)S(1)}) custom-call(bf16[208,384]{1,0:T(8,128)(2,1)S(1)} %collective-permute-done.11.refs_0_, bf16[208,384]{1,0:T(8,128)(2,1)S(1)} %collective-permute-done.12.refs_1_, ...), custom_call_target="tpu_custom_call" | custom-call | flops 490733568 | bytes 319488 | tf_op jit(solution)/shard_map/pallas_call | solution.py:149
  29.7 1.6 %collective-permute-start.13 = (bf16[312,384]{1,0:T(8,128)(2,1)S(1)}, bf16[312,384]{1,0:T(8,128)(2,1)S(1)}, u32[]{:S(2)}, u32[]{:S(2)}) collective-permute-start(bf16[312,384]{1,0:T(8,128)(2,1)S(1)} %get-tuple-element.58), channel_id=1, source_target_pairs={{0,16},{1,2},{2,1},{3,19},{16,0},{17,18},{18,17},{19,3},{4,20},{5,... | collective-permute-start | bytes 718856 | tf_op jit(solution)/shard_map/ppermute | solution.py:48
  31.4 1.5 %collective-permute-start.10 = (bf16[208,384]{1,0:T(8,128)(2,1)S(1)}, bf16[208,384]{1,0:T(8,128)(2,1)S(1)}, u32[]{:S(2)}, u32[]{:S(2)}) collective-permute-start(bf16[208,384]{1,0:T(8,128)(2,1)S(1)} %get-tuple-element.54.refs_10_), channel_id=1, source_target_pairs={{0,16},{1,17},{2,18},{3,19},{4,20},{5,10},{6,9},{7,23},{8,24},{9,6... | collective-permute-start | bytes 479240 | tf_op jit(solution)/shard_map/ppermute | solution.py:82
  32.9 4.5 %collective-permute-done.13.refs_2_ = bf16[312,384]{1,0:T(8,128)(2,1)S(1)} collective-permute-done((bf16[312,384]{1,0:T(8,128)(2,1)S(1)}, bf16[312,384]{1,0:T(8,128)(2,1)S(1)}, u32[]{:S(2)}, u32[]{:S(2)}) %collective-permute-start.13) | collective-permute-done | bytes 239648 | tf_op jit(solution)/shard_map/ppermute | solution.py:48
  37.4 1.7 %collective-permute-start.9 = (bf16[208,384]{1,0:T(8,128)(2,1)S(1)}, bf16[208,384]{1,0:T(8,128)(2,1)S(1)}, u32[]{:S(2)}, u32[]{:S(2)}) collective-permute-start(bf16[208,384]{1,0:T(8,128)(2,1)S(1)} %get-tuple-element.54.refs_10_), channel_id=1, source_target_pairs={{0,16},{1,6},{2,5},{3,19},{4,20},{5,2},{6,1},{7,23},{8,24},{9,14},... | collective-permute-start | bytes 479240 | tf_op jit(solution)/shard_map/ppermute | solution.py:82
  39.6 4.0 %shard_map.144.partial = f32[624,1152]{1,0:T(8,128)S(1)} custom-call(bf16[208,384]{1,0:T(8,128)(2,1)S(1)} %get-tuple-element.57.refs_0_, bf16[416,384]{1,0:T(8,128)(2,1)S(1)} %get-tuple-element.52.refs_1_, bf16[312,384]{1,0:T(8,128)(2,1)S(1)} %collective-permute-done.13.refs_2_, bf16[312,384]{1,0:T(8,128)(2,1)S(1)} %collective-permute-done.14.refs_3_, ...), custom_call_target="tpu_custom_call" | custom-call | flops 3312451584 | bytes 1916928 | tf_op jit(solution)/shard_map/pallas_call | solution.py:149
  43.7 2.4 %shard_map.145.partial = f32[624,1152]{1,0:T(8,128)S(1)} custom-call(bf16[416,384]{1,0:T(8,128)(2,1)S(1)} %collective-permute-done.5.low, bf16[416,384]{1,0:T(8,128)(2,1)S(1)} %collective-permute-done.7.high, bf16[208,384]{1,0:T(8,128)(2,1)S(1)} %collective-permute-done.9.off_low, bf16[208,384]{1,0:T(8,128)(2,1)S(1)} %collective-permute-done.10.off_high, ...), custom_call_target="tpu_custom_call" | custom-call | flops 1656225792 | bytes 1916928 | tf_op jit(solution)/shard_map/pallas_call | solution.py:149
  49.4 1.4 %collective-permute-start.19 = (bf16[208,384]{1,0:T(8,128)(2,1)S(1)}, bf16[208,384]{1,0:T(8,128)(2,1)S(1)}, u32[]{:S(2)}, u32[]{:S(2)}) collective-permute-start(bf16[208,384]{1,0:T(8,128)(2,1)S(1)} %get-tuple-element.62), channel_id=1, source_target_pairs={{0,16},{1,6},{2,5},{3,19},{4,20},{5,2},{6,1},{7,23},{8,24},{9,14},... | collective-permute-start | bytes 479240 | tf_op jit(solution)/shard_map/ppermute | solution.py:82
  50.8 4.1 %collective-permute-done.21.refs_1_ = bf16[312,384]{1,0:T(8,128)(2,1)S(1)} collective-permute-done((bf16[312,384]{1,0:T(8,128)(2,1)S(1)}, bf16[312,384]{1,0:T(8,128)(2,1)S(1)}, u32[]{:S(2)}, u32[]{:S(2)}) %collective-permute-start.21) | collective-permute-done | bytes 239648 | tf_op jit(solution)/shard_map/ppermute | solution.py:48
  55.5 2.4 %collective-permute-done.15.low = bf16[416,384]{1,0:T(8,128)(2,1)S(1)} collective-permute-done((bf16[416,384]{1,0:T(8,128)(2,1)S(1)}, bf16[416,384]{1,0:T(8,128)(2,1)S(1)}, u32[]{:S(2)}, u32[]{:S(2)}) %collective-permute-start.15) | collective-permute-done | bytes 319520 | tf_op jit(solution)/shard_map/ppermute | solution.py:62
  58.4 4.0 %shard_map.147.partial = f32[624,1152]{1,0:T(8,128)S(1)} custom-call(bf16[624,384]{1,0:T(8,128)(2,1)S(1)} %get-tuple-element.63.refs_0_, bf16[312,384]{1,0:T(8,128)(2,1)S(1)} %collective-permute-done.21.refs_1_, bf16[312,384]{1,0:T(8,128)(2,1)S(1)} %collective-permute-done.22.refs_2_, bf16[3456,1152]{1,0:T(8,128)(2,1)S(1)} %get-tuple-element.61.refs_3_.packed), custom_call_target="tpu_custom_call" | custom-call | flops 3312451584 | bytes 1916928 | tf_op jit(solution)/shard_map/pallas_call | solution.py:149
  62.5 2.2 %shard_map.148.partial = f32[624,1152]{1,0:T(8,128)S(1)} custom-call(bf16[416,384]{1,0:T(8,128)(2,1)S(1)} %collective-permute-done.15.low, bf16[416,384]{1,0:T(8,128)(2,1)S(1)} %collective-permute-done.17.high, bf16[208,384]{1,0:T(8,128)(2,1)S(1)} %collective-permute-done.19.off_low, bf16[208,384]{1,0:T(8,128)(2,1)S(1)} %collective-permute-done.20.off_high, ...), custom_call_target="tpu_custom_call" | custom-call | flops 1656225792 | bytes 1916928 | tf_op jit(solution)/shard_map/pallas_call | solution.py:149
  64.7 2.8 %shard_map.149 = (bf16[624,384]{1,0:T(8,128)(2,1)}, f32[384,384]{1,0:T(8,128)S(1)}, bf16[384,384]{1,0:T(8,128)(2,1)S(1)}) custom-call(bf16[416,384]{1,0:T(8,128)(2,1)S(1)} %collective-permute-done.16.low, bf16[416,384]{1,0:T(8,128)(2,1)S(1)} %collective-permute-done.18.high, bf16[3456,1152]{1,0:T(8,128)(2,1)S(1)} %get-tuple-element.61.refs_3_.packed, ...), custom_call_target="tpu_custom_call" | custom-call | flops 2208301056 | bytes 1916928 | tf_op jit(solution)/shard_map/pallas_call | solution.py:149
  67.5 1.6 %collective-permute-done.23 = bf16[384,384]{1,0:T(8,128)(2,1)S(1)} collective-permute-done((bf16[384,384]{1,0:T(8,128)(2,1)S(1)}, bf16[384,384]{1,0:T(8,128)(2,1)S(1)}, u32[]{:S(2)}, u32[]{:S(2)}) %collective-permute-start.23) | collective-permute-done | bytes 294944 | tf_op jit(solution)/shard_map/ppermute | solution.py:20
  70.6 2.1 %collective-permute-start.26 = (bf16[96,384]{1,0:T(8,128)(2,1)S(1)}, bf16[96,384]{1,0:T(8,128)(2,1)S(1)}, u32[]{:S(2)}, u32[]{:S(2)}) collective-permute-start(bf16[96,384]{1,0:T(8,128)(2,1)S(1)} %get-tuple-element.84), channel_id=1, source_target_pairs={{0,18},{1,19},{2,16},{3,17},{16,2},{17,3},{18,0},{19,1},{4,22},{5,... | collective-permute-start | bytes 221192 | tf_op jit(solution)/shard_map/ppermute | solution.py:99
  73.7 2.6 %collective-permute-done.26 = bf16[96,384]{1,0:T(8,128)(2,1)S(1)} collective-permute-done((bf16[96,384]{1,0:T(8,128)(2,1)S(1)}, bf16[96,384]{1,0:T(8,128)(2,1)S(1)}, u32[]{:S(2)}, u32[]{:S(2)}) %collective-permute-start.26) | collective-permute-done | bytes 73760 | tf_op jit(solution)/shard_map/ppermute | solution.py:99
  77.6 1.8 %collective-permute-start.28 = (bf16[96,384]{1,0:T(8,128)(2,1)S(1)}, bf16[96,384]{1,0:T(8,128)(2,1)S(1)}, u32[]{:S(2)}, u32[]{:S(2)}) collective-permute-start(bf16[96,384]{1,0:T(8,128)(2,1)S(1)} %add_convert_fusion.1), channel_id=1, source_target_pairs={{0,8},{4,12},{8,0},{12,4},{1,9},{5,13},{9,1},{13,5},{2,10},{6,14},... | collective-permute-start | bytes 221192 | tf_op jit(solution)/shard_map/ppermute | solution.py:20
  79.4 1.4 %collective-permute-start.29 = (bf16[96,384]{1,0:T(8,128)(2,1)S(1)}, bf16[96,384]{1,0:T(8,128)(2,1)S(1)}, u32[]{:S(2)}, u32[]{:S(2)}) collective-permute-start(bf16[96,384]{1,0:T(8,128)(2,1)S(1)} %add_convert_fusion.1), channel_id=1, source_target_pairs={{0,12},{4,8},{8,4},{12,0},{1,13},{5,9},{9,5},{13,1},{2,14},{6,10},... | collective-permute-start | bytes 221192 | tf_op jit(solution)/shard_map/ppermute | solution.py:20
  81.1 3.3 %collective-permute-done.28 = bf16[96,384]{1,0:T(8,128)(2,1)S(1)} collective-permute-done((bf16[96,384]{1,0:T(8,128)(2,1)S(1)}, bf16[96,384]{1,0:T(8,128)(2,1)S(1)}, u32[]{:S(2)}, u32[]{:S(2)}) %collective-permute-start.28) | collective-permute-done | bytes 73760 | tf_op jit(solution)/shard_map/ppermute | solution.py:20
  86.7 1.4 %collective-permute-start.31 = (bf16[96,384]{1,0:T(8,128)(2,1)S(1)}, bf16[96,384]{1,0:T(8,128)(2,1)S(1)}, u32[]{:S(2)}, u32[]{:S(2)}) collective-permute-start(bf16[96,384]{1,0:T(8,128)(2,1)S(1)} %get-tuple-element.78), channel_id=1, source_target_pairs={{0,16},{1,17},{2,18},{3,19},{16,0},{17,1},{18,2},{19,3},{4,20},{5,... | collective-permute-start | bytes 221192 | tf_op jit(solution)/shard_map/ppermute | solution.py:99
  91.1 2.3 %collective-permute-done.32 = bf16[96,384]{1,0:T(8,128)(2,1)S(1)} collective-permute-done((bf16[96,384]{1,0:T(8,128)(2,1)S(1)}, bf16[96,384]{1,0:T(8,128)(2,1)S(1)}, u32[]{:S(2)}, u32[]{:S(2)}) %collective-permute-start.32) | collective-permute-done | bytes 73760 | tf_op jit(solution)/shard_map/ppermute | solution.py:99
  93.4 1.6 %collective-permute-done.33 = bf16[384,384]{1,0:T(8,128)(2,1)S(1)} collective-permute-done((bf16[384,384]{1,0:T(8,128)(2,1)S(1)}, bf16[384,384]{1,0:T(8,128)(2,1)S(1)}, u32[]{:S(2)}, u32[]{:S(2)}) %collective-permute-start.33) | collective-permute-done | bytes 294944 | tf_op jit(solution)/shard_map/ppermute | solution.py:20
  (60 shorter events, 16.6 us)
Async XLA Ops:
  2.0 14.7 %collective-permute-start.2 = (bf16[624,384]{1,0:T(8,128)(2,1)S(1)}, bf16[624,384]{1,0:T(8,128)(2,1)S(1)}, u32[]{:S(2)}, u32[]{:S(2)}) collective-permute-start(bf16[624,384]{1,0:T(8,128)(2,1)S(1)} %get-tuple-element.42.normed), channel_id=1, source_target_pairs={{0,1},{1,0},{2,3},{3,2},{4,5},{5,4},{6,7},{7,6},{8,9},{9,8},{10,11... | collective-permute-start | bytes 1437704 | tf_op jit(solution)/shard_map/ppermute | solution.py:20
  2.6 7.5 %collective-permute-start.3 = (bf16[208,384]{1,0:T(8,128)(2,1)S(1)}, bf16[208,384]{1,0:T(8,128)(2,1)S(1)}, u32[]{:S(2)}, u32[]{:S(2)}) collective-permute-start(bf16[208,384]{1,0:T(8,128)(2,1)S(1)} %get-tuple-element.48), channel_id=1, source_target_pairs={{0,2},{1,3},{2,0},{3,1},{4,6},{5,7},{6,4},{7,5},{8,10},{9,11},{10,... | collective-permute-start | bytes 479240 | tf_op jit(solution)/shard_map/ppermute | solution.py:20
  5.1 8.4 %collective-permute-start = (bf16[208,384]{1,0:T(8,128)(2,1)S(1)}, bf16[208,384]{1,0:T(8,128)(2,1)S(1)}, u32[]{:S(2)}, u32[]{:S(2)}) collective-permute-start(bf16[208,384]{1,0:T(8,128)(2,1)S(1)} %get-tuple-element.40), channel_id=1, source_target_pairs={{0,2},{1,3},{2,0},{3,1},{4,6},{5,7},{6,4},{7,5},{8,10},{9,11},{10,... | collective-permute-start | bytes 479240 | tf_op jit(solution)/shard_map/ppermute | solution.py:20
  5.2 11.5 %collective-permute-start.11 = (bf16[208,384]{1,0:T(8,128)(2,1)S(1)}, bf16[208,384]{1,0:T(8,128)(2,1)S(1)}, u32[]{:S(2)}, u32[]{:S(2)}) collective-permute-start(bf16[208,384]{1,0:T(8,128)(2,1)S(1)} %get-tuple-element.55), channel_id=1, source_target_pairs={{0,2},{1,3},{2,0},{3,1},{4,6},{5,7},{6,4},{7,5},{8,10},{9,11},{10,... | collective-permute-start | bytes 479240 | tf_op jit(solution)/shard_map/ppermute | solution.py:20
  10.1 12.8 %collective-permute-start.4 = (bf16[208,384]{1,0:T(8,128)(2,1)S(1)}, bf16[208,384]{1,0:T(8,128)(2,1)S(1)}, u32[]{:S(2)}, u32[]{:S(2)}) collective-permute-start(bf16[208,384]{1,0:T(8,128)(2,1)S(1)} %collective-permute-done.3.refs_0_), channel_id=1, source_target_pairs={{0,1},{1,0},{2,3},{3,2},{4,5},{5,4},{6,7},{7,6},{8,9},{9,8},{10,11... | collective-permute-start | bytes 479240 | tf_op jit(solution)/shard_map/ppermute | solution.py:20
  13.5 10.9 %collective-permute-start.1 = (bf16[208,384]{1,0:T(8,128)(2,1)S(1)}, bf16[208,384]{1,0:T(8,128)(2,1)S(1)}, u32[]{:S(2)}, u32[]{:S(2)}) collective-permute-start(bf16[208,384]{1,0:T(8,128)(2,1)S(1)} %collective-permute-done.refs_0_), channel_id=1, source_target_pairs={{0,1},{1,0},{2,3},{3,2},{4,5},{5,4},{6,7},{7,6},{8,9},{9,8},{10,11... | collective-permute-start | bytes 479240 | tf_op jit(solution)/shard_map/ppermute | solution.py:20
  16.7 11.4 %collective-permute-start.12 = (bf16[208,384]{1,0:T(8,128)(2,1)S(1)}, bf16[208,384]{1,0:T(8,128)(2,1)S(1)}, u32[]{:S(2)}, u32[]{:S(2)}) collective-permute-start(bf16[208,384]{1,0:T(8,128)(2,1)S(1)} %collective-permute-done.11.refs_0_), channel_id=1, source_target_pairs={{0,1},{1,0},{2,3},{3,2},{4,5},{5,4},{6,7},{7,6},{8,9},{9,8},{10,11... | collective-permute-start | bytes 479240 | tf_op jit(solution)/shard_map/ppermute | solution.py:20
  26.0 13.1 %collective-permute-start.5 = (bf16[416,384]{1,0:T(8,128)(2,1)S(1)}, bf16[416,384]{1,0:T(8,128)(2,1)S(1)}, u32[]{:S(2)}, u32[]{:S(2)}) collective-permute-start(bf16[416,384]{1,0:T(8,128)(2,1)S(1)} %get-tuple-element.52.refs_1_), channel_id=1, source_target_pairs={{0,4},{1,5},{2,6},{3,7},{4,0},{5,1},{6,2},{7,3},{8,12},{9,13},{10,... | collective-permute-start | bytes 958472 | tf_op jit(solution)/shard_map/ppermute | solution.py:62
  27.9 11.4 %collective-permute-start.7 = (bf16[416,384]{1,0:T(8,128)(2,1)S(1)}, bf16[416,384]{1,0:T(8,128)(2,1)S(1)}, u32[]{:S(2)}, u32[]{:S(2)}) collective-permute-start(bf16[416,384]{1,0:T(8,128)(2,1)S(1)} %get-tuple-element.52.refs_1_), channel_id=1, source_target_pairs={{0,1},{1,0},{2,3},{3,2},{4,8},{5,9},{6,10},{7,11},{8,4},{9,5},{10,... | collective-permute-start | bytes 958472 | tf_op jit(solution)/shard_map/ppermute | solution.py:62
  29.7 7.7 %collective-permute-start.13 = (bf16[312,384]{1,0:T(8,128)(2,1)S(1)}, bf16[312,384]{1,0:T(8,128)(2,1)S(1)}, u32[]{:S(2)}, u32[]{:S(2)}) collective-permute-start(bf16[312,384]{1,0:T(8,128)(2,1)S(1)} %get-tuple-element.58), channel_id=1, source_target_pairs={{0,16},{1,2},{2,1},{3,19},{16,0},{17,18},{18,17},{19,3},{4,20},{5,... | collective-permute-start | bytes 718856 | tf_op jit(solution)/shard_map/ppermute | solution.py:48
  31.2 8.4 %collective-permute-start.14 = (bf16[312,384]{1,0:T(8,128)(2,1)S(1)}, bf16[312,384]{1,0:T(8,128)(2,1)S(1)}, u32[]{:S(2)}, u32[]{:S(2)}) collective-permute-start(bf16[312,384]{1,0:T(8,128)(2,1)S(1)} %get-tuple-element.59), channel_id=1, source_target_pairs={{0,1},{1,0},{2,3},{3,2},{4,5},{5,4},{6,7},{7,6},{8,9},{9,8},{10,11... | collective-permute-start | bytes 718856 | tf_op jit(solution)/shard_map/ppermute | solution.py:20
  31.4 12.3 %collective-permute-start.10 = (bf16[208,384]{1,0:T(8,128)(2,1)S(1)}, bf16[208,384]{1,0:T(8,128)(2,1)S(1)}, u32[]{:S(2)}, u32[]{:S(2)}) collective-permute-start(bf16[208,384]{1,0:T(8,128)(2,1)S(1)} %get-tuple-element.54.refs_10_), channel_id=1, source_target_pairs={{0,16},{1,17},{2,18},{3,19},{4,20},{5,10},{6,9},{7,23},{8,24},{9,6... | collective-permute-start | bytes 479240 | tf_op jit(solution)/shard_map/ppermute | solution.py:82
  37.4 6.3 %collective-permute-start.9 = (bf16[208,384]{1,0:T(8,128)(2,1)S(1)}, bf16[208,384]{1,0:T(8,128)(2,1)S(1)}, u32[]{:S(2)}, u32[]{:S(2)}) collective-permute-start(bf16[208,384]{1,0:T(8,128)(2,1)S(1)} %get-tuple-element.54.refs_10_), channel_id=1, source_target_pairs={{0,16},{1,6},{2,5},{3,19},{4,20},{5,2},{6,1},{7,23},{8,24},{9,14},... | collective-permute-start | bytes 479240 | tf_op jit(solution)/shard_map/ppermute | solution.py:82
  39.1 7.0 %collective-permute-start.6 = (bf16[416,384]{1,0:T(8,128)(2,1)S(1)}, bf16[416,384]{1,0:T(8,128)(2,1)S(1)}, u32[]{:S(2)}, u32[]{:S(2)}) collective-permute-start(bf16[416,384]{1,0:T(8,128)(2,1)S(1)} %collective-permute-done.5.low), channel_id=1, source_target_pairs={{0,1},{1,0},{2,3},{3,2},{4,5},{5,4},{6,7},{7,6},{8,9},{9,8},{10,11... | collective-permute-start | bytes 958472 | tf_op jit(solution)/shard_map/ppermute | solution.py:20
  39.3 6.8 %collective-permute-start.8 = (bf16[416,384]{1,0:T(8,128)(2,1)S(1)}, bf16[416,384]{1,0:T(8,128)(2,1)S(1)}, u32[]{:S(2)}, u32[]{:S(2)}) collective-permute-start(bf16[416,384]{1,0:T(8,128)(2,1)S(1)} %collective-permute-done.7.high), channel_id=1, source_target_pairs={{0,1},{1,0},{2,3},{3,2},{4,5},{5,4},{6,7},{7,6},{8,9},{9,8},{10,11... | collective-permute-start | bytes 958472 | tf_op jit(solution)/shard_map/ppermute | solution.py:20
  47.4 10.5 %collective-permute-start.15 = (bf16[416,384]{1,0:T(8,128)(2,1)S(1)}, bf16[416,384]{1,0:T(8,128)(2,1)S(1)}, u32[]{:S(2)}, u32[]{:S(2)}) collective-permute-start(bf16[416,384]{1,0:T(8,128)(2,1)S(1)} %get-tuple-element.60), channel_id=1, source_target_pairs={{0,4},{1,5},{2,6},{3,7},{4,0},{5,1},{6,2},{7,3},{8,12},{9,13},{10,... | collective-permute-start | bytes 958472 | tf_op jit(solution)/shard_map/ppermute | solution.py:62
  48.7 9.2 %collective-permute-start.17 = (bf16[416,384]{1,0:T(8,128)(2,1)S(1)}, bf16[416,384]{1,0:T(8,128)(2,1)S(1)}, u32[]{:S(2)}, u32[]{:S(2)}) collective-permute-start(bf16[416,384]{1,0:T(8,128)(2,1)S(1)} %get-tuple-element.60), channel_id=1, source_target_pairs={{0,1},{1,0},{2,3},{3,2},{4,8},{5,9},{6,10},{7,11},{8,4},{9,5},{10,... | collective-permute-start | bytes 958472 | tf_op jit(solution)/shard_map/ppermute | solution.py:62
  48.7 6.1 %collective-permute-start.21 = (bf16[312,384]{1,0:T(8,128)(2,1)S(1)}, bf16[312,384]{1,0:T(8,128)(2,1)S(1)}, u32[]{:S(2)}, u32[]{:S(2)}) collective-permute-start(bf16[312,384]{1,0:T(8,128)(2,1)S(1)} %get-tuple-element.64), channel_id=1, source_target_pairs={{0,16},{1,2},{2,1},{3,19},{16,0},{17,18},{18,17},{19,3},{4,20},{5,... | collective-permute-start | bytes 718856 | tf_op jit(solution)/shard_map/ppermute | solution.py:48
  49.4 9.0 %collective-permute-start.22 = (bf16[312,384]{1,0:T(8,128)(2,1)S(1)}, bf16[312,384]{1,0:T(8,128)(2,1)S(1)}, u32[]{:S(2)}, u32[]{:S(2)}) collective-permute-start(bf16[312,384]{1,0:T(8,128)(2,1)S(1)} %get-tuple-element.65), channel_id=1, source_target_pairs={{0,1},{1,0},{2,3},{3,2},{4,5},{5,4},{6,7},{7,6},{8,9},{9,8},{10,11... | collective-permute-start | bytes 718856 | tf_op jit(solution)/shard_map/ppermute | solution.py:20
  49.4 13.1 %collective-permute-start.19 = (bf16[208,384]{1,0:T(8,128)(2,1)S(1)}, bf16[208,384]{1,0:T(8,128)(2,1)S(1)}, u32[]{:S(2)}, u32[]{:S(2)}) collective-permute-start(bf16[208,384]{1,0:T(8,128)(2,1)S(1)} %get-tuple-element.62), channel_id=1, source_target_pairs={{0,16},{1,6},{2,5},{3,19},{4,20},{5,2},{6,1},{7,23},{8,24},{9,14},... | collective-permute-start | bytes 479240 | tf_op jit(solution)/shard_map/ppermute | solution.py:82
  54.8 7.6 %collective-permute-start.20 = (bf16[208,384]{1,0:T(8,128)(2,1)S(1)}, bf16[208,384]{1,0:T(8,128)(2,1)S(1)}, u32[]{:S(2)}, u32[]{:S(2)}) collective-permute-start(bf16[208,384]{1,0:T(8,128)(2,1)S(1)} %get-tuple-element.62), channel_id=1, source_target_pairs={{0,16},{1,17},{2,18},{3,19},{4,20},{5,10},{6,9},{7,23},{8,24},{9,6... | collective-permute-start | bytes 479240 | tf_op jit(solution)/shard_map/ppermute | solution.py:82
  57.9 6.8 %collective-permute-start.16 = (bf16[416,384]{1,0:T(8,128)(2,1)S(1)}, bf16[416,384]{1,0:T(8,128)(2,1)S(1)}, u32[]{:S(2)}, u32[]{:S(2)}) collective-permute-start(bf16[416,384]{1,0:T(8,128)(2,1)S(1)} %collective-permute-done.15.low), channel_id=1, source_target_pairs={{0,1},{1,0},{2,3},{3,2},{4,5},{5,4},{6,7},{7,6},{8,9},{9,8},{10,11... | collective-permute-start | bytes 958472 | tf_op jit(solution)/shard_map/ppermute | solution.py:20
  57.9 6.8 %collective-permute-start.18 = (bf16[416,384]{1,0:T(8,128)(2,1)S(1)}, bf16[416,384]{1,0:T(8,128)(2,1)S(1)}, u32[]{:S(2)}, u32[]{:S(2)}) collective-permute-start(bf16[416,384]{1,0:T(8,128)(2,1)S(1)} %collective-permute-done.17.high), channel_id=1, source_target_pairs={{0,1},{1,0},{2,3},{3,2},{4,5},{5,4},{6,7},{7,6},{8,9},{9,8},{10,11... | collective-permute-start | bytes 958472 | tf_op jit(solution)/shard_map/ppermute | solution.py:20
  69.2 4.4 %collective-permute-start.24 = (bf16[96,384]{1,0:T(8,128)(2,1)S(1)}, bf16[96,384]{1,0:T(8,128)(2,1)S(1)}, u32[]{:S(2)}, u32[]{:S(2)}) collective-permute-start(bf16[96,384]{1,0:T(8,128)(2,1)S(1)} %get-tuple-element.83), channel_id=1, source_target_pairs={{0,2},{1,3},{2,0},{3,1},{16,18},{17,19},{18,16},{19,17},{4,6},{5,7... | collective-permute-start | bytes 221192 | tf_op jit(solution)/shard_map/ppermute | solution.py:99
  69.2 4.4 %collective-permute-start.25 = (bf16[96,384]{1,0:T(8,128)(2,1)S(1)}, bf16[96,384]{1,0:T(8,128)(2,1)S(1)}, u32[]{:S(2)}, u32[]{:S(2)}) collective-permute-start(bf16[96,384]{1,0:T(8,128)(2,1)S(1)} %get-tuple-element.85), channel_id=1, source_target_pairs={{0,16},{1,17},{2,18},{3,19},{16,0},{17,1},{18,2},{19,3},{4,20},{5,... | collective-permute-start | bytes 221192 | tf_op jit(solution)/shard_map/ppermute | solution.py:99
  70.6 5.7 %collective-permute-start.26 = (bf16[96,384]{1,0:T(8,128)(2,1)S(1)}, bf16[96,384]{1,0:T(8,128)(2,1)S(1)}, u32[]{:S(2)}, u32[]{:S(2)}) collective-permute-start(bf16[96,384]{1,0:T(8,128)(2,1)S(1)} %get-tuple-element.84), channel_id=1, source_target_pairs={{0,18},{1,19},{2,16},{3,17},{16,2},{17,3},{18,0},{19,1},{4,22},{5,... | collective-permute-start | bytes 221192 | tf_op jit(solution)/shard_map/ppermute | solution.py:99
  76.3 4.8 %collective-permute-start.27 = (bf16[96,384]{1,0:T(8,128)(2,1)S(1)}, bf16[96,384]{1,0:T(8,128)(2,1)S(1)}, u32[]{:S(2)}, u32[]{:S(2)}) collective-permute-start(bf16[96,384]{1,0:T(8,128)(2,1)S(1)} %add_convert_fusion.1), channel_id=1, source_target_pairs={{0,4},{4,0},{8,12},{12,8},{1,5},{5,1},{9,13},{13,9},{2,6},{6,2},{1... | collective-permute-start | bytes 221192 | tf_op jit(solution)/shard_map/ppermute | solution.py:20
  77.6 6.8 %collective-permute-start.28 = (bf16[96,384]{1,0:T(8,128)(2,1)S(1)}, bf16[96,384]{1,0:T(8,128)(2,1)S(1)}, u32[]{:S(2)}, u32[]{:S(2)}) collective-permute-start(bf16[96,384]{1,0:T(8,128)(2,1)S(1)} %add_convert_fusion.1), channel_id=1, source_target_pairs={{0,8},{4,12},{8,0},{12,4},{1,9},{5,13},{9,1},{13,5},{2,10},{6,14},... | collective-permute-start | bytes 221192 | tf_op jit(solution)/shard_map/ppermute | solution.py:20
  79.4 6.3 %collective-permute-start.29 = (bf16[96,384]{1,0:T(8,128)(2,1)S(1)}, bf16[96,384]{1,0:T(8,128)(2,1)S(1)}, u32[]{:S(2)}, u32[]{:S(2)}) collective-permute-start(bf16[96,384]{1,0:T(8,128)(2,1)S(1)} %add_convert_fusion.1), channel_id=1, source_target_pairs={{0,12},{4,8},{8,4},{12,0},{1,13},{5,9},{9,5},{13,1},{2,14},{6,10},... | collective-permute-start | bytes 221192 | tf_op jit(solution)/shard_map/ppermute | solution.py:20
  85.8 4.4 %collective-permute-start.30 = (bf16[96,384]{1,0:T(8,128)(2,1)S(1)}, bf16[96,384]{1,0:T(8,128)(2,1)S(1)}, u32[]{:S(2)}, u32[]{:S(2)}) collective-permute-start(bf16[96,384]{1,0:T(8,128)(2,1)S(1)} %get-tuple-element.78), channel_id=1, source_target_pairs={{0,2},{1,3},{2,0},{3,1},{16,18},{17,19},{18,16},{19,17},{4,6},{5,7... | collective-permute-start | bytes 221192 | tf_op jit(solution)/shard_map/ppermute | solution.py:99
  86.7 4.4 %collective-permute-start.31 = (bf16[96,384]{1,0:T(8,128)(2,1)S(1)}, bf16[96,384]{1,0:T(8,128)(2,1)S(1)}, u32[]{:S(2)}, u32[]{:S(2)}) collective-permute-start(bf16[96,384]{1,0:T(8,128)(2,1)S(1)} %get-tuple-element.78), channel_id=1, source_target_pairs={{0,16},{1,17},{2,18},{3,19},{16,0},{17,1},{18,2},{19,3},{4,20},{5,... | collective-permute-start | bytes 221192 | tf_op jit(solution)/shard_map/ppermute | solution.py:99
  88.1 5.3 %collective-permute-start.32 = (bf16[96,384]{1,0:T(8,128)(2,1)S(1)}, bf16[96,384]{1,0:T(8,128)(2,1)S(1)}, u32[]{:S(2)}, u32[]{:S(2)}) collective-permute-start(bf16[96,384]{1,0:T(8,128)(2,1)S(1)} %get-tuple-element.78), channel_id=1, source_target_pairs={{0,18},{1,19},{2,16},{3,17},{16,2},{17,3},{18,0},{19,1},{4,22},{5,... | collective-permute-start | bytes 221192 | tf_op jit(solution)/shard_map/ppermute | solution.py:99
  (4 other events, 11.9 us)

commit v3 on v2

--- a/solution.py
+++ b/solution.py
@@ -63,24 +63,14 @@
     return results
 
 
-def corner_pairings(value):
-    clips, blocks, count = (lax.axis_size(axis) for axis in ("dp", "tm", "space"))
-    rows = dict(across_pairs())
-    results = []
-    for first in range(2):
-        pairs = []
-        for clip in range(clips):
-            for block in range(blocks):
-                other = ((block - first) ^ 1) + first
-                for place in range(count):
-                    if place in rows and 0 <= other < blocks:
-                        target = (clip * blocks + other) * count + rows[place]
-                    else:
-                        target = ((clip ^ 1) * blocks + block) * count + place
-                    if target < clips * blocks * count:
-                        pairs.append(((clip * blocks + block) * count + place, target))
-        results.append(lax.ppermute(value, ("dp", "tm", "space"), pairs))
-    return results
+def across_next_frames(value):
+    count = lax.axis_size("space")
+    pairs = [
+        (block * count + source, (block + 1) * count + target)
+        for block in range(lax.axis_size("tm") - 1)
+        for source, target in across_pairs()
+    ]
+    return lax.ppermute(value, ("tm", "space"), pairs)
 
 
 def take_rows(value, index, rows):
@@ -97,6 +87,10 @@
             target = (other // chips * chips + other % chips) * 2 + core
             pairs.append((source, target))
     return lax.ppermute(value, ("dp", "space"), pairs)
+
+
+def span_permute(value, mask):
+    return xor_permute(value, "tm", mask)
 
 
 def sum_everywhere(mine, yours):
@@ -115,7 +109,7 @@
     for piece in arrived:
         chunk = chunk + piece.astype(F32)
     chunk = chunk.astype(BF16)
-    pieces = [chunk] + [xor_permute(chunk, "tm", mask) for mask in range(1, tm_count)]
+    pieces = [chunk] + [span_permute(chunk, mask) for mask in range(1, tm_count)]
     pieces = [piece.astype(F32) for piece in pieces]
     while len(pieces) > 1:
         pieces = [pieces[i] + pieces[i + 1] for i in range(0, len(pieces), 2)]
@@ -336,13 +330,12 @@
         partial[pl.ds(frame * per_frame, per_frame)] = total
 
 
-def earlier_body(columns, low, high, off_low, off_high, packed, partial, total, stacked):
+def earlier_body(columns, low, high, off, packed, partial, total, stacked):
     odd = is_odd()
     per_frame = stacked.shape[0] // 2
     for frame in range(2):
         tail = choose_frames((low, high), pl.ds(frame * per_frame, per_frame))
-        edge = choose_frames((off_low, off_high), pl.ds(frame * columns, columns))
-        edge = jnp.where(has_across(), edge, jnp.zeros_like(edge))
+        edge = off[pl.ds(frame * columns, columns)]
         stack_rows(columns, odd, tail, jnp.zeros_like(edge), edge, stacked, frame)
     for frame in range(partial.shape[0] // per_frame):
         here = pl.ds(frame * per_frame, per_frame)
@@ -506,12 +499,12 @@
 
     def from_earlier(late, off):
         pair = frame_pairings(late)
-        corner = corner_pairings(off)
+        corner = across_next_frames(off)
         partner = [xor_permute(frames, "space", 1) for frames in pair]
         return pair, corner, partner
 
     def earlier_part(pair, corner, packed, partial):
-        args = [*pair, *corner, packed, partial]
+        args = [*pair, corner, packed, partial]
         return call(
             functools.partial(earlier_body, columns),
             shape(tokens, 3 * channels, F32), [VMEM] * len(args), VMEM,

time: 96.2 us -> 95 us (0.988)
    ppermute x2, waiting for transfers between devices: 8.62 us -> 0.01 us  [across_permute(): return lax.ppermute(value, ('dp', 'space'), pairs)]
    ppermute x4, waiting for transfers between devices: 2.39 us -> 9.34 us  [frame_pairings(): results.append(lax.ppermute(value, ('tm', 'space'), pairs))]
    ppermute x4 -> x2, starting transfers between devices: 5.21 us -> 1.72 us  [across_next_frames(): return lax.ppermute(value, ('tm', 'space'), pairs)]
    ppermute x18, starting transfers between devices: 10.9 us -> 11.9 us  [xor_permute(): return lax.ppermute(value, axis, [(i, i ^ mask) for i in range(count)])]
  transfers between devices with their start and end apart: 34 -> 32, of which waited for: 17 -> 15; matrix products, arithmetic and copies ran while one was open for 0% -> 0% of each run, Pallas kernels for 24% -> 25%
where the time goes in v3:
time: 95 us; the launch traced here: 94.8 us
  waiting for transfers between devices  35.9 us (38%)
  Pallas kernels  28.7 us (30%)
  starting transfers between devices  27.9 us (29%)
  other arithmetic  1.26 us (1%)
    pallas_call x11, Pallas kernels, call(): pl.pallas_call(body, out_shape=outs, in_specs=specs, out_specs=out_specs,...  28.7 us
    ppermute x18, waiting for transfers between devices, xor_permute(): return lax.ppermute(value, axis, [(i, i ^ mask) for i in range(count)])  18.3 us
    ppermute x18, starting transfers between devices, xor_permute(): return lax.ppermute(value, axis, [(i, i ^ mask) for i in range(count)])  11.9 us
    ppermute x4, waiting for transfers between devices, frame_pairings(): results.append(lax.ppermute(value, ('tm', 'space'), pairs))  9.34 us
    ppermute x6, waiting for transfers between devices, plane_permute(): return lax.ppermute(value, ('dp', 'space'), pairs)  8.22 us
    ppermute x6, starting transfers between devices, plane_permute(): return lax.ppermute(value, ('dp', 'space'), pairs)  7.11 us
    ppermute x4, starting transfers between devices, frame_pairings(): results.append(lax.ppermute(value, ('tm', 'space'), pairs))  4.21 us
    ppermute x2, starting transfers between devices, across_permute(): return lax.ppermute(value, ('dp', 'space'), pairs)  3.04 us
  transfers between devices with their start and end apart: 32, of which 15 were waited for; matrix products, arithmetic and copies ran while one was open for 0% of the time, Pallas kernels for 25%

profile of v3, /device:TPU:0, one launch (start us, length us, event | category | flops | bytes accessed | tf_op | source)
XLA Modules:
  0.0 94.8 jit_solution(3642879057075751074)
XLA Ops:
  0.6 1.4 %shard_map.139 = (bf16[624,384]{1,0:T(8,128)(2,1)S(1)}, bf16[624,384]{1,0:T(8,128)(2,1)S(1)}, bf16[208,384]{1,0:T(8,128)(2,1)S(1)}, bf16[208,384]{1,0:T(8,128)(2,1)S(1)}, bf16[208,384]{1,0:T(8,128)(2,1)S(1)}) custom-call(bf16[3,208,384]{2,1,0:T(8,128)(2,1)} %bitcast.2, f32[384]{0:T(512)} %gain_hbm.1), custom_call_target="tpu_custom_call" | custom-call | bytes 958464 | tf_op jit(solution)/shard_map/pallas_call | solution.py:143
  2.6 2.6 %collective-permute-start.3 = (bf16[208,384]{1,0:T(8,128)(2,1)S(1)}, bf16[208,384]{1,0:T(8,128)(2,1)S(1)}, u32[]{:S(2)}, u32[]{:S(2)}) collective-permute-start(bf16[208,384]{1,0:T(8,128)(2,1)S(1)} %get-tuple-element.48), channel_id=1, source_target_pairs={{0,2},{1,3},{2,0},{3,1},{4,6},{5,7},{6,4},{7,5},{8,10},{9,11},{10,... | collective-permute-start | bytes 479240 | tf_op jit(solution)/shard_map/ppermute | solution.py:20
  5.2 1.9 %collective-permute-start.10 = (bf16[208,384]{1,0:T(8,128)(2,1)S(1)}, bf16[208,384]{1,0:T(8,128)(2,1)S(1)}, u32[]{:S(2)}, u32[]{:S(2)}) collective-permute-start(bf16[208,384]{1,0:T(8,128)(2,1)S(1)} %get-tuple-element.55), channel_id=1, source_target_pairs={{0,2},{1,3},{2,0},{3,1},{4,6},{5,7},{6,4},{7,5},{8,10},{9,11},{10,... | collective-permute-start | bytes 479240 | tf_op jit(solution)/shard_map/ppermute | solution.py:20
  7.2 2.9 %collective-permute-done.3.refs_0_ = bf16[208,384]{1,0:T(8,128)(2,1)S(1)} collective-permute-done((bf16[208,384]{1,0:T(8,128)(2,1)S(1)}, bf16[208,384]{1,0:T(8,128)(2,1)S(1)}, u32[]{:S(2)}, u32[]{:S(2)}) %collective-permute-start.3) | collective-permute-done | bytes 159776 | tf_op jit(solution)/shard_map/ppermute | solution.py:20
  10.1 3.4 %collective-permute-done.refs_0_ = bf16[208,384]{1,0:T(8,128)(2,1)S(1)} collective-permute-done((bf16[208,384]{1,0:T(8,128)(2,1)S(1)}, bf16[208,384]{1,0:T(8,128)(2,1)S(1)}, u32[]{:S(2)}, u32[]{:S(2)}) %collective-permute-start) | collective-permute-done | bytes 159776 | tf_op jit(solution)/shard_map/ppermute | solution.py:20
  13.5 3.2 %collective-permute-done.10.refs_0_ = bf16[208,384]{1,0:T(8,128)(2,1)S(1)} collective-permute-done((bf16[208,384]{1,0:T(8,128)(2,1)S(1)}, bf16[208,384]{1,0:T(8,128)(2,1)S(1)}, u32[]{:S(2)}, u32[]{:S(2)}) %collective-permute-start.10) | collective-permute-done | bytes 159776 | tf_op jit(solution)/shard_map/ppermute | solution.py:20
  16.7 6.1 %shard_map.140 = (bf16[384,768]{1,0:T(8,128)(2,1)S(1)}, bf16[384,384]{1,0:T(8,128)(2,1)S(1)}, bf16[384,384]{1,0:T(8,128)(2,1)S(1)}, bf16[3456,1152]{1,0:T(8,128)...) custom-call(bf16[624,384]{1,0:T(8,128)(2,1)S(1)} %get-tuple-element., ...), custom_call_target="tpu_custom_call" | custom-call | flops 1288175616 | bytes 17694720 | tf_op jit(solution)/shard_map/pallas_call | solution.py:143
  22.9 1.6 %shard_map.141 = (bf16[208,384]{1,0:T(8,128)(2,1)S(1)}, bf16[208,384]{1,0:T(8,128)(2,1)S(1)}, bf16[104,384]{1,0:T(8,128)(2,1)S(1)}, bf16[104,384]{1,0:T(8,128)(2,1)S(1)}) custom-call(bf16[208,384]{1,0:T(8,128)(2,1)S(1)} %collective-permute-done.3.refs_0_, bf16[208,384]{1,0:T(8,128)(2,1)S(1)} %collective-permute-done.4.refs_1_, ...), custom_call_target="tpu_custom_call" | custom-call | flops 490733568 | bytes 319488 | tf_op jit(solution)/shard_map/pallas_call | solution.py:143
  24.4 1.6 %shard_map.142 = (bf16[416,384]{1,0:T(8,128)(2,1)S(1)}, bf16[208,384]{1,0:T(8,128)(2,1)S(1)}, bf16[208,384]{1,0:T(8,128)(2,1)S(1)}, bf16[208,384]{1,0:T(8,128)(2,1)S(1)}) custom-call(bf16[208,384]{1,0:T(8,128)(2,1)S(1)} %collective-permute-done.refs_0_, bf16[208,384]{1,0:T(8,128)(2,1)S(1)} %collective-permute-done.1.refs_1_, ...), custom_call_target="tpu_custom_call" | custom-call | flops 490733568 | bytes 319488 | tf_op jit(solution)/shard_map/pallas_call | solution.py:143
  26.0 1.9 %collective-permute-start.5 = (bf16[416,384]{1,0:T(8,128)(2,1)S(1)}, bf16[416,384]{1,0:T(8,128)(2,1)S(1)}, u32[]{:S(2)}, u32[]{:S(2)}) collective-permute-start(bf16[416,384]{1,0:T(8,128)(2,1)S(1)} %get-tuple-element.52.refs_1_), channel_id=1, source_target_pairs={{0,4},{1,5},{2,6},{3,7},{4,0},{5,1},{6,2},{7,3},{8,12},{9,13},{10,... | collective-permute-start | bytes 958472 | tf_op jit(solution)/shard_map/ppermute | solution.py:62
  28.1 1.6 %shard_map.143 = (bf16[208,384]{1,0:T(8,128)(2,1)S(1)}, bf16[208,384]{1,0:T(8,128)(2,1)S(1)}, bf16[312,384]{1,0:T(8,128)(2,1)S(1)}, bf16[312,384]{1,0:T(8,128)(2,1)S(1)}) custom-call(bf16[208,384]{1,0:T(8,128)(2,1)S(1)} %collective-permute-done.10.refs_0_, bf16[208,384]{1,0:T(8,128)(2,1)S(1)} %collective-permute-done.11.refs_1_, ...), custom_call_target="tpu_custom_call" | custom-call | flops 490733568 | bytes 319488 | tf_op jit(solution)/shard_map/pallas_call | solution.py:143
  29.7 1.6 %collective-permute-start.12 = (bf16[312,384]{1,0:T(8,128)(2,1)S(1)}, bf16[312,384]{1,0:T(8,128)(2,1)S(1)}, u32[]{:S(2)}, u32[]{:S(2)}) collective-permute-start(bf16[312,384]{1,0:T(8,128)(2,1)S(1)} %get-tuple-element.58), channel_id=1, source_target_pairs={{0,16},{1,2},{2,1},{3,19},{16,0},{17,18},{18,17},{19,3},{4,20},{5,... | collective-permute-start | bytes 718856 | tf_op jit(solution)/shard_map/ppermute | solution.py:48
  32.2 3.9 %collective-permute-done.5.low = bf16[416,384]{1,0:T(8,128)(2,1)S(1)} collective-permute-done((bf16[416,384]{1,0:T(8,128)(2,1)S(1)}, bf16[416,384]{1,0:T(8,128)(2,1)S(1)}, u32[]{:S(2)}, u32[]{:S(2)}) %collective-permute-start.5) | collective-permute-done | bytes 319520 | tf_op jit(solution)/shard_map/ppermute | solution.py:62
  37.1 4.0 %shard_map.144.partial = f32[624,1152]{1,0:T(8,128)S(1)} custom-call(bf16[208,384]{1,0:T(8,128)(2,1)S(1)} %get-tuple-element.57.refs_0_, bf16[416,384]{1,0:T(8,128)(2,1)S(1)} %get-tuple-element.52.refs_1_, bf16[312,384]{1,0:T(8,128)(2,1)S(1)} %collective-permute-done.12.refs_2_, bf16[312,384]{1,0:T(8,128)(2,1)S(1)} %collective-permute-done.13.refs_3_, ...), custom_call_target="tpu_custom_call" | custom-call | flops 3312451584 | bytes 1916928 | tf_op jit(solution)/shard_map/pallas_call | solution.py:143
  41.2 2.2 %shard_map.145.partial = f32[624,1152]{1,0:T(8,128)S(1)} custom-call(bf16[416,384]{1,0:T(8,128)(2,1)S(1)} %collective-permute-done.5.low, bf16[416,384]{1,0:T(8,128)(2,1)S(1)} %collective-permute-done.7.high, bf16[208,384]{1,0:T(8,128)(2,1)S(1)} %collective-permute-done.9.off, bf16[3456,1152]{1,0:T(8,128)(2,1)S(1)} %get-tuple-element.53.refs_4_.packed, ...), custom_call_target="tpu_custom_call" | custom-call | flops 1656225792 | bytes 1916928 | tf_op jit(solution)/shard_map/pallas_call | solution.py:143
  44.8 1.9 %collective-permute-start.14 = (bf16[416,384]{1,0:T(8,128)(2,1)S(1)}, bf16[416,384]{1,0:T(8,128)(2,1)S(1)}, u32[]{:S(2)}, u32[]{:S(2)}) collective-permute-start(bf16[416,384]{1,0:T(8,128)(2,1)S(1)} %get-tuple-element.60), channel_id=1, source_target_pairs={{0,4},{1,5},{2,6},{3,7},{4,0},{5,1},{6,2},{7,3},{8,12},{9,13},{10,... | collective-permute-start | bytes 958472 | tf_op jit(solution)/shard_map/ppermute | solution.py:62
  46.9 1.5 %collective-permute-start.19 = (bf16[312,384]{1,0:T(8,128)(2,1)S(1)}, bf16[312,384]{1,0:T(8,128)(2,1)S(1)}, u32[]{:S(2)}, u32[]{:S(2)}) collective-permute-start(bf16[312,384]{1,0:T(8,128)(2,1)S(1)} %get-tuple-element.64), channel_id=1, source_target_pairs={{0,16},{1,2},{2,1},{3,19},{16,0},{17,18},{18,17},{19,3},{4,20},{5,... | collective-permute-start | bytes 718856 | tf_op jit(solution)/shard_map/ppermute | solution.py:48
  49.4 5.5 %collective-permute-done.14.low = bf16[416,384]{1,0:T(8,128)(2,1)S(1)} collective-permute-done((bf16[416,384]{1,0:T(8,128)(2,1)S(1)}, bf16[416,384]{1,0:T(8,128)(2,1)S(1)}, u32[]{:S(2)}, u32[]{:S(2)}) %collective-permute-start.14) | collective-permute-done | bytes 319520 | tf_op jit(solution)/shard_map/ppermute | solution.py:62
  55.4 4.1 %shard_map.147.partial = f32[624,1152]{1,0:T(8,128)S(1)} custom-call(bf16[624,384]{1,0:T(8,128)(2,1)S(1)} %get-tuple-element.63.refs_0_, bf16[312,384]{1,0:T(8,128)(2,1)S(1)} %collective-permute-done.19.refs_1_, bf16[312,384]{1,0:T(8,128)(2,1)S(1)} %collective-permute-done.20.refs_2_, bf16[3456,1152]{1,0:T(8,128)(2,1)S(1)} %get-tuple-element.61.refs_3_.packed), custom_call_target="tpu_custom_call" | custom-call | flops 3312451584 | bytes 1916928 | tf_op jit(solution)/shard_map/pallas_call | solution.py:143
  59.5 2.1 %shard_map.148.partial = f32[624,1152]{1,0:T(8,128)S(1)} custom-call(bf16[416,384]{1,0:T(8,128)(2,1)S(1)} %collective-permute-done.14.low, bf16[416,384]{1,0:T(8,128)(2,1)S(1)} %collective-permute-done.16.high, bf16[208,384]{1,0:T(8,128)(2,1)S(1)} %collective-permute-done.18.off, bf16[3456,1152]{1,0:T(8,128)(2,1)S(1)} %get-tuple-element.61.refs_3_.packed, ...), custom_call_target="tpu_custom_call" | custom-call | flops 1656225792 | bytes 1916928 | tf_op jit(solution)/shard_map/pallas_call | solution.py:143
  61.6 2.8 %shard_map.149 = (bf16[624,384]{1,0:T(8,128)(2,1)}, f32[384,384]{1,0:T(8,128)S(1)}, bf16[384,384]{1,0:T(8,128)(2,1)S(1)}) custom-call(bf16[416,384]{1,0:T(8,128)(2,1)S(1)} %collective-permute-done.15.low, bf16[416,384]{1,0:T(8,128)(2,1)S(1)} %collective-permute-done.17.high, bf16[3456,1152]{1,0:T(8,128)(2,1)S(1)} %get-tuple-element.61.refs_3_.packed, ...), custom_call_target="tpu_custom_call" | custom-call | flops 2208301056 | bytes 1916928 | tf_op jit(solution)/shard_map/pallas_call | solution.py:143
  64.4 1.6 %collective-permute-done.21 = bf16[384,384]{1,0:T(8,128)(2,1)S(1)} collective-permute-done((bf16[384,384]{1,0:T(8,128)(2,1)S(1)}, bf16[384,384]{1,0:T(8,128)(2,1)S(1)}, u32[]{:S(2)}, u32[]{:S(2)}) %collective-permute-start.21) | collective-permute-done | bytes 294944 | tf_op jit(solution)/shard_map/ppermute | solution.py:20
  66.1 1.6 %collective-permute-start.22 = (bf16[96,384]{1,0:T(8,128)(2,1)S(1)}, bf16[96,384]{1,0:T(8,128)(2,1)S(1)}, u32[]{:S(2)}, u32[]{:S(2)}) collective-permute-start(bf16[96,384]{1,0:T(8,128)(2,1)S(1)} %get-tuple-element.83), channel_id=1, source_target_pairs={{0,2},{1,3},{2,0},{3,1},{16,18},{17,19},{18,16},{19,17},{4,6},{5,7... | collective-permute-start | bytes 221192 | tf_op jit(solution)/shard_map/ppermute | solution.py:89
  67.7 1.5 %collective-permute-start.23 = (bf16[96,384]{1,0:T(8,128)(2,1)S(1)}, bf16[96,384]{1,0:T(8,128)(2,1)S(1)}, u32[]{:S(2)}, u32[]{:S(2)}) collective-permute-start(bf16[96,384]{1,0:T(8,128)(2,1)S(1)} %get-tuple-element.85), channel_id=1, source_target_pairs={{0,16},{1,17},{2,18},{3,19},{16,0},{17,1},{18,2},{19,3},{4,20},{5,... | collective-permute-start | bytes 221192 | tf_op jit(solution)/shard_map/ppermute | solution.py:89
  70.5 2.3 %collective-permute-done.23 = bf16[96,384]{1,0:T(8,128)(2,1)S(1)} collective-permute-done((bf16[96,384]{1,0:T(8,128)(2,1)S(1)}, bf16[96,384]{1,0:T(8,128)(2,1)S(1)}, u32[]{:S(2)}, u32[]{:S(2)}) %collective-permute-start.23) | collective-permute-done | bytes 73760 | tf_op jit(solution)/shard_map/ppermute | solution.py:89
  72.8 1.6 %collective-permute-done.24 = bf16[96,384]{1,0:T(8,128)(2,1)S(1)} collective-permute-done((bf16[96,384]{1,0:T(8,128)(2,1)S(1)}, bf16[96,384]{1,0:T(8,128)(2,1)S(1)}, u32[]{:S(2)}, u32[]{:S(2)}) %collective-permute-start.24) | collective-permute-done | bytes 73760 | tf_op jit(solution)/shard_map/ppermute | solution.py:89
  74.5 1.8 %collective-permute-start.25 = (bf16[96,384]{1,0:T(8,128)(2,1)S(1)}, bf16[96,384]{1,0:T(8,128)(2,1)S(1)}, u32[]{:S(2)}, u32[]{:S(2)}) collective-permute-start(bf16[96,384]{1,0:T(8,128)(2,1)S(1)} %add_convert_fusion.1), channel_id=1, source_target_pairs={{0,4},{4,0},{8,12},{12,8},{1,5},{5,1},{9,13},{13,9},{2,6},{6,2},{1... | collective-permute-start | bytes 221192 | tf_op jit(solution)/shard_map/ppermute | solution.py:20
  76.3 1.9 %collective-permute-start.26 = (bf16[96,384]{1,0:T(8,128)(2,1)S(1)}, bf16[96,384]{1,0:T(8,128)(2,1)S(1)}, u32[]{:S(2)}, u32[]{:S(2)}) collective-permute-start(bf16[96,384]{1,0:T(8,128)(2,1)S(1)} %add_convert_fusion.1), channel_id=1, source_target_pairs={{0,8},{4,12},{8,0},{12,4},{1,9},{5,13},{9,1},{13,5},{2,10},{6,14},... | collective-permute-start | bytes 221192 | tf_op jit(solution)/shard_map/ppermute | solution.py:20
  79.7 5.2 %collective-permute-done.26 = bf16[96,384]{1,0:T(8,128)(2,1)S(1)} collective-permute-done((bf16[96,384]{1,0:T(8,128)(2,1)S(1)}, bf16[96,384]{1,0:T(8,128)(2,1)S(1)}, u32[]{:S(2)}, u32[]{:S(2)}) %collective-permute-start.26) | collective-permute-done | bytes 73760 | tf_op jit(solution)/shard_map/ppermute | solution.py:20
  86.8 1.8 %collective-permute-start.30 = (bf16[96,384]{1,0:T(8,128)(2,1)S(1)}, bf16[96,384]{1,0:T(8,128)(2,1)S(1)}, u32[]{:S(2)}, u32[]{:S(2)}) collective-permute-start(bf16[96,384]{1,0:T(8,128)(2,1)S(1)} %get-tuple-element.78), channel_id=1, source_target_pairs={{0,18},{1,19},{2,16},{3,17},{16,2},{17,3},{18,0},{19,1},{4,22},{5,... | collective-permute-start | bytes 221192 | tf_op jit(solution)/shard_map/ppermute | solution.py:89
  90.5 1.6 %collective-permute-done.30 = bf16[96,384]{1,0:T(8,128)(2,1)S(1)} collective-permute-done((bf16[96,384]{1,0:T(8,128)(2,1)S(1)}, bf16[96,384]{1,0:T(8,128)(2,1)S(1)}, u32[]{:S(2)}, u32[]{:S(2)}) %collective-permute-start.30) | collective-permute-done | bytes 73760 | tf_op jit(solution)/shard_map/ppermute | solution.py:89
  92.1 1.6 %collective-permute-done.31 = bf16[384,384]{1,0:T(8,128)(2,1)S(1)} collective-permute-done((bf16[384,384]{1,0:T(8,128)(2,1)S(1)}, bf16[384,384]{1,0:T(8,128)(2,1)S(1)}, u32[]{:S(2)}, u32[]{:S(2)}) %collective-permute-start.31) | collective-permute-done | bytes 294944 | tf_op jit(solution)/shard_map/ppermute | solution.py:20
  (56 shorter events, 14.0 us)
Async XLA Ops:
  2.0 14.7 %collective-permute-start.2 = (bf16[624,384]{1,0:T(8,128)(2,1)S(1)}, bf16[624,384]{1,0:T(8,128)(2,1)S(1)}, u32[]{:S(2)}, u32[]{:S(2)}) collective-permute-start(bf16[624,384]{1,0:T(8,128)(2,1)S(1)} %get-tuple-element.42.normed), channel_id=1, source_target_pairs={{0,1},{1,0},{2,3},{3,2},{4,5},{5,4},{6,7},{7,6},{8,9},{9,8},{10,11... | collective-permute-start | bytes 1437704 | tf_op jit(solution)/shard_map/ppermute | solution.py:20
  2.6 7.5 %collective-permute-start.3 = (bf16[208,384]{1,0:T(8,128)(2,1)S(1)}, bf16[208,384]{1,0:T(8,128)(2,1)S(1)}, u32[]{:S(2)}, u32[]{:S(2)}) collective-permute-start(bf16[208,384]{1,0:T(8,128)(2,1)S(1)} %get-tuple-element.48), channel_id=1, source_target_pairs={{0,2},{1,3},{2,0},{3,1},{4,6},{5,7},{6,4},{7,5},{8,10},{9,11},{10,... | collective-permute-start | bytes 479240 | tf_op jit(solution)/shard_map/ppermute | solution.py:20
  5.1 8.4 %collective-permute-start = (bf16[208,384]{1,0:T(8,128)(2,1)S(1)}, bf16[208,384]{1,0:T(8,128)(2,1)S(1)}, u32[]{:S(2)}, u32[]{:S(2)}) collective-permute-start(bf16[208,384]{1,0:T(8,128)(2,1)S(1)} %get-tuple-element.40), channel_id=1, source_target_pairs={{0,2},{1,3},{2,0},{3,1},{4,6},{5,7},{6,4},{7,5},{8,10},{9,11},{10,... | collective-permute-start | bytes 479240 | tf_op jit(solution)/shard_map/ppermute | solution.py:20
  5.2 11.5 %collective-permute-start.10 = (bf16[208,384]{1,0:T(8,128)(2,1)S(1)}, bf16[208,384]{1,0:T(8,128)(2,1)S(1)}, u32[]{:S(2)}, u32[]{:S(2)}) collective-permute-start(bf16[208,384]{1,0:T(8,128)(2,1)S(1)} %get-tuple-element.55), channel_id=1, source_target_pairs={{0,2},{1,3},{2,0},{3,1},{4,6},{5,7},{6,4},{7,5},{8,10},{9,11},{10,... | collective-permute-start | bytes 479240 | tf_op jit(solution)/shard_map/ppermute | solution.py:20
  10.1 12.8 %collective-permute-start.4 = (bf16[208,384]{1,0:T(8,128)(2,1)S(1)}, bf16[208,384]{1,0:T(8,128)(2,1)S(1)}, u32[]{:S(2)}, u32[]{:S(2)}) collective-permute-start(bf16[208,384]{1,0:T(8,128)(2,1)S(1)} %collective-permute-done.3.refs_0_), channel_id=1, source_target_pairs={{0,1},{1,0},{2,3},{3,2},{4,5},{5,4},{6,7},{7,6},{8,9},{9,8},{10,11... | collective-permute-start | bytes 479240 | tf_op jit(solution)/shard_map/ppermute | solution.py:20
  13.5 10.9 %collective-permute-start.1 = (bf16[208,384]{1,0:T(8,128)(2,1)S(1)}, bf16[208,384]{1,0:T(8,128)(2,1)S(1)}, u32[]{:S(2)}, u32[]{:S(2)}) collective-permute-start(bf16[208,384]{1,0:T(8,128)(2,1)S(1)} %collective-permute-done.refs_0_), channel_id=1, source_target_pairs={{0,1},{1,0},{2,3},{3,2},{4,5},{5,4},{6,7},{7,6},{8,9},{9,8},{10,11... | collective-permute-start | bytes 479240 | tf_op jit(solution)/shard_map/ppermute | solution.py:20
  16.7 11.4 %collective-permute-start.11 = (bf16[208,384]{1,0:T(8,128)(2,1)S(1)}, bf16[208,384]{1,0:T(8,128)(2,1)S(1)}, u32[]{:S(2)}, u32[]{:S(2)}) collective-permute-start(bf16[208,384]{1,0:T(8,128)(2,1)S(1)} %collective-permute-done.10.refs_0_), channel_id=1, source_target_pairs={{0,1},{1,0},{2,3},{3,2},{4,5},{5,4},{6,7},{7,6},{8,9},{9,8},{10,11... | collective-permute-start | bytes 479240 | tf_op jit(solution)/shard_map/ppermute | solution.py:20
  26.0 10.1 %collective-permute-start.5 = (bf16[416,384]{1,0:T(8,128)(2,1)S(1)}, bf16[416,384]{1,0:T(8,128)(2,1)S(1)}, u32[]{:S(2)}, u32[]{:S(2)}) collective-permute-start(bf16[416,384]{1,0:T(8,128)(2,1)S(1)} %get-tuple-element.52.refs_1_), channel_id=1, source_target_pairs={{0,4},{1,5},{2,6},{3,7},{4,0},{5,1},{6,2},{7,3},{8,12},{9,13},{10,... | collective-permute-start | bytes 958472 | tf_op jit(solution)/shard_map/ppermute | solution.py:62
  27.9 9.2 %collective-permute-start.7 = (bf16[416,384]{1,0:T(8,128)(2,1)S(1)}, bf16[416,384]{1,0:T(8,128)(2,1)S(1)}, u32[]{:S(2)}, u32[]{:S(2)}) collective-permute-start(bf16[416,384]{1,0:T(8,128)(2,1)S(1)} %get-tuple-element.52.refs_1_), channel_id=1, source_target_pairs={{0,1},{1,0},{2,3},{3,2},{4,8},{5,9},{6,10},{7,11},{8,4},{9,5},{10,... | collective-permute-start | bytes 958472 | tf_op jit(solution)/shard_map/ppermute | solution.py:62
  29.7 7.5 %collective-permute-start.12 = (bf16[312,384]{1,0:T(8,128)(2,1)S(1)}, bf16[312,384]{1,0:T(8,128)(2,1)S(1)}, u32[]{:S(2)}, u32[]{:S(2)}) collective-permute-start(bf16[312,384]{1,0:T(8,128)(2,1)S(1)} %get-tuple-element.58), channel_id=1, source_target_pairs={{0,16},{1,2},{2,1},{3,19},{16,0},{17,18},{18,17},{19,3},{4,20},{5,... | collective-permute-start | bytes 718856 | tf_op jit(solution)/shard_map/ppermute | solution.py:48
  31.2 5.9 %collective-permute-start.13 = (bf16[312,384]{1,0:T(8,128)(2,1)S(1)}, bf16[312,384]{1,0:T(8,128)(2,1)S(1)}, u32[]{:S(2)}, u32[]{:S(2)}) collective-permute-start(bf16[312,384]{1,0:T(8,128)(2,1)S(1)} %get-tuple-element.59), channel_id=1, source_target_pairs={{0,1},{1,0},{2,3},{3,2},{4,5},{5,4},{6,7},{7,6},{8,9},{9,8},{10,11... | collective-permute-start | bytes 718856 | tf_op jit(solution)/shard_map/ppermute | solution.py:20
  31.4 9.9 %collective-permute-start.9 = (bf16[208,384]{1,0:T(8,128)(2,1)S(1)}, bf16[208,384]{1,0:T(8,128)(2,1)S(1)}, u32[]{:S(2)}, u32[]{:S(2)}) collective-permute-start(bf16[208,384]{1,0:T(8,128)(2,1)S(1)} %get-tuple-element.54.refs_10_), channel_id=1, source_target_pairs={{1,6},{2,5},{5,10},{6,9},{9,14},{10,13},{17,22},{18,21},{21,26},{2... | collective-permute-start | bytes 479240 | tf_op jit(solution)/shard_map/ppermute | solution.py:73
  36.1 7.3 %collective-permute-start.6 = (bf16[416,384]{1,0:T(8,128)(2,1)S(1)}, bf16[416,384]{1,0:T(8,128)(2,1)S(1)}, u32[]{:S(2)}, u32[]{:S(2)}) collective-permute-start(bf16[416,384]{1,0:T(8,128)(2,1)S(1)} %collective-permute-done.5.low), channel_id=1, source_target_pairs={{0,1},{1,0},{2,3},{3,2},{4,5},{5,4},{6,7},{7,6},{8,9},{9,8},{10,11... | collective-permute-start | bytes 958472 | tf_op jit(solution)/shard_map/ppermute | solution.py:20
  37.1 6.4 %collective-permute-start.8 = (bf16[416,384]{1,0:T(8,128)(2,1)S(1)}, bf16[416,384]{1,0:T(8,128)(2,1)S(1)}, u32[]{:S(2)}, u32[]{:S(2)}) collective-permute-start(bf16[416,384]{1,0:T(8,128)(2,1)S(1)} %collective-permute-done.7.high), channel_id=1, source_target_pairs={{0,1},{1,0},{2,3},{3,2},{4,5},{5,4},{6,7},{7,6},{8,9},{9,8},{10,11... | collective-permute-start | bytes 958472 | tf_op jit(solution)/shard_map/ppermute | solution.py:20
  44.8 10.1 %collective-permute-start.14 = (bf16[416,384]{1,0:T(8,128)(2,1)S(1)}, bf16[416,384]{1,0:T(8,128)(2,1)S(1)}, u32[]{:S(2)}, u32[]{:S(2)}) collective-permute-start(bf16[416,384]{1,0:T(8,128)(2,1)S(1)} %get-tuple-element.60), channel_id=1, source_target_pairs={{0,4},{1,5},{2,6},{3,7},{4,0},{5,1},{6,2},{7,3},{8,12},{9,13},{10,... | collective-permute-start | bytes 958472 | tf_op jit(solution)/shard_map/ppermute | solution.py:62
  46.7 8.2 %collective-permute-start.16 = (bf16[416,384]{1,0:T(8,128)(2,1)S(1)}, bf16[416,384]{1,0:T(8,128)(2,1)S(1)}, u32[]{:S(2)}, u32[]{:S(2)}) collective-permute-start(bf16[416,384]{1,0:T(8,128)(2,1)S(1)} %get-tuple-element.60), channel_id=1, source_target_pairs={{0,1},{1,0},{2,3},{3,2},{4,8},{5,9},{6,10},{7,11},{8,4},{9,5},{10,... | collective-permute-start | bytes 958472 | tf_op jit(solution)/shard_map/ppermute | solution.py:62
  46.9 8.5 %collective-permute-start.19 = (bf16[312,384]{1,0:T(8,128)(2,1)S(1)}, bf16[312,384]{1,0:T(8,128)(2,1)S(1)}, u32[]{:S(2)}, u32[]{:S(2)}) collective-permute-start(bf16[312,384]{1,0:T(8,128)(2,1)S(1)} %get-tuple-element.64), channel_id=1, source_target_pairs={{0,16},{1,2},{2,1},{3,19},{16,0},{17,18},{18,17},{19,3},{4,20},{5,... | collective-permute-start | bytes 718856 | tf_op jit(solution)/shard_map/ppermute | solution.py:48
  48.4 7.0 %collective-permute-start.20 = (bf16[312,384]{1,0:T(8,128)(2,1)S(1)}, bf16[312,384]{1,0:T(8,128)(2,1)S(1)}, u32[]{:S(2)}, u32[]{:S(2)}) collective-permute-start(bf16[312,384]{1,0:T(8,128)(2,1)S(1)} %get-tuple-element.65), channel_id=1, source_target_pairs={{0,1},{1,0},{2,3},{3,2},{4,5},{5,4},{6,7},{7,6},{8,9},{9,8},{10,11... | collective-permute-start | bytes 718856 | tf_op jit(solution)/shard_map/ppermute | solution.py:20
  48.5 10.9 %collective-permute-start.18 = (bf16[208,384]{1,0:T(8,128)(2,1)S(1)}, bf16[208,384]{1,0:T(8,128)(2,1)S(1)}, u32[]{:S(2)}, u32[]{:S(2)}) collective-permute-start(bf16[208,384]{1,0:T(8,128)(2,1)S(1)} %get-tuple-element.62), channel_id=1, source_target_pairs={{1,6},{2,5},{5,10},{6,9},{9,14},{10,13},{17,22},{18,21},{21,26},{2... | collective-permute-start | bytes 479240 | tf_op jit(solution)/shard_map/ppermute | solution.py:73
  54.9 6.7 %collective-permute-start.15 = (bf16[416,384]{1,0:T(8,128)(2,1)S(1)}, bf16[416,384]{1,0:T(8,128)(2,1)S(1)}, u32[]{:S(2)}, u32[]{:S(2)}) collective-permute-start(bf16[416,384]{1,0:T(8,128)(2,1)S(1)} %collective-permute-done.14.low), channel_id=1, source_target_pairs={{0,1},{1,0},{2,3},{3,2},{4,5},{5,4},{6,7},{7,6},{8,9},{9,8},{10,11... | collective-permute-start | bytes 958472 | tf_op jit(solution)/shard_map/ppermute | solution.py:20
  54.9 6.7 %collective-permute-start.17 = (bf16[416,384]{1,0:T(8,128)(2,1)S(1)}, bf16[416,384]{1,0:T(8,128)(2,1)S(1)}, u32[]{:S(2)}, u32[]{:S(2)}) collective-permute-start(bf16[416,384]{1,0:T(8,128)(2,1)S(1)} %collective-permute-done.16.high), channel_id=1, source_target_pairs={{0,1},{1,0},{2,3},{3,2},{4,5},{5,4},{6,7},{7,6},{8,9},{9,8},{10,11... | collective-permute-start | bytes 958472 | tf_op jit(solution)/shard_map/ppermute | solution.py:20
  64.4 1.6 %collective-permute-start.21 = (bf16[384,384]{1,0:T(8,128)(2,1)S(1)}, bf16[384,384]{1,0:T(8,128)(2,1)S(1)}, u32[]{:S(2)}, u32[]{:S(2)}) collective-permute-start(bf16[384,384]{1,0:T(8,128)(2,1)S(1)} %get-tuple-element.76), channel_id=1, source_target_pairs={{0,1},{1,0},{2,3},{3,2},{4,5},{5,4},{6,7},{7,6},{8,9},{9,8},{10,11... | collective-permute-start | bytes 884744 | tf_op jit(solution)/shard_map/ppermute | solution.py:20
  66.1 4.4 %collective-permute-start.22 = (bf16[96,384]{1,0:T(8,128)(2,1)S(1)}, bf16[96,384]{1,0:T(8,128)(2,1)S(1)}, u32[]{:S(2)}, u32[]{:S(2)}) collective-permute-start(bf16[96,384]{1,0:T(8,128)(2,1)S(1)} %get-tuple-element.83), channel_id=1, source_target_pairs={{0,2},{1,3},{2,0},{3,1},{16,18},{17,19},{18,16},{19,17},{4,6},{5,7... | collective-permute-start | bytes 221192 | tf_op jit(solution)/shard_map/ppermute | solution.py:89
  67.7 5.1 %collective-permute-start.23 = (bf16[96,384]{1,0:T(8,128)(2,1)S(1)}, bf16[96,384]{1,0:T(8,128)(2,1)S(1)}, u32[]{:S(2)}, u32[]{:S(2)}) collective-permute-start(bf16[96,384]{1,0:T(8,128)(2,1)S(1)} %get-tuple-element.85), channel_id=1, source_target_pairs={{0,16},{1,17},{2,18},{3,19},{16,0},{17,1},{18,2},{19,3},{4,20},{5,... | collective-permute-start | bytes 221192 | tf_op jit(solution)/shard_map/ppermute | solution.py:89
  69.2 5.3 %collective-permute-start.24 = (bf16[96,384]{1,0:T(8,128)(2,1)S(1)}, bf16[96,384]{1,0:T(8,128)(2,1)S(1)}, u32[]{:S(2)}, u32[]{:S(2)}) collective-permute-start(bf16[96,384]{1,0:T(8,128)(2,1)S(1)} %get-tuple-element.84), channel_id=1, source_target_pairs={{0,18},{1,19},{2,16},{3,17},{16,2},{17,3},{18,0},{19,1},{4,22},{5,... | collective-permute-start | bytes 221192 | tf_op jit(solution)/shard_map/ppermute | solution.py:89
  74.5 5.2 %collective-permute-start.25 = (bf16[96,384]{1,0:T(8,128)(2,1)S(1)}, bf16[96,384]{1,0:T(8,128)(2,1)S(1)}, u32[]{:S(2)}, u32[]{:S(2)}) collective-permute-start(bf16[96,384]{1,0:T(8,128)(2,1)S(1)} %add_convert_fusion.1), channel_id=1, source_target_pairs={{0,4},{4,0},{8,12},{12,8},{1,5},{5,1},{9,13},{13,9},{2,6},{6,2},{1... | collective-permute-start | bytes 221192 | tf_op jit(solution)/shard_map/ppermute | solution.py:20
  76.3 8.6 %collective-permute-start.26 = (bf16[96,384]{1,0:T(8,128)(2,1)S(1)}, bf16[96,384]{1,0:T(8,128)(2,1)S(1)}, u32[]{:S(2)}, u32[]{:S(2)}) collective-permute-start(bf16[96,384]{1,0:T(8,128)(2,1)S(1)} %add_convert_fusion.1), channel_id=1, source_target_pairs={{0,8},{4,12},{8,0},{12,4},{1,9},{5,13},{9,1},{13,5},{2,10},{6,14},... | collective-permute-start | bytes 221192 | tf_op jit(solution)/shard_map/ppermute | solution.py:20
  78.2 6.7 %collective-permute-start.27 = (bf16[96,384]{1,0:T(8,128)(2,1)S(1)}, bf16[96,384]{1,0:T(8,128)(2,1)S(1)}, u32[]{:S(2)}, u32[]{:S(2)}) collective-permute-start(bf16[96,384]{1,0:T(8,128)(2,1)S(1)} %add_convert_fusion.1), channel_id=1, source_target_pairs={{0,12},{4,8},{8,4},{12,0},{1,13},{5,9},{9,5},{13,1},{2,14},{6,10},... | collective-permute-start | bytes 221192 | tf_op jit(solution)/shard_map/ppermute | solution.py:20
  85.0 4.4 %collective-permute-start.28 = (bf16[96,384]{1,0:T(8,128)(2,1)S(1)}, bf16[96,384]{1,0:T(8,128)(2,1)S(1)}, u32[]{:S(2)}, u32[]{:S(2)}) collective-permute-start(bf16[96,384]{1,0:T(8,128)(2,1)S(1)} %get-tuple-element.78), channel_id=1, source_target_pairs={{0,2},{1,3},{2,0},{3,1},{16,18},{17,19},{18,16},{19,17},{4,6},{5,7... | collective-permute-start | bytes 221192 | tf_op jit(solution)/shard_map/ppermute | solution.py:89
  86.1 4.4 %collective-permute-start.29 = (bf16[96,384]{1,0:T(8,128)(2,1)S(1)}, bf16[96,384]{1,0:T(8,128)(2,1)S(1)}, u32[]{:S(2)}, u32[]{:S(2)}) collective-permute-start(bf16[96,384]{1,0:T(8,128)(2,1)S(1)} %get-tuple-element.78), channel_id=1, source_target_pairs={{0,16},{1,17},{2,18},{3,19},{16,0},{17,1},{18,2},{19,3},{4,20},{5,... | collective-permute-start | bytes 221192 | tf_op jit(solution)/shard_map/ppermute | solution.py:89
  86.8 5.3 %collective-permute-start.30 = (bf16[96,384]{1,0:T(8,128)(2,1)S(1)}, bf16[96,384]{1,0:T(8,128)(2,1)S(1)}, u32[]{:S(2)}, u32[]{:S(2)}) collective-permute-start(bf16[96,384]{1,0:T(8,128)(2,1)S(1)} %get-tuple-element.78), channel_id=1, source_target_pairs={{0,18},{1,19},{2,16},{3,17},{16,2},{17,3},{18,0},{19,1},{4,22},{5,... | collective-permute-start | bytes 221192 | tf_op jit(solution)/shard_map/ppermute | solution.py:89
  92.0 1.6 %collective-permute-start.31 = (bf16[384,384]{1,0:T(8,128)(2,1)S(1)}, bf16[384,384]{1,0:T(8,128)(2,1)S(1)}, u32[]{:S(2)}, u32[]{:S(2)}) collective-permute-start(bf16[384,384]{1,0:T(8,128)(2,1)S(1)} %constant_dynamic-update-slice_fusion), channel_id=1, source_target_pairs={{0,1},{1,0},{2,3},{3,2},{4,5},{5,4},{6,7},{7,6},{8,9},{9,8},{10,11... | collective-permute-start | bytes 884744 | tf_op jit(solution)/shard_map/ppermute | solution.py:20
  (2 other events, 8.4 us)

commit v4 on v3

--- a/solution.py
+++ b/solution.py
@@ -337,7 +337,7 @@
         tail = choose_frames((low, high), pl.ds(frame * per_frame, per_frame))
         edge = off[pl.ds(frame * columns, columns)]
         stack_rows(columns, odd, tail, jnp.zeros_like(edge), edge, stacked, frame)
-    for frame in range(partial.shape[0] // per_frame):
+    for frame in range(total.shape[0] // per_frame):
         here = pl.ds(frame * per_frame, per_frame)
         total[here] = taps_sum((0, 1), frame, stacked, packed, per_frame, partial[here])
 
@@ -366,7 +366,7 @@
 
 
 def first_body(
-    columns, low, high, packed, partial, gain, act, late, on, off, off_late
+    columns, low, high, packed, changed, partial, gain, act, late, on, off, off_late
 ):
     odd = is_odd()
     terms = partner_terms(columns, odd, (low, high), packed)
@@ -374,9 +374,7 @@
     frame_count = partial.shape[0] // per_frame
     for frame in range(frame_count - 1, -1, -1):
         here = pl.ds(frame * per_frame, per_frame)
-        total = partial[here]
-        if frame < 2:
-            total = total + terms[frame]
+        total = changed[here] + terms[frame] if frame < 2 else partial[here]
         total = shift_columns(total, columns)
         active = silu(root_norm(total, gain[...].reshape(1, -1))).astype(BF16)
         act[here] = active
@@ -389,7 +387,7 @@
             off_late[pl.ds(at * columns, columns)] = far
 
 
-def last_body(columns, token_total, low, high, packed, partial, *refs):
+def last_body(columns, token_total, low, high, packed, changed, partial, *refs):
     slope, hidden_t, latent_t, predicted, s_out, teacher, mine, yours, signals = refs[-9:]
     mids = refs[:-9]
     odd = is_odd()
@@ -398,9 +396,7 @@
     frame_count = partial.shape[0] // per_frame
     for frame in range(frame_count - 1, -1, -1):
         here = pl.ds(frame * per_frame, per_frame)
-        total = partial[here]
-        if frame < 2:
-            total = total + terms[frame]
+        total = changed[here] + terms[frame] if frame < 2 else partial[here]
         total = shift_columns(total, columns)
         taught = (mids[frame][...].astype(F32) + total).astype(BF16)
         teacher[here] = taught
@@ -507,7 +503,7 @@
         args = [*pair, corner, packed, partial]
         return call(
             functools.partial(earlier_body, columns),
-            shape(tokens, 3 * channels, F32), [VMEM] * len(args), VMEM,
+            shape(2 * per_frame, 3 * channels, F32), [VMEM] * len(args), VMEM,
             [stacked(2)], 9 * tokens * unit, 8 * tokens * channels, *args,
         )
 
@@ -524,8 +520,8 @@
     pair, corner, partner = from_earlier(late, off_late)
     groups = [(1, acts[frame]) for frame in range(early)] + [(2, late)]
     partial = own_part(groups, on, off, packed_first)
-    partial = earlier_part(pair, corner, packed_first, partial)
-    args = [*partner, packed_first, partial, conv_gain_second]
+    changed = earlier_part(pair, corner, packed_first, partial)
+    args = [*partner, packed_first, changed, partial, conv_gain_second]
     act, late, on, off, off_late = call(
         functools.partial(first_body, columns),
         [rows_of(frame_count), rows_of(2), edges_of(frame_count), edges_of(frame_count), edges_of(2)],
@@ -535,9 +531,9 @@
     pair, corner, partner = from_earlier(late, off_late)
     partial = own_part([(frame_count, act)], on, off, packed_second)
     token_total = tokens * lax.axis_size("dp") * lax.axis_size("tm") * lax.axis_size("space")
-    partial = earlier_part(pair, corner, packed_second, partial)
+    changed = earlier_part(pair, corner, packed_second, partial)
     args = [
-        *partner, packed_second, partial, *(mids[frame] for frame in range(frame_count)),
+        *partner, packed_second, changed, partial, *(mids[frame] for frame in range(frame_count)),
         slope, hidden_t, latent_t, predicted, student_out,
     ]
     teacher, mine, yours = call(

time: 95 us -> 94.9 us (level)
  transfers between devices with their start and end apart: 32 -> 32, of which waited for: 15 -> 15; matrix products, arithmetic and copies ran while one was open for 0% -> 0% of each run, Pallas kernels for 25% -> 24%
where the time goes in v4:
time: 94.9 us; the launch traced here: 94.8 us
  waiting for transfers between devices  35.9 us (38%)
  Pallas kernels  28.7 us (30%)
  starting transfers between devices  27.9 us (29%)
  other arithmetic  1.26 us (1%)
    pallas_call x11, Pallas kernels, call(): pl.pallas_call(body, out_shape=outs, in_specs=specs, out_specs=out_specs,...  28.7 us
    ppermute x18, waiting for transfers between devices, xor_permute(): return lax.ppermute(value, axis, [(i, i ^ mask) for i in range(count)])  18.3 us
    ppermute x18, starting transfers between devices, xor_permute(): return lax.ppermute(value, axis, [(i, i ^ mask) for i in range(count)])  11.9 us
    ppermute x4, waiting for transfers between devices, frame_pairings(): results.append(lax.ppermute(value, ('tm', 'space'), pairs))  9.34 us
    ppermute x6, waiting for transfers between devices, plane_permute(): return lax.ppermute(value, ('dp', 'space'), pairs)  8.22 us
    ppermute x6, starting transfers between devices, plane_permute(): return lax.ppermute(value, ('dp', 'space'), pairs)  7.11 us
    ppermute x4, starting transfers between devices, frame_pairings(): results.append(lax.ppermute(value, ('tm', 'space'), pairs))  4.21 us
    ppermute x2, starting transfers between devices, across_permute(): return lax.ppermute(value, ('dp', 'space'), pairs)  3.04 us
  transfers between devices with their start and end apart: 32, of which 15 were waited for; matrix products, arithmetic and copies ran while one was open for 0% of the time, Pallas kernels for 24%

profile of v4, /device:TPU:0, one launch (start us, length us, event | category | flops | bytes accessed | tf_op | source)
XLA Modules:
  0.0 94.8 jit_solution(2919153139706434046)
XLA Ops:
  0.6 1.4 %shard_map.139 = (bf16[624,384]{1,0:T(8,128)(2,1)S(1)}, bf16[624,384]{1,0:T(8,128)(2,1)S(1)}, bf16[208,384]{1,0:T(8,128)(2,1)S(1)}, bf16[208,384]{1,0:T(8,128)(2,1)S(1)}, bf16[208,384]{1,0:T(8,128)(2,1)S(1)}) custom-call(bf16[3,208,384]{2,1,0:T(8,128)(2,1)} %bitcast.2, f32[384]{0:T(512)} %gain_hbm.1), custom_call_target="tpu_custom_call" | custom-call | bytes 958464 | tf_op jit(solution)/shard_map/pallas_call | solution.py:143
  2.6 2.6 %collective-permute-start.3 = (bf16[208,384]{1,0:T(8,128)(2,1)S(1)}, bf16[208,384]{1,0:T(8,128)(2,1)S(1)}, u32[]{:S(2)}, u32[]{:S(2)}) collective-permute-start(bf16[208,384]{1,0:T(8,128)(2,1)S(1)} %get-tuple-element.48), channel_id=1, source_target_pairs={{0,2},{1,3},{2,0},{3,1},{4,6},{5,7},{6,4},{7,5},{8,10},{9,11},{10,... | collective-permute-start | bytes 479240 | tf_op jit(solution)/shard_map/ppermute | solution.py:20
  5.2 1.9 %collective-permute-start.10 = (bf16[208,384]{1,0:T(8,128)(2,1)S(1)}, bf16[208,384]{1,0:T(8,128)(2,1)S(1)}, u32[]{:S(2)}, u32[]{:S(2)}) collective-permute-start(bf16[208,384]{1,0:T(8,128)(2,1)S(1)} %get-tuple-element.55), channel_id=1, source_target_pairs={{0,2},{1,3},{2,0},{3,1},{4,6},{5,7},{6,4},{7,5},{8,10},{9,11},{10,... | collective-permute-start | bytes 479240 | tf_op jit(solution)/shard_map/ppermute | solution.py:20
  7.2 2.9 %collective-permute-done.3.refs_0_ = bf16[208,384]{1,0:T(8,128)(2,1)S(1)} collective-permute-done((bf16[208,384]{1,0:T(8,128)(2,1)S(1)}, bf16[208,384]{1,0:T(8,128)(2,1)S(1)}, u32[]{:S(2)}, u32[]{:S(2)}) %collective-permute-start.3) | collective-permute-done | bytes 159776 | tf_op jit(solution)/shard_map/ppermute | solution.py:20
  10.1 3.4 %collective-permute-done.refs_0_ = bf16[208,384]{1,0:T(8,128)(2,1)S(1)} collective-permute-done((bf16[208,384]{1,0:T(8,128)(2,1)S(1)}, bf16[208,384]{1,0:T(8,128)(2,1)S(1)}, u32[]{:S(2)}, u32[]{:S(2)}) %collective-permute-start) | collective-permute-done | bytes 159776 | tf_op jit(solution)/shard_map/ppermute | solution.py:20
  13.5 3.2 %collective-permute-done.10.refs_0_ = bf16[208,384]{1,0:T(8,128)(2,1)S(1)} collective-permute-done((bf16[208,384]{1,0:T(8,128)(2,1)S(1)}, bf16[208,384]{1,0:T(8,128)(2,1)S(1)}, u32[]{:S(2)}, u32[]{:S(2)}) %collective-permute-start.10) | collective-permute-done | bytes 159776 | tf_op jit(solution)/shard_map/ppermute | solution.py:20
  16.7 6.1 %shard_map.140 = (bf16[384,768]{1,0:T(8,128)(2,1)S(1)}, bf16[384,384]{1,0:T(8,128)(2,1)S(1)}, bf16[384,384]{1,0:T(8,128)(2,1)S(1)}, bf16[3456,1152]{1,0:T(8,128)...) custom-call(bf16[624,384]{1,0:T(8,128)(2,1)S(1)} %get-tuple-element., ...), custom_call_target="tpu_custom_call" | custom-call | flops 1288175616 | bytes 17694720 | tf_op jit(solution)/shard_map/pallas_call | solution.py:143
  22.9 1.6 %shard_map.141 = (bf16[208,384]{1,0:T(8,128)(2,1)S(1)}, bf16[208,384]{1,0:T(8,128)(2,1)S(1)}, bf16[104,384]{1,0:T(8,128)(2,1)S(1)}, bf16[104,384]{1,0:T(8,128)(2,1)S(1)}) custom-call(bf16[208,384]{1,0:T(8,128)(2,1)S(1)} %collective-permute-done.3.refs_0_, bf16[208,384]{1,0:T(8,128)(2,1)S(1)} %collective-permute-done.4.refs_1_, ...), custom_call_target="tpu_custom_call" | custom-call | flops 490733568 | bytes 319488 | tf_op jit(solution)/shard_map/pallas_call | solution.py:143
  24.4 1.6 %shard_map.142 = (bf16[416,384]{1,0:T(8,128)(2,1)S(1)}, bf16[208,384]{1,0:T(8,128)(2,1)S(1)}, bf16[208,384]{1,0:T(8,128)(2,1)S(1)}, bf16[208,384]{1,0:T(8,128)(2,1)S(1)}) custom-call(bf16[208,384]{1,0:T(8,128)(2,1)S(1)} %collective-permute-done.refs_0_, bf16[208,384]{1,0:T(8,128)(2,1)S(1)} %collective-permute-done.1.refs_1_, ...), custom_call_target="tpu_custom_call" | custom-call | flops 490733568 | bytes 319488 | tf_op jit(solution)/shard_map/pallas_call | solution.py:143
  26.0 1.9 %collective-permute-start.5 = (bf16[416,384]{1,0:T(8,128)(2,1)S(1)}, bf16[416,384]{1,0:T(8,128)(2,1)S(1)}, u32[]{:S(2)}, u32[]{:S(2)}) collective-permute-start(bf16[416,384]{1,0:T(8,128)(2,1)S(1)} %get-tuple-element.52.refs_1_), channel_id=1, source_target_pairs={{0,4},{1,5},{2,6},{3,7},{4,0},{5,1},{6,2},{7,3},{8,12},{9,13},{10,... | collective-permute-start | bytes 958472 | tf_op jit(solution)/shard_map/ppermute | solution.py:62
  28.1 1.6 %shard_map.143 = (bf16[208,384]{1,0:T(8,128)(2,1)S(1)}, bf16[208,384]{1,0:T(8,128)(2,1)S(1)}, bf16[312,384]{1,0:T(8,128)(2,1)S(1)}, bf16[312,384]{1,0:T(8,128)(2,1)S(1)}) custom-call(bf16[208,384]{1,0:T(8,128)(2,1)S(1)} %collective-permute-done.10.refs_0_, bf16[208,384]{1,0:T(8,128)(2,1)S(1)} %collective-permute-done.11.refs_1_, ...), custom_call_target="tpu_custom_call" | custom-call | flops 490733568 | bytes 319488 | tf_op jit(solution)/shard_map/pallas_call | solution.py:143
  29.7 1.6 %collective-permute-start.12 = (bf16[312,384]{1,0:T(8,128)(2,1)S(1)}, bf16[312,384]{1,0:T(8,128)(2,1)S(1)}, u32[]{:S(2)}, u32[]{:S(2)}) collective-permute-start(bf16[312,384]{1,0:T(8,128)(2,1)S(1)} %get-tuple-element.58), channel_id=1, source_target_pairs={{0,16},{1,2},{2,1},{3,19},{16,0},{17,18},{18,17},{19,3},{4,20},{5,... | collective-permute-start | bytes 718856 | tf_op jit(solution)/shard_map/ppermute | solution.py:48
  32.2 3.9 %collective-permute-done.5.low = bf16[416,384]{1,0:T(8,128)(2,1)S(1)} collective-permute-done((bf16[416,384]{1,0:T(8,128)(2,1)S(1)}, bf16[416,384]{1,0:T(8,128)(2,1)S(1)}, u32[]{:S(2)}, u32[]{:S(2)}) %collective-permute-start.5) | collective-permute-done | bytes 319520 | tf_op jit(solution)/shard_map/ppermute | solution.py:62
  37.1 4.1 %shard_map.144.partial = f32[624,1152]{1,0:T(8,128)S(1)} custom-call(bf16[208,384]{1,0:T(8,128)(2,1)S(1)} %get-tuple-element.57.refs_0_, bf16[416,384]{1,0:T(8,128)(2,1)S(1)} %get-tuple-element.52.refs_1_, bf16[312,384]{1,0:T(8,128)(2,1)S(1)} %collective-permute-done.12.refs_2_, bf16[312,384]{1,0:T(8,128)(2,1)S(1)} %collective-permute-done.13.refs_3_, ...), custom_call_target="tpu_custom_call" | custom-call | flops 3312451584 | bytes 1916928 | tf_op jit(solution)/shard_map/pallas_call | solution.py:143
  41.2 2.1 %shard_map.145.changed = f32[416,1152]{1,0:T(8,128)S(1)} custom-call(bf16[416,384]{1,0:T(8,128)(2,1)S(1)} %collective-permute-done.5.low, bf16[416,384]{1,0:T(8,128)(2,1)S(1)} %collective-permute-done.7.high, bf16[208,384]{1,0:T(8,128)(2,1)S(1)} %collective-permute-done.9.off, bf16[3456,1152]{1,0:T(8,128)(2,1)S(1)} %get-tuple-element.53.refs_4_.packed, ...), custom_call_target="tpu_custom_call" | custom-call | flops 1656225792 | bytes 1916928 | tf_op jit(solution)/shard_map/pallas_call | solution.py:143
  44.7 1.9 %collective-permute-start.14 = (bf16[416,384]{1,0:T(8,128)(2,1)S(1)}, bf16[416,384]{1,0:T(8,128)(2,1)S(1)}, u32[]{:S(2)}, u32[]{:S(2)}) collective-permute-start(bf16[416,384]{1,0:T(8,128)(2,1)S(1)} %get-tuple-element.60), channel_id=1, source_target_pairs={{0,4},{1,5},{2,6},{3,7},{4,0},{5,1},{6,2},{7,3},{8,12},{9,13},{10,... | collective-permute-start | bytes 958472 | tf_op jit(solution)/shard_map/ppermute | solution.py:62
  46.9 1.5 %collective-permute-start.19 = (bf16[312,384]{1,0:T(8,128)(2,1)S(1)}, bf16[312,384]{1,0:T(8,128)(2,1)S(1)}, u32[]{:S(2)}, u32[]{:S(2)}) collective-permute-start(bf16[312,384]{1,0:T(8,128)(2,1)S(1)} %get-tuple-element.64), channel_id=1, source_target_pairs={{0,16},{1,2},{2,1},{3,19},{16,0},{17,18},{18,17},{19,3},{4,20},{5,... | collective-permute-start | bytes 718856 | tf_op jit(solution)/shard_map/ppermute | solution.py:48
  49.4 5.5 %collective-permute-done.14.low = bf16[416,384]{1,0:T(8,128)(2,1)S(1)} collective-permute-done((bf16[416,384]{1,0:T(8,128)(2,1)S(1)}, bf16[416,384]{1,0:T(8,128)(2,1)S(1)}, u32[]{:S(2)}, u32[]{:S(2)}) %collective-permute-start.14) | collective-permute-done | bytes 319520 | tf_op jit(solution)/shard_map/ppermute | solution.py:62
  55.4 4.0 %shard_map.147.partial = f32[624,1152]{1,0:T(8,128)S(1)} custom-call(bf16[624,384]{1,0:T(8,128)(2,1)S(1)} %get-tuple-element.63.refs_0_, bf16[312,384]{1,0:T(8,128)(2,1)S(1)} %collective-permute-done.19.refs_1_, bf16[312,384]{1,0:T(8,128)(2,1)S(1)} %collective-permute-done.20.refs_2_, bf16[3456,1152]{1,0:T(8,128)(2,1)S(1)} %get-tuple-element.61.refs_3_.packed), custom_call_target="tpu_custom_call" | custom-call | flops 3312451584 | bytes 1916928 | tf_op jit(solution)/shard_map/pallas_call | solution.py:143
  59.4 2.2 %shard_map.148.changed = f32[416,1152]{1,0:T(8,128)S(1)} custom-call(bf16[416,384]{1,0:T(8,128)(2,1)S(1)} %collective-permute-done.14.low, bf16[416,384]{1,0:T(8,128)(2,1)S(1)} %collective-permute-done.16.high, bf16[208,384]{1,0:T(8,128)(2,1)S(1)} %collective-permute-done.18.off, bf16[3456,1152]{1,0:T(8,128)(2,1)S(1)} %get-tuple-element.61.refs_3_.packed, ...), custom_call_target="tpu_custom_call" | custom-call | flops 1656225792 | bytes 1916928 | tf_op jit(solution)/shard_map/pallas_call | solution.py:143
  61.6 2.8 %shard_map.149 = (bf16[624,384]{1,0:T(8,128)(2,1)}, f32[384,384]{1,0:T(8,128)S(1)}, bf16[384,384]{1,0:T(8,128)(2,1)S(1)}) custom-call(bf16[416,384]{1,0:T(8,128)(2,1)S(1)} %collective-permute-done.15.low, bf16[416,384]{1,0:T(8,128)(2,1)S(1)} %collective-permute-done.17.high, bf16[3456,1152]{1,0:T(8,128)(2,1)S(1)} %get-tuple-element.61.refs_3_.packed, ...), custom_call_target="tpu_custom_call" | custom-call | flops 2208301056 | bytes 1916928 | tf_op jit(solution)/shard_map/pallas_call | solution.py:143
  64.4 1.6 %collective-permute-done.21 = bf16[384,384]{1,0:T(8,128)(2,1)S(1)} collective-permute-done((bf16[384,384]{1,0:T(8,128)(2,1)S(1)}, bf16[384,384]{1,0:T(8,128)(2,1)S(1)}, u32[]{:S(2)}, u32[]{:S(2)}) %collective-permute-start.21) | collective-permute-done | bytes 294944 | tf_op jit(solution)/shard_map/ppermute | solution.py:20
  66.1 1.6 %collective-permute-start.22 = (bf16[96,384]{1,0:T(8,128)(2,1)S(1)}, bf16[96,384]{1,0:T(8,128)(2,1)S(1)}, u32[]{:S(2)}, u32[]{:S(2)}) collective-permute-start(bf16[96,384]{1,0:T(8,128)(2,1)S(1)} %get-tuple-element.83), channel_id=1, source_target_pairs={{0,2},{1,3},{2,0},{3,1},{16,18},{17,19},{18,16},{19,17},{4,6},{5,7... | collective-permute-start | bytes 221192 | tf_op jit(solution)/shard_map/ppermute | solution.py:89
  67.7 1.5 %collective-permute-start.23 = (bf16[96,384]{1,0:T(8,128)(2,1)S(1)}, bf16[96,384]{1,0:T(8,128)(2,1)S(1)}, u32[]{:S(2)}, u32[]{:S(2)}) collective-permute-start(bf16[96,384]{1,0:T(8,128)(2,1)S(1)} %get-tuple-element.85), channel_id=1, source_target_pairs={{0,16},{1,17},{2,18},{3,19},{16,0},{17,1},{18,2},{19,3},{4,20},{5,... | collective-permute-start | bytes 221192 | tf_op jit(solution)/shard_map/ppermute | solution.py:89
  70.5 2.3 %collective-permute-done.23 = bf16[96,384]{1,0:T(8,128)(2,1)S(1)} collective-permute-done((bf16[96,384]{1,0:T(8,128)(2,1)S(1)}, bf16[96,384]{1,0:T(8,128)(2,1)S(1)}, u32[]{:S(2)}, u32[]{:S(2)}) %collective-permute-start.23) | collective-permute-done | bytes 73760 | tf_op jit(solution)/shard_map/ppermute | solution.py:89
  72.8 1.6 %collective-permute-done.24 = bf16[96,384]{1,0:T(8,128)(2,1)S(1)} collective-permute-done((bf16[96,384]{1,0:T(8,128)(2,1)S(1)}, bf16[96,384]{1,0:T(8,128)(2,1)S(1)}, u32[]{:S(2)}, u32[]{:S(2)}) %collective-permute-start.24) | collective-permute-done | bytes 73760 | tf_op jit(solution)/shard_map/ppermute | solution.py:89
  74.5 1.8 %collective-permute-start.25 = (bf16[96,384]{1,0:T(8,128)(2,1)S(1)}, bf16[96,384]{1,0:T(8,128)(2,1)S(1)}, u32[]{:S(2)}, u32[]{:S(2)}) collective-permute-start(bf16[96,384]{1,0:T(8,128)(2,1)S(1)} %add_convert_fusion.1), channel_id=1, source_target_pairs={{0,4},{4,0},{8,12},{12,8},{1,5},{5,1},{9,13},{13,9},{2,6},{6,2},{1... | collective-permute-start | bytes 221192 | tf_op jit(solution)/shard_map/ppermute | solution.py:20
  76.3 1.9 %collective-permute-start.26 = (bf16[96,384]{1,0:T(8,128)(2,1)S(1)}, bf16[96,384]{1,0:T(8,128)(2,1)S(1)}, u32[]{:S(2)}, u32[]{:S(2)}) collective-permute-start(bf16[96,384]{1,0:T(8,128)(2,1)S(1)} %add_convert_fusion.1), channel_id=1, source_target_pairs={{0,8},{4,12},{8,0},{12,4},{1,9},{5,13},{9,1},{13,5},{2,10},{6,14},... | collective-permute-start | bytes 221192 | tf_op jit(solution)/shard_map/ppermute | solution.py:20
  79.7 5.2 %collective-permute-done.26 = bf16[96,384]{1,0:T(8,128)(2,1)S(1)} collective-permute-done((bf16[96,384]{1,0:T(8,128)(2,1)S(1)}, bf16[96,384]{1,0:T(8,128)(2,1)S(1)}, u32[]{:S(2)}, u32[]{:S(2)}) %collective-permute-start.26) | collective-permute-done | bytes 73760 | tf_op jit(solution)/shard_map/ppermute | solution.py:20
  86.8 1.8 %collective-permute-start.30 = (bf16[96,384]{1,0:T(8,128)(2,1)S(1)}, bf16[96,384]{1,0:T(8,128)(2,1)S(1)}, u32[]{:S(2)}, u32[]{:S(2)}) collective-permute-start(bf16[96,384]{1,0:T(8,128)(2,1)S(1)} %get-tuple-element.78), channel_id=1, source_target_pairs={{0,18},{1,19},{2,16},{3,17},{16,2},{17,3},{18,0},{19,1},{4,22},{5,... | collective-permute-start | bytes 221192 | tf_op jit(solution)/shard_map/ppermute | solution.py:89
  90.5 1.6 %collective-permute-done.30 = bf16[96,384]{1,0:T(8,128)(2,1)S(1)} collective-permute-done((bf16[96,384]{1,0:T(8,128)(2,1)S(1)}, bf16[96,384]{1,0:T(8,128)(2,1)S(1)}, u32[]{:S(2)}, u32[]{:S(2)}) %collective-permute-start.30) | collective-permute-done | bytes 73760 | tf_op jit(solution)/shard_map/ppermute | solution.py:89
  92.1 1.6 %collective-permute-done.31 = bf16[384,384]{1,0:T(8,128)(2,1)S(1)} collective-permute-done((bf16[384,384]{1,0:T(8,128)(2,1)S(1)}, bf16[384,384]{1,0:T(8,128)(2,1)S(1)}, u32[]{:S(2)}, u32[]{:S(2)}) %collective-permute-start.31) | collective-permute-done | bytes 294944 | tf_op jit(solution)/shard_map/ppermute | solution.py:20
  (56 shorter events, 14.0 us)
Async XLA Ops:
  2.0 14.7 %collective-permute-start.2 = (bf16[624,384]{1,0:T(8,128)(2,1)S(1)}, bf16[624,384]{1,0:T(8,128)(2,1)S(1)}, u32[]{:S(2)}, u32[]{:S(2)}) collective-permute-start(bf16[624,384]{1,0:T(8,128)(2,1)S(1)} %get-tuple-element.42.normed), channel_id=1, source_target_pairs={{0,1},{1,0},{2,3},{3,2},{4,5},{5,4},{6,7},{7,6},{8,9},{9,8},{10,11... | collective-permute-start | bytes 1437704 | tf_op jit(solution)/shard_map/ppermute | solution.py:20
  2.6 7.5 %collective-permute-start.3 = (bf16[208,384]{1,0:T(8,128)(2,1)S(1)}, bf16[208,384]{1,0:T(8,128)(2,1)S(1)}, u32[]{:S(2)}, u32[]{:S(2)}) collective-permute-start(bf16[208,384]{1,0:T(8,128)(2,1)S(1)} %get-tuple-element.48), channel_id=1, source_target_pairs={{0,2},{1,3},{2,0},{3,1},{4,6},{5,7},{6,4},{7,5},{8,10},{9,11},{10,... | collective-permute-start | bytes 479240 | tf_op jit(solution)/shard_map/ppermute | solution.py:20
  5.1 8.4 %collective-permute-start = (bf16[208,384]{1,0:T(8,128)(2,1)S(1)}, bf16[208,384]{1,0:T(8,128)(2,1)S(1)}, u32[]{:S(2)}, u32[]{:S(2)}) collective-permute-start(bf16[208,384]{1,0:T(8,128)(2,1)S(1)} %get-tuple-element.40), channel_id=1, source_target_pairs={{0,2},{1,3},{2,0},{3,1},{4,6},{5,7},{6,4},{7,5},{8,10},{9,11},{10,... | collective-permute-start | bytes 479240 | tf_op jit(solution)/shard_map/ppermute | solution.py:20
  5.2 11.5 %collective-permute-start.10 = (bf16[208,384]{1,0:T(8,128)(2,1)S(1)}, bf16[208,384]{1,0:T(8,128)(2,1)S(1)}, u32[]{:S(2)}, u32[]{:S(2)}) collective-permute-start(bf16[208,384]{1,0:T(8,128)(2,1)S(1)} %get-tuple-element.55), channel_id=1, source_target_pairs={{0,2},{1,3},{2,0},{3,1},{4,6},{5,7},{6,4},{7,5},{8,10},{9,11},{10,... | collective-permute-start | bytes 479240 | tf_op jit(solution)/shard_map/ppermute | solution.py:20
  10.1 12.8 %collective-permute-start.4 = (bf16[208,384]{1,0:T(8,128)(2,1)S(1)}, bf16[208,384]{1,0:T(8,128)(2,1)S(1)}, u32[]{:S(2)}, u32[]{:S(2)}) collective-permute-start(bf16[208,384]{1,0:T(8,128)(2,1)S(1)} %collective-permute-done.3.refs_0_), channel_id=1, source_target_pairs={{0,1},{1,0},{2,3},{3,2},{4,5},{5,4},{6,7},{7,6},{8,9},{9,8},{10,11... | collective-permute-start | bytes 479240 | tf_op jit(solution)/shard_map/ppermute | solution.py:20
  13.5 10.9 %collective-permute-start.1 = (bf16[208,384]{1,0:T(8,128)(2,1)S(1)}, bf16[208,384]{1,0:T(8,128)(2,1)S(1)}, u32[]{:S(2)}, u32[]{:S(2)}) collective-permute-start(bf16[208,384]{1,0:T(8,128)(2,1)S(1)} %collective-permute-done.refs_0_), channel_id=1, source_target_pairs={{0,1},{1,0},{2,3},{3,2},{4,5},{5,4},{6,7},{7,6},{8,9},{9,8},{10,11... | collective-permute-start | bytes 479240 | tf_op jit(solution)/shard_map/ppermute | solution.py:20
  16.7 11.4 %collective-permute-start.11 = (bf16[208,384]{1,0:T(8,128)(2,1)S(1)}, bf16[208,384]{1,0:T(8,128)(2,1)S(1)}, u32[]{:S(2)}, u32[]{:S(2)}) collective-permute-start(bf16[208,384]{1,0:T(8,128)(2,1)S(1)} %collective-permute-done.10.refs_0_), channel_id=1, source_target_pairs={{0,1},{1,0},{2,3},{3,2},{4,5},{5,4},{6,7},{7,6},{8,9},{9,8},{10,11... | collective-permute-start | bytes 479240 | tf_op jit(solution)/shard_map/ppermute | solution.py:20
  26.0 10.1 %collective-permute-start.5 = (bf16[416,384]{1,0:T(8,128)(2,1)S(1)}, bf16[416,384]{1,0:T(8,128)(2,1)S(1)}, u32[]{:S(2)}, u32[]{:S(2)}) collective-permute-start(bf16[416,384]{1,0:T(8,128)(2,1)S(1)} %get-tuple-element.52.refs_1_), channel_id=1, source_target_pairs={{0,4},{1,5},{2,6},{3,7},{4,0},{5,1},{6,2},{7,3},{8,12},{9,13},{10,... | collective-permute-start | bytes 958472 | tf_op jit(solution)/shard_map/ppermute | solution.py:62
  27.9 9.2 %collective-permute-start.7 = (bf16[416,384]{1,0:T(8,128)(2,1)S(1)}, bf16[416,384]{1,0:T(8,128)(2,1)S(1)}, u32[]{:S(2)}, u32[]{:S(2)}) collective-permute-start(bf16[416,384]{1,0:T(8,128)(2,1)S(1)} %get-tuple-element.52.refs_1_), channel_id=1, source_target_pairs={{0,1},{1,0},{2,3},{3,2},{4,8},{5,9},{6,10},{7,11},{8,4},{9,5},{10,... | collective-permute-start | bytes 958472 | tf_op jit(solution)/shard_map/ppermute | solution.py:62
  29.7 7.5 %collective-permute-start.12 = (bf16[312,384]{1,0:T(8,128)(2,1)S(1)}, bf16[312,384]{1,0:T(8,128)(2,1)S(1)}, u32[]{:S(2)}, u32[]{:S(2)}) collective-permute-start(bf16[312,384]{1,0:T(8,128)(2,1)S(1)} %get-tuple-element.58), channel_id=1, source_target_pairs={{0,16},{1,2},{2,1},{3,19},{16,0},{17,18},{18,17},{19,3},{4,20},{5,... | collective-permute-start | bytes 718856 | tf_op jit(solution)/shard_map/ppermute | solution.py:48
  31.2 5.9 %collective-permute-start.13 = (bf16[312,384]{1,0:T(8,128)(2,1)S(1)}, bf16[312,384]{1,0:T(8,128)(2,1)S(1)}, u32[]{:S(2)}, u32[]{:S(2)}) collective-permute-start(bf16[312,384]{1,0:T(8,128)(2,1)S(1)} %get-tuple-element.59), channel_id=1, source_target_pairs={{0,1},{1,0},{2,3},{3,2},{4,5},{5,4},{6,7},{7,6},{8,9},{9,8},{10,11... | collective-permute-start | bytes 718856 | tf_op jit(solution)/shard_map/ppermute | solution.py:20
  31.4 9.9 %collective-permute-start.9 = (bf16[208,384]{1,0:T(8,128)(2,1)S(1)}, bf16[208,384]{1,0:T(8,128)(2,1)S(1)}, u32[]{:S(2)}, u32[]{:S(2)}) collective-permute-start(bf16[208,384]{1,0:T(8,128)(2,1)S(1)} %get-tuple-element.54.refs_10_), channel_id=1, source_target_pairs={{1,6},{2,5},{5,10},{6,9},{9,14},{10,13},{17,22},{18,21},{21,26},{2... | collective-permute-start | bytes 479240 | tf_op jit(solution)/shard_map/ppermute | solution.py:73
  36.1 7.3 %collective-permute-start.6 = (bf16[416,384]{1,0:T(8,128)(2,1)S(1)}, bf16[416,384]{1,0:T(8,128)(2,1)S(1)}, u32[]{:S(2)}, u32[]{:S(2)}) collective-permute-start(bf16[416,384]{1,0:T(8,128)(2,1)S(1)} %collective-permute-done.5.low), channel_id=1, source_target_pairs={{0,1},{1,0},{2,3},{3,2},{4,5},{5,4},{6,7},{7,6},{8,9},{9,8},{10,11... | collective-permute-start | bytes 958472 | tf_op jit(solution)/shard_map/ppermute | solution.py:20
  37.1 6.3 %collective-permute-start.8 = (bf16[416,384]{1,0:T(8,128)(2,1)S(1)}, bf16[416,384]{1,0:T(8,128)(2,1)S(1)}, u32[]{:S(2)}, u32[]{:S(2)}) collective-permute-start(bf16[416,384]{1,0:T(8,128)(2,1)S(1)} %collective-permute-done.7.high), channel_id=1, source_target_pairs={{0,1},{1,0},{2,3},{3,2},{4,5},{5,4},{6,7},{7,6},{8,9},{9,8},{10,11... | collective-permute-start | bytes 958472 | tf_op jit(solution)/shard_map/ppermute | solution.py:20
  44.7 10.1 %collective-permute-start.14 = (bf16[416,384]{1,0:T(8,128)(2,1)S(1)}, bf16[416,384]{1,0:T(8,128)(2,1)S(1)}, u32[]{:S(2)}, u32[]{:S(2)}) collective-permute-start(bf16[416,384]{1,0:T(8,128)(2,1)S(1)} %get-tuple-element.60), channel_id=1, source_target_pairs={{0,4},{1,5},{2,6},{3,7},{4,0},{5,1},{6,2},{7,3},{8,12},{9,13},{10,... | collective-permute-start | bytes 958472 | tf_op jit(solution)/shard_map/ppermute | solution.py:62
  46.6 8.2 %collective-permute-start.16 = (bf16[416,384]{1,0:T(8,128)(2,1)S(1)}, bf16[416,384]{1,0:T(8,128)(2,1)S(1)}, u32[]{:S(2)}, u32[]{:S(2)}) collective-permute-start(bf16[416,384]{1,0:T(8,128)(2,1)S(1)} %get-tuple-element.60), channel_id=1, source_target_pairs={{0,1},{1,0},{2,3},{3,2},{4,8},{5,9},{6,10},{7,11},{8,4},{9,5},{10,... | collective-permute-start | bytes 958472 | tf_op jit(solution)/shard_map/ppermute | solution.py:62
  46.9 8.5 %collective-permute-start.19 = (bf16[312,384]{1,0:T(8,128)(2,1)S(1)}, bf16[312,384]{1,0:T(8,128)(2,1)S(1)}, u32[]{:S(2)}, u32[]{:S(2)}) collective-permute-start(bf16[312,384]{1,0:T(8,128)(2,1)S(1)} %get-tuple-element.64), channel_id=1, source_target_pairs={{0,16},{1,2},{2,1},{3,19},{16,0},{17,18},{18,17},{19,3},{4,20},{5,... | collective-permute-start | bytes 718856 | tf_op jit(solution)/shard_map/ppermute | solution.py:48
  48.3 7.0 %collective-permute-start.20 = (bf16[312,384]{1,0:T(8,128)(2,1)S(1)}, bf16[312,384]{1,0:T(8,128)(2,1)S(1)}, u32[]{:S(2)}, u32[]{:S(2)}) collective-permute-start(bf16[312,384]{1,0:T(8,128)(2,1)S(1)} %get-tuple-element.65), channel_id=1, source_target_pairs={{0,1},{1,0},{2,3},{3,2},{4,5},{5,4},{6,7},{7,6},{8,9},{9,8},{10,11... | collective-permute-start | bytes 718856 | tf_op jit(solution)/shard_map/ppermute | solution.py:20
  48.5 10.9 %collective-permute-start.18 = (bf16[208,384]{1,0:T(8,128)(2,1)S(1)}, bf16[208,384]{1,0:T(8,128)(2,1)S(1)}, u32[]{:S(2)}, u32[]{:S(2)}) collective-permute-start(bf16[208,384]{1,0:T(8,128)(2,1)S(1)} %get-tuple-element.62), channel_id=1, source_target_pairs={{1,6},{2,5},{5,10},{6,9},{9,14},{10,13},{17,22},{18,21},{21,26},{2... | collective-permute-start | bytes 479240 | tf_op jit(solution)/shard_map/ppermute | solution.py:73
  54.8 6.8 %collective-permute-start.15 = (bf16[416,384]{1,0:T(8,128)(2,1)S(1)}, bf16[416,384]{1,0:T(8,128)(2,1)S(1)}, u32[]{:S(2)}, u32[]{:S(2)}) collective-permute-start(bf16[416,384]{1,0:T(8,128)(2,1)S(1)} %collective-permute-done.14.low), channel_id=1, source_target_pairs={{0,1},{1,0},{2,3},{3,2},{4,5},{5,4},{6,7},{7,6},{8,9},{9,8},{10,11... | collective-permute-start | bytes 958472 | tf_op jit(solution)/shard_map/ppermute | solution.py:20
  54.8 6.8 %collective-permute-start.17 = (bf16[416,384]{1,0:T(8,128)(2,1)S(1)}, bf16[416,384]{1,0:T(8,128)(2,1)S(1)}, u32[]{:S(2)}, u32[]{:S(2)}) collective-permute-start(bf16[416,384]{1,0:T(8,128)(2,1)S(1)} %collective-permute-done.16.high), channel_id=1, source_target_pairs={{0,1},{1,0},{2,3},{3,2},{4,5},{5,4},{6,7},{7,6},{8,9},{9,8},{10,11... | collective-permute-start | bytes 958472 | tf_op jit(solution)/shard_map/ppermute | solution.py:20
  64.4 1.6 %collective-permute-start.21 = (bf16[384,384]{1,0:T(8,128)(2,1)S(1)}, bf16[384,384]{1,0:T(8,128)(2,1)S(1)}, u32[]{:S(2)}, u32[]{:S(2)}) collective-permute-start(bf16[384,384]{1,0:T(8,128)(2,1)S(1)} %get-tuple-element.76), channel_id=1, source_target_pairs={{0,1},{1,0},{2,3},{3,2},{4,5},{5,4},{6,7},{7,6},{8,9},{9,8},{10,11... | collective-permute-start | bytes 884744 | tf_op jit(solution)/shard_map/ppermute | solution.py:20
  66.1 4.4 %collective-permute-start.22 = (bf16[96,384]{1,0:T(8,128)(2,1)S(1)}, bf16[96,384]{1,0:T(8,128)(2,1)S(1)}, u32[]{:S(2)}, u32[]{:S(2)}) collective-permute-start(bf16[96,384]{1,0:T(8,128)(2,1)S(1)} %get-tuple-element.83), channel_id=1, source_target_pairs={{0,2},{1,3},{2,0},{3,1},{16,18},{17,19},{18,16},{19,17},{4,6},{5,7... | collective-permute-start | bytes 221192 | tf_op jit(solution)/shard_map/ppermute | solution.py:89
  67.7 5.1 %collective-permute-start.23 = (bf16[96,384]{1,0:T(8,128)(2,1)S(1)}, bf16[96,384]{1,0:T(8,128)(2,1)S(1)}, u32[]{:S(2)}, u32[]{:S(2)}) collective-permute-start(bf16[96,384]{1,0:T(8,128)(2,1)S(1)} %get-tuple-element.85), channel_id=1, source_target_pairs={{0,16},{1,17},{2,18},{3,19},{16,0},{17,1},{18,2},{19,3},{4,20},{5,... | collective-permute-start | bytes 221192 | tf_op jit(solution)/shard_map/ppermute | solution.py:89
  69.2 5.3 %collective-permute-start.24 = (bf16[96,384]{1,0:T(8,128)(2,1)S(1)}, bf16[96,384]{1,0:T(8,128)(2,1)S(1)}, u32[]{:S(2)}, u32[]{:S(2)}) collective-permute-start(bf16[96,384]{1,0:T(8,128)(2,1)S(1)} %get-tuple-element.84), channel_id=1, source_target_pairs={{0,18},{1,19},{2,16},{3,17},{16,2},{17,3},{18,0},{19,1},{4,22},{5,... | collective-permute-start | bytes 221192 | tf_op jit(solution)/shard_map/ppermute | solution.py:89
  74.5 5.2 %collective-permute-start.25 = (bf16[96,384]{1,0:T(8,128)(2,1)S(1)}, bf16[96,384]{1,0:T(8,128)(2,1)S(1)}, u32[]{:S(2)}, u32[]{:S(2)}) collective-permute-start(bf16[96,384]{1,0:T(8,128)(2,1)S(1)} %add_convert_fusion.1), channel_id=1, source_target_pairs={{0,4},{4,0},{8,12},{12,8},{1,5},{5,1},{9,13},{13,9},{2,6},{6,2},{1... | collective-permute-start | bytes 221192 | tf_op jit(solution)/shard_map/ppermute | solution.py:20
  76.3 8.6 %collective-permute-start.26 = (bf16[96,384]{1,0:T(8,128)(2,1)S(1)}, bf16[96,384]{1,0:T(8,128)(2,1)S(1)}, u32[]{:S(2)}, u32[]{:S(2)}) collective-permute-start(bf16[96,384]{1,0:T(8,128)(2,1)S(1)} %add_convert_fusion.1), channel_id=1, source_target_pairs={{0,8},{4,12},{8,0},{12,4},{1,9},{5,13},{9,1},{13,5},{2,10},{6,14},... | collective-permute-start | bytes 221192 | tf_op jit(solution)/shard_map/ppermute | solution.py:20
  78.2 6.7 %collective-permute-start.27 = (bf16[96,384]{1,0:T(8,128)(2,1)S(1)}, bf16[96,384]{1,0:T(8,128)(2,1)S(1)}, u32[]{:S(2)}, u32[]{:S(2)}) collective-permute-start(bf16[96,384]{1,0:T(8,128)(2,1)S(1)} %add_convert_fusion.1), channel_id=1, source_target_pairs={{0,12},{4,8},{8,4},{12,0},{1,13},{5,9},{9,5},{13,1},{2,14},{6,10},... | collective-permute-start | bytes 221192 | tf_op jit(solution)/shard_map/ppermute | solution.py:20
  85.0 4.4 %collective-permute-start.28 = (bf16[96,384]{1,0:T(8,128)(2,1)S(1)}, bf16[96,384]{1,0:T(8,128)(2,1)S(1)}, u32[]{:S(2)}, u32[]{:S(2)}) collective-permute-start(bf16[96,384]{1,0:T(8,128)(2,1)S(1)} %get-tuple-element.78), channel_id=1, source_target_pairs={{0,2},{1,3},{2,0},{3,1},{16,18},{17,19},{18,16},{19,17},{4,6},{5,7... | collective-permute-start | bytes 221192 | tf_op jit(solution)/shard_map/ppermute | solution.py:89
  86.1 4.4 %collective-permute-start.29 = (bf16[96,384]{1,0:T(8,128)(2,1)S(1)}, bf16[96,384]{1,0:T(8,128)(2,1)S(1)}, u32[]{:S(2)}, u32[]{:S(2)}) collective-permute-start(bf16[96,384]{1,0:T(8,128)(2,1)S(1)} %get-tuple-element.78), channel_id=1, source_target_pairs={{0,16},{1,17},{2,18},{3,19},{16,0},{17,1},{18,2},{19,3},{4,20},{5,... | collective-permute-start | bytes 221192 | tf_op jit(solution)/shard_map/ppermute | solution.py:89
  86.8 5.3 %collective-permute-start.30 = (bf16[96,384]{1,0:T(8,128)(2,1)S(1)}, bf16[96,384]{1,0:T(8,128)(2,1)S(1)}, u32[]{:S(2)}, u32[]{:S(2)}) collective-permute-start(bf16[96,384]{1,0:T(8,128)(2,1)S(1)} %get-tuple-element.78), channel_id=1, source_target_pairs={{0,18},{1,19},{2,16},{3,17},{16,2},{17,3},{18,0},{19,1},{4,22},{5,... | collective-permute-start | bytes 221192 | tf_op jit(solution)/shard_map/ppermute | solution.py:89
  92.0 1.6 %collective-permute-start.31 = (bf16[384,384]{1,0:T(8,128)(2,1)S(1)}, bf16[384,384]{1,0:T(8,128)(2,1)S(1)}, u32[]{:S(2)}, u32[]{:S(2)}) collective-permute-start(bf16[384,384]{1,0:T(8,128)(2,1)S(1)} %constant_dynamic-update-slice_fusion), channel_id=1, source_target_pairs={{0,1},{1,0},{2,3},{3,2},{4,5},{5,4},{6,7},{7,6},{8,9},{9,8},{10,11... | collective-permute-start | bytes 884744 | tf_op jit(solution)/shard_map/ppermute | solution.py:20
  (2 other events, 8.3 us)

commit v5 on v4

--- a/solution.py
+++ b/solution.py
@@ -201,9 +201,23 @@
         frames[frame][...] = result
 
 
+def tap_copies(taps, packed, sem):
+    channels = taps.shape[3]
+    return [
+        pltpu.make_async_copy(
+            taps.at[t, r, c],
+            packed.at[pl.ds((3 * t + r) * channels, channels), pl.ds(c * channels, channels)],
+            sem,
+        )
+        for t in range(3)
+        for r in range(3)
+        for c in range(3)
+    ]
+
+
 def prepare_body(
-    latent, normed, partner, query_hbm, key_hbm, value_hbm, out_hbm, in_hbm, back_hbm, first_hbm, second_hbm,
-    w_both, w_out, s_out, first, second, slope, hidden_t, latent_t, predicted,
+    latent, normed, partner, query_hbm, key_hbm, value_hbm, out_hbm, in_hbm, back_hbm, first_hbm,
+    w_both, w_out, s_out, first, slope, hidden_t, latent_t, predicted,
     queries, own_both, partner_both, w_query, s_in, sems,
 ):
     channels = latent.shape[1]
@@ -215,15 +229,7 @@
         pltpu.make_async_copy(back_hbm, s_out, sems.at[1]),
     ]
     rest = [pltpu.make_async_copy(out_hbm, w_out, sems.at[5])]
-    for at, (taps, packed) in enumerate(((first_hbm, first), (second_hbm, second))):
-        for t in range(3):
-            for r in range(3):
-                for c in range(3):
-                    row = (3 * t + r) * channels
-                    block = packed.at[pl.ds(row, channels), pl.ds(c * channels, channels)]
-                    rest.append(
-                        pltpu.make_async_copy(taps.at[t, r, c], block, sems.at[6 + 3 * at + t])
-                    )
+    rest += tap_copies(first_hbm, first, sems.at[6])
     for copy in early + rest:
         copy.start()
     tokens = latent[...]
@@ -309,14 +315,22 @@
     )
 
 
-def own_body(groups, columns, *refs):
+def own_body(groups, columns, fetch, *refs):
     odd = is_odd()
     far = has_across()
-    off, on, packed, partial, stacked = refs[-5:]
+    own_refs, refs = refs[: len(groups)], refs[len(groups) :]
+    copies = []
+    if fetch:
+        off, on, packed, taps, partial, fetched, stacked, sem = refs
+        copies = tap_copies(taps, fetched, sem.at[0])
+    else:
+        off, on, packed, partial, stacked = refs
+    for copy in copies:
+        copy.start()
     frame_count = sum(groups)
     per_frame = partial.shape[0] // frame_count
     at = 0
-    for own, frames in zip(refs[:-5], groups, strict=True):
+    for own, frames in zip(own_refs, groups, strict=True):
         for frame in range(frames):
             edge = pl.ds(at * columns, columns)
             stack_rows(
@@ -328,6 +342,8 @@
     for frame in range(frame_count):
         total = taps_sum(sources, frame, stacked, packed, per_frame, None)
         partial[pl.ds(frame * per_frame, per_frame)] = total
+    for copy in copies:
+        copy.wait()
 
 
 def earlier_body(columns, low, high, off, packed, partial, total, stacked):
@@ -457,16 +473,16 @@
     wide = shape(tokens, channels, F32)
     turned = shape(channels, tokens, BF16)
     both = shape(tokens, 2 * channels, BF16)
-    weights = (w_query, w_key, w_value, w_out, student_in, student_out, conv_first, conv_second)
+    weights = (w_query, w_key, w_value, w_out, student_in, student_out, conv_first)
     (
-        w_both, w_out, student_out, packed_first, packed_second,
+        w_both, w_out, student_out, packed_first,
         slope, hidden_t, latent_t, predicted, queries, own_both, partner_both,
     ) = call(
         prepare_body,
-        [shape(channels, 2 * channels, BF16), square, square, packed_shape, packed_shape,
+        [shape(channels, 2 * channels, BF16), square, square, packed_shape,
          wide, turned, turned, wide, rows_of(frame_count), both, both],
-        [VMEM] * 3 + [HBM] * len(weights), [VMEM] * 12,
-        [pltpu.VMEM((channels, channels), BF16)] * 2 + [pltpu.SemaphoreType.DMA((12,))],
+        [VMEM] * 3 + [HBM] * len(weights), [VMEM] * 11,
+        [pltpu.VMEM((channels, channels), BF16)] * 2 + [pltpu.SemaphoreType.DMA((7,))],
         7 * tokens * unit, 60 * channels * channels * 2,
         latent_rows, normed, xor_permute(normed, "space", 1), *weights,
     )
@@ -507,19 +523,21 @@
             [stacked(2)], 9 * tokens * unit, 8 * tokens * channels, *args,
         )
 
-    def own_part(groups, on, off, packed):
+    def own_part(groups, on, off, packed, *taps):
         halo = [across_permute(off)]
         halo.append(xor_permute(on, "space", 1))
         args = [*(own for _, own in groups), *halo, packed]
+        outs = [shape(tokens, 3 * channels, F32)] + [packed_shape] * len(taps)
         return call(
-            functools.partial(own_body, [group[0] for group in groups], columns),
-            shape(tokens, 3 * channels, F32), [VMEM] * len(args), VMEM,
-            [stacked(frame_count)], 18 * tokens * unit, 8 * tokens * channels, *args,
+            functools.partial(own_body, [group[0] for group in groups], columns, bool(taps)),
+            outs, [VMEM] * len(args) + [HBM] * len(taps), [VMEM] * len(outs),
+            [stacked(frame_count)] + [pltpu.SemaphoreType.DMA((1,))] * len(taps),
+            18 * tokens * unit, 8 * tokens * channels, *args, *taps,
         )
 
     pair, corner, partner = from_earlier(late, off_late)
     groups = [(1, acts[frame]) for frame in range(early)] + [(2, late)]
-    partial = own_part(groups, on, off, packed_first)
+    partial, packed_second = own_part(groups, on, off, packed_first, conv_second)
     changed = earlier_part(pair, corner, packed_first, partial)
     args = [*partner, packed_first, changed, partial, conv_gain_second]
     act, late, on, off, off_late = call(
@@ -529,7 +547,7 @@
         9 * tokens * unit, 8 * tokens * channels, *args,
     )
     pair, corner, partner = from_earlier(late, off_late)
-    partial = own_part([(frame_count, act)], on, off, packed_second)
+    (partial,) = own_part([(frame_count, act)], on, off, packed_second)
     token_total = tokens * lax.axis_size("dp") * lax.axis_size("tm") * lax.axis_size("space")
     changed = earlier_part(pair, corner, packed_second, partial)
     args = [

time: 94.9 us -> 95.4 us (level)
  transfers between devices with their start and end apart: 32 -> 32, of which waited for: 15 -> 15; matrix products, arithmetic and copies ran while one was open for 0% -> 0% of each run, Pallas kernels for 24% -> 25%
where the time goes in v5:
time: 95.4 us; the launch traced here: 95.2 us
  waiting for transfers between devices  35.6 us (37%)
  Pallas kernels  29.5 us (31%)
  starting transfers between devices  28 us (29%)
  other arithmetic  1.26 us (1%)
    pallas_call x11, Pallas kernels, call(): pl.pallas_call(body, out_shape=outs, in_specs=specs, out_specs=out_specs,...  29.5 us
    ppermute x18, waiting for transfers between devices, xor_permute(): return lax.ppermute(value, axis, [(i, i ^ mask) for i in range(count)])  18.3 us
    ppermute x18, starting transfers between devices, xor_permute(): return lax.ppermute(value, axis, [(i, i ^ mask) for i in range(count)])  11.9 us
    ppermute x4, waiting for transfers between devices, frame_pairings(): results.append(lax.ppermute(value, ('tm', 'space'), pairs))  9.33 us
    ppermute x6, waiting for transfers between devices, plane_permute(): return lax.ppermute(value, ('dp', 'space'), pairs)  7.9 us
    ppermute x6, starting transfers between devices, plane_permute(): return lax.ppermute(value, ('dp', 'space'), pairs)  7.11 us
    ppermute x4, starting transfers between devices, frame_pairings(): results.append(lax.ppermute(value, ('tm', 'space'), pairs))  4.2 us
    ppermute x2, starting transfers between devices, across_permute(): return lax.ppermute(value, ('dp', 'space'), pairs)  3.04 us
  transfers between devices with their start and end apart: 32, of which 15 were waited for; matrix products, arithmetic and copies ran while one was open for 0% of the time, Pallas kernels for 25%

profile of v5, /device:TPU:0, one launch (start us, length us, event | category | flops | bytes accessed | tf_op | source)
XLA Modules:
  0.0 95.2 jit_solution(3958481444660208044)
XLA Ops:
  0.6 1.4 %shard_map.139 = (bf16[624,384]{1,0:T(8,128)(2,1)S(1)}, bf16[624,384]{1,0:T(8,128)(2,1)S(1)}, bf16[208,384]{1,0:T(8,128)(2,1)S(1)}, bf16[208,384]{1,0:T(8,128)(2,1)S(1)}, bf16[208,384]{1,0:T(8,128)(2,1)S(1)}) custom-call(bf16[3,208,384]{2,1,0:T(8,128)(2,1)} %bitcast.2, f32[384]{0:T(512)} %gain_hbm.1), custom_call_target="tpu_custom_call" | custom-call | bytes 958464 | tf_op jit(solution)/shard_map/pallas_call | solution.py:143
  2.6 2.6 %collective-permute-start.3 = (bf16[208,384]{1,0:T(8,128)(2,1)S(1)}, bf16[208,384]{1,0:T(8,128)(2,1)S(1)}, u32[]{:S(2)}, u32[]{:S(2)}) collective-permute-start(bf16[208,384]{1,0:T(8,128)(2,1)S(1)} %get-tuple-element.49), channel_id=1, source_target_pairs={{0,2},{1,3},{2,0},{3,1},{4,6},{5,7},{6,4},{7,5},{8,10},{9,11},{10,... | collective-permute-start | bytes 479240 | tf_op jit(solution)/shard_map/ppermute | solution.py:20
  5.2 1.9 %collective-permute-start.10 = (bf16[208,384]{1,0:T(8,128)(2,1)S(1)}, bf16[208,384]{1,0:T(8,128)(2,1)S(1)}, u32[]{:S(2)}, u32[]{:S(2)}) collective-permute-start(bf16[208,384]{1,0:T(8,128)(2,1)S(1)} %get-tuple-element.56), channel_id=1, source_target_pairs={{0,2},{1,3},{2,0},{3,1},{4,6},{5,7},{6,4},{7,5},{8,10},{9,11},{10,... | collective-permute-start | bytes 479240 | tf_op jit(solution)/shard_map/ppermute | solution.py:20
  7.2 2.9 %collective-permute-done.3.refs_0_ = bf16[208,384]{1,0:T(8,128)(2,1)S(1)} collective-permute-done((bf16[208,384]{1,0:T(8,128)(2,1)S(1)}, bf16[208,384]{1,0:T(8,128)(2,1)S(1)}, u32[]{:S(2)}, u32[]{:S(2)}) %collective-permute-start.3) | collective-permute-done | bytes 159776 | tf_op jit(solution)/shard_map/ppermute | solution.py:20
  10.1 3.4 %collective-permute-done.refs_0_ = bf16[208,384]{1,0:T(8,128)(2,1)S(1)} collective-permute-done((bf16[208,384]{1,0:T(8,128)(2,1)S(1)}, bf16[208,384]{1,0:T(8,128)(2,1)S(1)}, u32[]{:S(2)}, u32[]{:S(2)}) %collective-permute-start) | collective-permute-done | bytes 159776 | tf_op jit(solution)/shard_map/ppermute | solution.py:20
  13.5 3.2 %collective-permute-done.10.refs_0_ = bf16[208,384]{1,0:T(8,128)(2,1)S(1)} collective-permute-done((bf16[208,384]{1,0:T(8,128)(2,1)S(1)}, bf16[208,384]{1,0:T(8,128)(2,1)S(1)}, u32[]{:S(2)}, u32[]{:S(2)}) %collective-permute-start.10) | collective-permute-done | bytes 159776 | tf_op jit(solution)/shard_map/ppermute | solution.py:20
  16.7 3.9 %shard_map.140 = (bf16[384,768]{1,0:T(8,128)(2,1)S(1)}, bf16[384,384]{1,0:T(8,128)(2,1)S(1)}, bf16[384,384]{1,0:T(8,128)(2,1)S(1)}, bf16[3456,1152]{1,0:T(8,128)...) custom-call(bf16[624,384]{1,0:T(8,128)(2,1)S(1)} %get-tuple-element., ...), custom_call_target="tpu_custom_call" | custom-call | flops 1288175616 | bytes 17694720 | tf_op jit(solution)/shard_map/pallas_call | solution.py:143
  20.6 1.6 %shard_map.141 = (bf16[208,384]{1,0:T(8,128)(2,1)S(1)}, bf16[208,384]{1,0:T(8,128)(2,1)S(1)}, bf16[104,384]{1,0:T(8,128)(2,1)S(1)}, bf16[104,384]{1,0:T(8,128)(2,1)S(1)}) custom-call(bf16[208,384]{1,0:T(8,128)(2,1)S(1)} %collective-permute-done.3.refs_0_, bf16[208,384]{1,0:T(8,128)(2,1)S(1)} %collective-permute-done.4.refs_1_, ...), custom_call_target="tpu_custom_call" | custom-call | flops 490733568 | bytes 319488 | tf_op jit(solution)/shard_map/pallas_call | solution.py:143
  22.2 1.6 %shard_map.142 = (bf16[416,384]{1,0:T(8,128)(2,1)S(1)}, bf16[208,384]{1,0:T(8,128)(2,1)S(1)}, bf16[208,384]{1,0:T(8,128)(2,1)S(1)}, bf16[208,384]{1,0:T(8,128)(2,1)S(1)}) custom-call(bf16[208,384]{1,0:T(8,128)(2,1)S(1)} %collective-permute-done.refs_0_, bf16[208,384]{1,0:T(8,128)(2,1)S(1)} %collective-permute-done.1.refs_1_, ...), custom_call_target="tpu_custom_call" | custom-call | flops 490733568 | bytes 319488 | tf_op jit(solution)/shard_map/pallas_call | solution.py:143
  23.7 1.9 %collective-permute-start.5 = (bf16[416,384]{1,0:T(8,128)(2,1)S(1)}, bf16[416,384]{1,0:T(8,128)(2,1)S(1)}, u32[]{:S(2)}, u32[]{:S(2)}) collective-permute-start(bf16[416,384]{1,0:T(8,128)(2,1)S(1)} %get-tuple-element.53.refs_1_), channel_id=1, source_target_pairs={{0,4},{1,5},{2,6},{3,7},{4,0},{5,1},{6,2},{7,3},{8,12},{9,13},{10,... | collective-permute-start | bytes 958472 | tf_op jit(solution)/shard_map/ppermute | solution.py:62
  25.8 1.6 %shard_map.143 = (bf16[208,384]{1,0:T(8,128)(2,1)S(1)}, bf16[208,384]{1,0:T(8,128)(2,1)S(1)}, bf16[312,384]{1,0:T(8,128)(2,1)S(1)}, bf16[312,384]{1,0:T(8,128)(2,1)S(1)}) custom-call(bf16[208,384]{1,0:T(8,128)(2,1)S(1)} %collective-permute-done.10.refs_0_, bf16[208,384]{1,0:T(8,128)(2,1)S(1)} %collective-permute-done.11.refs_1_, ...), custom_call_target="tpu_custom_call" | custom-call | flops 490733568 | bytes 319488 | tf_op jit(solution)/shard_map/pallas_call | solution.py:143
  27.4 1.6 %collective-permute-start.12 = (bf16[312,384]{1,0:T(8,128)(2,1)S(1)}, bf16[312,384]{1,0:T(8,128)(2,1)S(1)}, u32[]{:S(2)}, u32[]{:S(2)}) collective-permute-start(bf16[312,384]{1,0:T(8,128)(2,1)S(1)} %get-tuple-element.59), channel_id=1, source_target_pairs={{0,16},{1,2},{2,1},{3,19},{16,0},{17,18},{18,17},{19,3},{4,20},{5,... | collective-permute-start | bytes 718856 | tf_op jit(solution)/shard_map/ppermute | solution.py:48
  30.0 3.9 %collective-permute-done.5.low = bf16[416,384]{1,0:T(8,128)(2,1)S(1)} collective-permute-done((bf16[416,384]{1,0:T(8,128)(2,1)S(1)}, bf16[416,384]{1,0:T(8,128)(2,1)S(1)}, u32[]{:S(2)}, u32[]{:S(2)}) %collective-permute-start.5) | collective-permute-done | bytes 319520 | tf_op jit(solution)/shard_map/ppermute | solution.py:62
  34.9 6.9 %shard_map.144 = (f32[624,1152]{1,0:T(8,128)S(1)}, bf16[3456,1152]{1,0:T(8,128)(2,1)S(1)}) custom-call(bf16[208,384]{1,0:T(8,128)(2,1)S(1)} %get-tuple-element.58.refs_0_, bf16[416,384]{1,0:T(8,128)(2,1)S(1)} %get-tuple-element.53.refs_1_, bf16[312,384]{1,0:T(8,128)(2,1)S(1)} %collective-permute-done.12.refs_2_, ...), custom_call_target="tpu_custom_call" | custom-call | flops 3312451584 | bytes 1916928 | tf_op jit(solution)/shard_map/pallas_call | solution.py:143
  41.8 2.2 %shard_map.145.changed = f32[416,1152]{1,0:T(8,128)S(1)} custom-call(bf16[416,384]{1,0:T(8,128)(2,1)S(1)} %collective-permute-done.5.low, bf16[416,384]{1,0:T(8,128)(2,1)S(1)} %collective-permute-done.7.high, bf16[208,384]{1,0:T(8,128)(2,1)S(1)} %collective-permute-done.9.off, bf16[3456,1152]{1,0:T(8,128)(2,1)S(1)} %get-tuple-element.54.refs_4_.packed, ...), custom_call_target="tpu_custom_call" | custom-call | flops 1656225792 | bytes 1916928 | tf_op jit(solution)/shard_map/pallas_call | solution.py:143
  44.1 1.3 %shard_map.146 = (bf16[624,384]{1,0:T(8,128)(2,1)S(1)}, bf16[416,384]{1,0:T(8,128)(2,1)S(1)}, bf16[312,384]{1,0:T(8,128)(2,1)S(1)}, bf16[312,384]{1,0:T(8,128)(2,1)S(1)}, bf16[208,384]{1,0:T(8,128)(2,1)S(1)}) custom-call(bf16[416,384]{1,0:T(8,128)(2,1)S(1)} %collective-permute-done.6.low, bf16[416,384]{1,0:T(8,128)(2,1)S(1)} %collective-permute-done.8.high, ...), custom_call_target="tpu_custom_call" | custom-call | flops 1656225792 | bytes 1916928 | tf_op jit(solution)/shard_map/pallas_call | solution.py:143
  45.4 1.9 %collective-permute-start.14 = (bf16[416,384]{1,0:T(8,128)(2,1)S(1)}, bf16[416,384]{1,0:T(8,128)(2,1)S(1)}, u32[]{:S(2)}, u32[]{:S(2)}) collective-permute-start(bf16[416,384]{1,0:T(8,128)(2,1)S(1)} %get-tuple-element.62), channel_id=1, source_target_pairs={{0,4},{1,5},{2,6},{3,7},{4,0},{5,1},{6,2},{7,3},{8,12},{9,13},{10,... | collective-permute-start | bytes 958472 | tf_op jit(solution)/shard_map/ppermute | solution.py:62
  47.5 1.5 %collective-permute-start.19 = (bf16[312,384]{1,0:T(8,128)(2,1)S(1)}, bf16[312,384]{1,0:T(8,128)(2,1)S(1)}, u32[]{:S(2)}, u32[]{:S(2)}) collective-permute-start(bf16[312,384]{1,0:T(8,128)(2,1)S(1)} %get-tuple-element.66), channel_id=1, source_target_pairs={{0,16},{1,2},{2,1},{3,19},{16,0},{17,18},{18,17},{19,3},{4,20},{5,... | collective-permute-start | bytes 718856 | tf_op jit(solution)/shard_map/ppermute | solution.py:48
  50.0 5.5 %collective-permute-done.14.low = bf16[416,384]{1,0:T(8,128)(2,1)S(1)} collective-permute-done((bf16[416,384]{1,0:T(8,128)(2,1)S(1)}, bf16[416,384]{1,0:T(8,128)(2,1)S(1)}, u32[]{:S(2)}, u32[]{:S(2)}) %collective-permute-start.14) | collective-permute-done | bytes 319520 | tf_op jit(solution)/shard_map/ppermute | solution.py:62
  56.0 4.1 %shard_map.147.partial = f32[624,1152]{1,0:T(8,128)S(1)} custom-call(bf16[624,384]{1,0:T(8,128)(2,1)S(1)} %get-tuple-element.65.refs_0_, bf16[312,384]{1,0:T(8,128)(2,1)S(1)} %collective-permute-done.19.refs_1_, bf16[312,384]{1,0:T(8,128)(2,1)S(1)} %collective-permute-done.20.refs_2_, bf16[3456,1152]{1,0:T(8,128)(2,1)S(1)} %get-tuple-element.63.refs_3_.packed), custom_call_target="tpu_custom_call" | custom-call | flops 3312451584 | bytes 1916928 | tf_op jit(solution)/shard_map/pallas_call | solution.py:143
  60.2 2.2 %shard_map.148.changed = f32[416,1152]{1,0:T(8,128)S(1)} custom-call(bf16[416,384]{1,0:T(8,128)(2,1)S(1)} %collective-permute-done.14.low, bf16[416,384]{1,0:T(8,128)(2,1)S(1)} %collective-permute-done.16.high, bf16[208,384]{1,0:T(8,128)(2,1)S(1)} %collective-permute-done.18.off, bf16[3456,1152]{1,0:T(8,128)(2,1)S(1)} %get-tuple-element.63.refs_3_.packed, ...), custom_call_target="tpu_custom_call" | custom-call | flops 1656225792 | bytes 1916928 | tf_op jit(solution)/shard_map/pallas_call | solution.py:143
  62.4 2.8 %shard_map.149 = (bf16[624,384]{1,0:T(8,128)(2,1)}, f32[384,384]{1,0:T(8,128)S(1)}, bf16[384,384]{1,0:T(8,128)(2,1)S(1)}) custom-call(bf16[416,384]{1,0:T(8,128)(2,1)S(1)} %collective-permute-done.15.low, bf16[416,384]{1,0:T(8,128)(2,1)S(1)} %collective-permute-done.17.high, bf16[3456,1152]{1,0:T(8,128)(2,1)S(1)} %get-tuple-element.63.refs_3_.packed, ...), custom_call_target="tpu_custom_call" | custom-call | flops 2208301056 | bytes 1916928 | tf_op jit(solution)/shard_map/pallas_call | solution.py:143
  65.2 1.6 %collective-permute-done.21 = bf16[384,384]{1,0:T(8,128)(2,1)S(1)} collective-permute-done((bf16[384,384]{1,0:T(8,128)(2,1)S(1)}, bf16[384,384]{1,0:T(8,128)(2,1)S(1)}, u32[]{:S(2)}, u32[]{:S(2)}) %collective-permute-start.21) | collective-permute-done | bytes 294944 | tf_op jit(solution)/shard_map/ppermute | solution.py:20
  66.9 1.6 %collective-permute-start.22 = (bf16[96,384]{1,0:T(8,128)(2,1)S(1)}, bf16[96,384]{1,0:T(8,128)(2,1)S(1)}, u32[]{:S(2)}, u32[]{:S(2)}) collective-permute-start(bf16[96,384]{1,0:T(8,128)(2,1)S(1)} %get-tuple-element.85), channel_id=1, source_target_pairs={{0,2},{1,3},{2,0},{3,1},{16,18},{17,19},{18,16},{19,17},{4,6},{5,7... | collective-permute-start | bytes 221192 | tf_op jit(solution)/shard_map/ppermute | solution.py:89
  68.5 1.5 %collective-permute-start.23 = (bf16[96,384]{1,0:T(8,128)(2,1)S(1)}, bf16[96,384]{1,0:T(8,128)(2,1)S(1)}, u32[]{:S(2)}, u32[]{:S(2)}) collective-permute-start(bf16[96,384]{1,0:T(8,128)(2,1)S(1)} %get-tuple-element.87), channel_id=1, source_target_pairs={{0,16},{1,17},{2,18},{3,19},{16,0},{17,1},{18,2},{19,3},{4,20},{5,... | collective-permute-start | bytes 221192 | tf_op jit(solution)/shard_map/ppermute | solution.py:89
  71.3 2.3 %collective-permute-done.23 = bf16[96,384]{1,0:T(8,128)(2,1)S(1)} collective-permute-done((bf16[96,384]{1,0:T(8,128)(2,1)S(1)}, bf16[96,384]{1,0:T(8,128)(2,1)S(1)}, u32[]{:S(2)}, u32[]{:S(2)}) %collective-permute-start.23) | collective-permute-done | bytes 73760 | tf_op jit(solution)/shard_map/ppermute | solution.py:89
  73.6 1.6 %collective-permute-done.24 = bf16[96,384]{1,0:T(8,128)(2,1)S(1)} collective-permute-done((bf16[96,384]{1,0:T(8,128)(2,1)S(1)}, bf16[96,384]{1,0:T(8,128)(2,1)S(1)}, u32[]{:S(2)}, u32[]{:S(2)}) %collective-permute-start.24) | collective-permute-done | bytes 73760 | tf_op jit(solution)/shard_map/ppermute | solution.py:89
  75.2 1.8 %collective-permute-start.25 = (bf16[96,384]{1,0:T(8,128)(2,1)S(1)}, bf16[96,384]{1,0:T(8,128)(2,1)S(1)}, u32[]{:S(2)}, u32[]{:S(2)}) collective-permute-start(bf16[96,384]{1,0:T(8,128)(2,1)S(1)} %add_convert_fusion.1), channel_id=1, source_target_pairs={{0,4},{4,0},{8,12},{12,8},{1,5},{5,1},{9,13},{13,9},{2,6},{6,2},{1... | collective-permute-start | bytes 221192 | tf_op jit(solution)/shard_map/ppermute | solution.py:20
  77.0 1.9 %collective-permute-start.26 = (bf16[96,384]{1,0:T(8,128)(2,1)S(1)}, bf16[96,384]{1,0:T(8,128)(2,1)S(1)}, u32[]{:S(2)}, u32[]{:S(2)}) collective-permute-start(bf16[96,384]{1,0:T(8,128)(2,1)S(1)} %add_convert_fusion.1), channel_id=1, source_target_pairs={{0,8},{4,12},{8,0},{12,4},{1,9},{5,13},{9,1},{13,5},{2,10},{6,14},... | collective-permute-start | bytes 221192 | tf_op jit(solution)/shard_map/ppermute | solution.py:20
  80.4 5.2 %collective-permute-done.26 = bf16[96,384]{1,0:T(8,128)(2,1)S(1)} collective-permute-done((bf16[96,384]{1,0:T(8,128)(2,1)S(1)}, bf16[96,384]{1,0:T(8,128)(2,1)S(1)}, u32[]{:S(2)}, u32[]{:S(2)}) %collective-permute-start.26) | collective-permute-done | bytes 73760 | tf_op jit(solution)/shard_map/ppermute | solution.py:20
  87.2 2.1 %collective-permute-start.30 = (bf16[96,384]{1,0:T(8,128)(2,1)S(1)}, bf16[96,384]{1,0:T(8,128)(2,1)S(1)}, u32[]{:S(2)}, u32[]{:S(2)}) collective-permute-start(bf16[96,384]{1,0:T(8,128)(2,1)S(1)} %get-tuple-element.80), channel_id=1, source_target_pairs={{0,18},{1,19},{2,16},{3,17},{16,2},{17,3},{18,0},{19,1},{4,22},{5,... | collective-permute-start | bytes 221192 | tf_op jit(solution)/shard_map/ppermute | solution.py:89
  92.5 1.6 %collective-permute-done.31 = bf16[384,384]{1,0:T(8,128)(2,1)S(1)} collective-permute-done((bf16[384,384]{1,0:T(8,128)(2,1)S(1)}, bf16[384,384]{1,0:T(8,128)(2,1)S(1)}, u32[]{:S(2)}, u32[]{:S(2)}) %collective-permute-start.31) | collective-permute-done | bytes 294944 | tf_op jit(solution)/shard_map/ppermute | solution.py:20
  (56 shorter events, 13.6 us)
Async XLA Ops:
  2.0 14.7 %collective-permute-start.2 = (bf16[624,384]{1,0:T(8,128)(2,1)S(1)}, bf16[624,384]{1,0:T(8,128)(2,1)S(1)}, u32[]{:S(2)}, u32[]{:S(2)}) collective-permute-start(bf16[624,384]{1,0:T(8,128)(2,1)S(1)} %get-tuple-element.43.normed), channel_id=1, source_target_pairs={{0,1},{1,0},{2,3},{3,2},{4,5},{5,4},{6,7},{7,6},{8,9},{9,8},{10,11... | collective-permute-start | bytes 1437704 | tf_op jit(solution)/shard_map/ppermute | solution.py:20
  2.6 7.5 %collective-permute-start.3 = (bf16[208,384]{1,0:T(8,128)(2,1)S(1)}, bf16[208,384]{1,0:T(8,128)(2,1)S(1)}, u32[]{:S(2)}, u32[]{:S(2)}) collective-permute-start(bf16[208,384]{1,0:T(8,128)(2,1)S(1)} %get-tuple-element.49), channel_id=1, source_target_pairs={{0,2},{1,3},{2,0},{3,1},{4,6},{5,7},{6,4},{7,5},{8,10},{9,11},{10,... | collective-permute-start | bytes 479240 | tf_op jit(solution)/shard_map/ppermute | solution.py:20
  5.1 8.4 %collective-permute-start = (bf16[208,384]{1,0:T(8,128)(2,1)S(1)}, bf16[208,384]{1,0:T(8,128)(2,1)S(1)}, u32[]{:S(2)}, u32[]{:S(2)}) collective-permute-start(bf16[208,384]{1,0:T(8,128)(2,1)S(1)} %get-tuple-element.41), channel_id=1, source_target_pairs={{0,2},{1,3},{2,0},{3,1},{4,6},{5,7},{6,4},{7,5},{8,10},{9,11},{10,... | collective-permute-start | bytes 479240 | tf_op jit(solution)/shard_map/ppermute | solution.py:20
  5.2 11.5 %collective-permute-start.10 = (bf16[208,384]{1,0:T(8,128)(2,1)S(1)}, bf16[208,384]{1,0:T(8,128)(2,1)S(1)}, u32[]{:S(2)}, u32[]{:S(2)}) collective-permute-start(bf16[208,384]{1,0:T(8,128)(2,1)S(1)} %get-tuple-element.56), channel_id=1, source_target_pairs={{0,2},{1,3},{2,0},{3,1},{4,6},{5,7},{6,4},{7,5},{8,10},{9,11},{10,... | collective-permute-start | bytes 479240 | tf_op jit(solution)/shard_map/ppermute | solution.py:20
  10.1 10.5 %collective-permute-start.4 = (bf16[208,384]{1,0:T(8,128)(2,1)S(1)}, bf16[208,384]{1,0:T(8,128)(2,1)S(1)}, u32[]{:S(2)}, u32[]{:S(2)}) collective-permute-start(bf16[208,384]{1,0:T(8,128)(2,1)S(1)} %collective-permute-done.3.refs_0_), channel_id=1, source_target_pairs={{0,1},{1,0},{2,3},{3,2},{4,5},{5,4},{6,7},{7,6},{8,9},{9,8},{10,11... | collective-permute-start | bytes 479240 | tf_op jit(solution)/shard_map/ppermute | solution.py:20
  13.5 8.6 %collective-permute-start.1 = (bf16[208,384]{1,0:T(8,128)(2,1)S(1)}, bf16[208,384]{1,0:T(8,128)(2,1)S(1)}, u32[]{:S(2)}, u32[]{:S(2)}) collective-permute-start(bf16[208,384]{1,0:T(8,128)(2,1)S(1)} %collective-permute-done.refs_0_), channel_id=1, source_target_pairs={{0,1},{1,0},{2,3},{3,2},{4,5},{5,4},{6,7},{7,6},{8,9},{9,8},{10,11... | collective-permute-start | bytes 479240 | tf_op jit(solution)/shard_map/ppermute | solution.py:20
  16.7 9.1 %collective-permute-start.11 = (bf16[208,384]{1,0:T(8,128)(2,1)S(1)}, bf16[208,384]{1,0:T(8,128)(2,1)S(1)}, u32[]{:S(2)}, u32[]{:S(2)}) collective-permute-start(bf16[208,384]{1,0:T(8,128)(2,1)S(1)} %collective-permute-done.10.refs_0_), channel_id=1, source_target_pairs={{0,1},{1,0},{2,3},{3,2},{4,5},{5,4},{6,7},{7,6},{8,9},{9,8},{10,11... | collective-permute-start | bytes 479240 | tf_op jit(solution)/shard_map/ppermute | solution.py:20
  23.7 10.1 %collective-permute-start.5 = (bf16[416,384]{1,0:T(8,128)(2,1)S(1)}, bf16[416,384]{1,0:T(8,128)(2,1)S(1)}, u32[]{:S(2)}, u32[]{:S(2)}) collective-permute-start(bf16[416,384]{1,0:T(8,128)(2,1)S(1)} %get-tuple-element.53.refs_1_), channel_id=1, source_target_pairs={{0,4},{1,5},{2,6},{3,7},{4,0},{5,1},{6,2},{7,3},{8,12},{9,13},{10,... | collective-permute-start | bytes 958472 | tf_op jit(solution)/shard_map/ppermute | solution.py:62
  25.6 9.2 %collective-permute-start.7 = (bf16[416,384]{1,0:T(8,128)(2,1)S(1)}, bf16[416,384]{1,0:T(8,128)(2,1)S(1)}, u32[]{:S(2)}, u32[]{:S(2)}) collective-permute-start(bf16[416,384]{1,0:T(8,128)(2,1)S(1)} %get-tuple-element.53.refs_1_), channel_id=1, source_target_pairs={{0,1},{1,0},{2,3},{3,2},{4,8},{5,9},{6,10},{7,11},{8,4},{9,5},{10,... | collective-permute-start | bytes 958472 | tf_op jit(solution)/shard_map/ppermute | solution.py:62
  27.4 7.5 %collective-permute-start.12 = (bf16[312,384]{1,0:T(8,128)(2,1)S(1)}, bf16[312,384]{1,0:T(8,128)(2,1)S(1)}, u32[]{:S(2)}, u32[]{:S(2)}) collective-permute-start(bf16[312,384]{1,0:T(8,128)(2,1)S(1)} %get-tuple-element.59), channel_id=1, source_target_pairs={{0,16},{1,2},{2,1},{3,19},{16,0},{17,18},{18,17},{19,3},{4,20},{5,... | collective-permute-start | bytes 718856 | tf_op jit(solution)/shard_map/ppermute | solution.py:48
  29.0 5.9 %collective-permute-start.13 = (bf16[312,384]{1,0:T(8,128)(2,1)S(1)}, bf16[312,384]{1,0:T(8,128)(2,1)S(1)}, u32[]{:S(2)}, u32[]{:S(2)}) collective-permute-start(bf16[312,384]{1,0:T(8,128)(2,1)S(1)} %get-tuple-element.60), channel_id=1, source_target_pairs={{0,1},{1,0},{2,3},{3,2},{4,5},{5,4},{6,7},{7,6},{8,9},{9,8},{10,11... | collective-permute-start | bytes 718856 | tf_op jit(solution)/shard_map/ppermute | solution.py:20
  29.1 12.7 %collective-permute-start.9 = (bf16[208,384]{1,0:T(8,128)(2,1)S(1)}, bf16[208,384]{1,0:T(8,128)(2,1)S(1)}, u32[]{:S(2)}, u32[]{:S(2)}) collective-permute-start(bf16[208,384]{1,0:T(8,128)(2,1)S(1)} %get-tuple-element.55.refs_10_), channel_id=1, source_target_pairs={{1,6},{2,5},{5,10},{6,9},{9,14},{10,13},{17,22},{18,21},{21,26},{2... | collective-permute-start | bytes 479240 | tf_op jit(solution)/shard_map/ppermute | solution.py:73
  33.8 10.2 %collective-permute-start.6 = (bf16[416,384]{1,0:T(8,128)(2,1)S(1)}, bf16[416,384]{1,0:T(8,128)(2,1)S(1)}, u32[]{:S(2)}, u32[]{:S(2)}) collective-permute-start(bf16[416,384]{1,0:T(8,128)(2,1)S(1)} %collective-permute-done.5.low), channel_id=1, source_target_pairs={{0,1},{1,0},{2,3},{3,2},{4,5},{5,4},{6,7},{7,6},{8,9},{9,8},{10,11... | collective-permute-start | bytes 958472 | tf_op jit(solution)/shard_map/ppermute | solution.py:20
  34.8 9.3 %collective-permute-start.8 = (bf16[416,384]{1,0:T(8,128)(2,1)S(1)}, bf16[416,384]{1,0:T(8,128)(2,1)S(1)}, u32[]{:S(2)}, u32[]{:S(2)}) collective-permute-start(bf16[416,384]{1,0:T(8,128)(2,1)S(1)} %collective-permute-done.7.high), channel_id=1, source_target_pairs={{0,1},{1,0},{2,3},{3,2},{4,5},{5,4},{6,7},{7,6},{8,9},{9,8},{10,11... | collective-permute-start | bytes 958472 | tf_op jit(solution)/shard_map/ppermute | solution.py:20
  45.4 10.1 %collective-permute-start.14 = (bf16[416,384]{1,0:T(8,128)(2,1)S(1)}, bf16[416,384]{1,0:T(8,128)(2,1)S(1)}, u32[]{:S(2)}, u32[]{:S(2)}) collective-permute-start(bf16[416,384]{1,0:T(8,128)(2,1)S(1)} %get-tuple-element.62), channel_id=1, source_target_pairs={{0,4},{1,5},{2,6},{3,7},{4,0},{5,1},{6,2},{7,3},{8,12},{9,13},{10,... | collective-permute-start | bytes 958472 | tf_op jit(solution)/shard_map/ppermute | solution.py:62
  47.3 8.2 %collective-permute-start.16 = (bf16[416,384]{1,0:T(8,128)(2,1)S(1)}, bf16[416,384]{1,0:T(8,128)(2,1)S(1)}, u32[]{:S(2)}, u32[]{:S(2)}) collective-permute-start(bf16[416,384]{1,0:T(8,128)(2,1)S(1)} %get-tuple-element.62), channel_id=1, source_target_pairs={{0,1},{1,0},{2,3},{3,2},{4,8},{5,9},{6,10},{7,11},{8,4},{9,5},{10,... | collective-permute-start | bytes 958472 | tf_op jit(solution)/shard_map/ppermute | solution.py:62
  47.5 8.5 %collective-permute-start.19 = (bf16[312,384]{1,0:T(8,128)(2,1)S(1)}, bf16[312,384]{1,0:T(8,128)(2,1)S(1)}, u32[]{:S(2)}, u32[]{:S(2)}) collective-permute-start(bf16[312,384]{1,0:T(8,128)(2,1)S(1)} %get-tuple-element.66), channel_id=1, source_target_pairs={{0,16},{1,2},{2,1},{3,19},{16,0},{17,18},{18,17},{19,3},{4,20},{5,... | collective-permute-start | bytes 718856 | tf_op jit(solution)/shard_map/ppermute | solution.py:48
  49.0 7.0 %collective-permute-start.20 = (bf16[312,384]{1,0:T(8,128)(2,1)S(1)}, bf16[312,384]{1,0:T(8,128)(2,1)S(1)}, u32[]{:S(2)}, u32[]{:S(2)}) collective-permute-start(bf16[312,384]{1,0:T(8,128)(2,1)S(1)} %get-tuple-element.67), channel_id=1, source_target_pairs={{0,1},{1,0},{2,3},{3,2},{4,5},{5,4},{6,7},{7,6},{8,9},{9,8},{10,11... | collective-permute-start | bytes 718856 | tf_op jit(solution)/shard_map/ppermute | solution.py:20
  49.2 11.0 %collective-permute-start.18 = (bf16[208,384]{1,0:T(8,128)(2,1)S(1)}, bf16[208,384]{1,0:T(8,128)(2,1)S(1)}, u32[]{:S(2)}, u32[]{:S(2)}) collective-permute-start(bf16[208,384]{1,0:T(8,128)(2,1)S(1)} %get-tuple-element.64), channel_id=1, source_target_pairs={{1,6},{2,5},{5,10},{6,9},{9,14},{10,13},{17,22},{18,21},{21,26},{2... | collective-permute-start | bytes 479240 | tf_op jit(solution)/shard_map/ppermute | solution.py:73
  55.5 6.9 %collective-permute-start.15 = (bf16[416,384]{1,0:T(8,128)(2,1)S(1)}, bf16[416,384]{1,0:T(8,128)(2,1)S(1)}, u32[]{:S(2)}, u32[]{:S(2)}) collective-permute-start(bf16[416,384]{1,0:T(8,128)(2,1)S(1)} %collective-permute-done.14.low), channel_id=1, source_target_pairs={{0,1},{1,0},{2,3},{3,2},{4,5},{5,4},{6,7},{7,6},{8,9},{9,8},{10,11... | collective-permute-start | bytes 958472 | tf_op jit(solution)/shard_map/ppermute | solution.py:20
  55.5 6.9 %collective-permute-start.17 = (bf16[416,384]{1,0:T(8,128)(2,1)S(1)}, bf16[416,384]{1,0:T(8,128)(2,1)S(1)}, u32[]{:S(2)}, u32[]{:S(2)}) collective-permute-start(bf16[416,384]{1,0:T(8,128)(2,1)S(1)} %collective-permute-done.16.high), channel_id=1, source_target_pairs={{0,1},{1,0},{2,3},{3,2},{4,5},{5,4},{6,7},{7,6},{8,9},{9,8},{10,11... | collective-permute-start | bytes 958472 | tf_op jit(solution)/shard_map/ppermute | solution.py:20
  65.2 1.6 %collective-permute-start.21 = (bf16[384,384]{1,0:T(8,128)(2,1)S(1)}, bf16[384,384]{1,0:T(8,128)(2,1)S(1)}, u32[]{:S(2)}, u32[]{:S(2)}) collective-permute-start(bf16[384,384]{1,0:T(8,128)(2,1)S(1)} %get-tuple-element.78), channel_id=1, source_target_pairs={{0,1},{1,0},{2,3},{3,2},{4,5},{5,4},{6,7},{7,6},{8,9},{9,8},{10,11... | collective-permute-start | bytes 884744 | tf_op jit(solution)/shard_map/ppermute | solution.py:20
  66.9 4.4 %collective-permute-start.22 = (bf16[96,384]{1,0:T(8,128)(2,1)S(1)}, bf16[96,384]{1,0:T(8,128)(2,1)S(1)}, u32[]{:S(2)}, u32[]{:S(2)}) collective-permute-start(bf16[96,384]{1,0:T(8,128)(2,1)S(1)} %get-tuple-element.85), channel_id=1, source_target_pairs={{0,2},{1,3},{2,0},{3,1},{16,18},{17,19},{18,16},{19,17},{4,6},{5,7... | collective-permute-start | bytes 221192 | tf_op jit(solution)/shard_map/ppermute | solution.py:89
  68.5 5.1 %collective-permute-start.23 = (bf16[96,384]{1,0:T(8,128)(2,1)S(1)}, bf16[96,384]{1,0:T(8,128)(2,1)S(1)}, u32[]{:S(2)}, u32[]{:S(2)}) collective-permute-start(bf16[96,384]{1,0:T(8,128)(2,1)S(1)} %get-tuple-element.87), channel_id=1, source_target_pairs={{0,16},{1,17},{2,18},{3,19},{16,0},{17,1},{18,2},{19,3},{4,20},{5,... | collective-permute-start | bytes 221192 | tf_op jit(solution)/shard_map/ppermute | solution.py:89
  69.9 5.3 %collective-permute-start.24 = (bf16[96,384]{1,0:T(8,128)(2,1)S(1)}, bf16[96,384]{1,0:T(8,128)(2,1)S(1)}, u32[]{:S(2)}, u32[]{:S(2)}) collective-permute-start(bf16[96,384]{1,0:T(8,128)(2,1)S(1)} %get-tuple-element.86), channel_id=1, source_target_pairs={{0,18},{1,19},{2,16},{3,17},{16,2},{17,3},{18,0},{19,1},{4,22},{5,... | collective-permute-start | bytes 221192 | tf_op jit(solution)/shard_map/ppermute | solution.py:89
  75.2 5.2 %collective-permute-start.25 = (bf16[96,384]{1,0:T(8,128)(2,1)S(1)}, bf16[96,384]{1,0:T(8,128)(2,1)S(1)}, u32[]{:S(2)}, u32[]{:S(2)}) collective-permute-start(bf16[96,384]{1,0:T(8,128)(2,1)S(1)} %add_convert_fusion.1), channel_id=1, source_target_pairs={{0,4},{4,0},{8,12},{12,8},{1,5},{5,1},{9,13},{13,9},{2,6},{6,2},{1... | collective-permute-start | bytes 221192 | tf_op jit(solution)/shard_map/ppermute | solution.py:20
  77.0 8.6 %collective-permute-start.26 = (bf16[96,384]{1,0:T(8,128)(2,1)S(1)}, bf16[96,384]{1,0:T(8,128)(2,1)S(1)}, u32[]{:S(2)}, u32[]{:S(2)}) collective-permute-start(bf16[96,384]{1,0:T(8,128)(2,1)S(1)} %add_convert_fusion.1), channel_id=1, source_target_pairs={{0,8},{4,12},{8,0},{12,4},{1,9},{5,13},{9,1},{13,5},{2,10},{6,14},... | collective-permute-start | bytes 221192 | tf_op jit(solution)/shard_map/ppermute | solution.py:20
  78.9 6.7 %collective-permute-start.27 = (bf16[96,384]{1,0:T(8,128)(2,1)S(1)}, bf16[96,384]{1,0:T(8,128)(2,1)S(1)}, u32[]{:S(2)}, u32[]{:S(2)}) collective-permute-start(bf16[96,384]{1,0:T(8,128)(2,1)S(1)} %add_convert_fusion.1), channel_id=1, source_target_pairs={{0,12},{4,8},{8,4},{12,0},{1,13},{5,9},{9,5},{13,1},{2,14},{6,10},... | collective-permute-start | bytes 221192 | tf_op jit(solution)/shard_map/ppermute | solution.py:20
  85.7 4.4 %collective-permute-start.28 = (bf16[96,384]{1,0:T(8,128)(2,1)S(1)}, bf16[96,384]{1,0:T(8,128)(2,1)S(1)}, u32[]{:S(2)}, u32[]{:S(2)}) collective-permute-start(bf16[96,384]{1,0:T(8,128)(2,1)S(1)} %get-tuple-element.80), channel_id=1, source_target_pairs={{0,2},{1,3},{2,0},{3,1},{16,18},{17,19},{18,16},{19,17},{4,6},{5,7... | collective-permute-start | bytes 221192 | tf_op jit(solution)/shard_map/ppermute | solution.py:89
  86.8 4.4 %collective-permute-start.29 = (bf16[96,384]{1,0:T(8,128)(2,1)S(1)}, bf16[96,384]{1,0:T(8,128)(2,1)S(1)}, u32[]{:S(2)}, u32[]{:S(2)}) collective-permute-start(bf16[96,384]{1,0:T(8,128)(2,1)S(1)} %get-tuple-element.80), channel_id=1, source_target_pairs={{0,16},{1,17},{2,18},{3,19},{16,0},{17,1},{18,2},{19,3},{4,20},{5,... | collective-permute-start | bytes 221192 | tf_op jit(solution)/shard_map/ppermute | solution.py:89
  87.2 5.3 %collective-permute-start.30 = (bf16[96,384]{1,0:T(8,128)(2,1)S(1)}, bf16[96,384]{1,0:T(8,128)(2,1)S(1)}, u32[]{:S(2)}, u32[]{:S(2)}) collective-permute-start(bf16[96,384]{1,0:T(8,128)(2,1)S(1)} %get-tuple-element.80), channel_id=1, source_target_pairs={{0,18},{1,19},{2,16},{3,17},{16,2},{17,3},{18,0},{19,1},{4,22},{5,... | collective-permute-start | bytes 221192 | tf_op jit(solution)/shard_map/ppermute | solution.py:89
  92.5 1.6 %collective-permute-start.31 = (bf16[384,384]{1,0:T(8,128)(2,1)S(1)}, bf16[384,384]{1,0:T(8,128)(2,1)S(1)}, u32[]{:S(2)}, u32[]{:S(2)}) collective-permute-start(bf16[384,384]{1,0:T(8,128)(2,1)S(1)} %constant_dynamic-update-slice_fusion), channel_id=1, source_target_pairs={{0,1},{1,0},{2,3},{3,2},{4,5},{5,4},{6,7},{7,6},{8,9},{9,8},{10,11... | collective-permute-start | bytes 884744 | tf_op jit(solution)/shard_map/ppermute | solution.py:20
  (2 other events, 22.2 us)
